TPU v7x, 32 devices: a whole 2x2x4 slice. The times are simulated.
32 devices in a mesh: ctx: 8 (over z, y), fsdp: 4 (over x, core).
Axes of the slice: x: 2, y: 2, z: 4, core: 2. Of those that a mesh axis runs over, the one named last changes fastest.
Arguments:
- tokens: bfloat16 [4, 1024, 576], P('fsdp', 'ctx'), may hold values from -6 to 6
- pair_of: int32 [4, 8], P('fsdp'), may hold values from 0 to 7, each once within a row
- gain_attn: bfloat16 [576], P('ctx'), may hold values from 0.099609375 to 1.8984375
- w_query: bfloat16 [576, 576], P('fsdp', 'ctx'), may hold values from -0.25 to 0.25
- key_weight: bfloat16 [576, 192], P('fsdp', 'ctx'), may hold values from -0.25 to 0.25
- value_weight: bfloat16 [576, 192], P('fsdp', 'ctx'), may hold values from -0.25 to 0.25
- w_out: bfloat16 [576, 576], P('fsdp', 'ctx'), may hold values from -6 to 6
- gain_ffn: bfloat16 [576], P('ctx'), may hold values from 0.099609375 to 1.8984375
- w_gate: bfloat16 [576, 1536], P('fsdp', 'ctx'), may hold values from -0.25 to 0.25
- w_up: bfloat16 [576, 1536], P('fsdp', 'ctx'), may hold values from -0.25 to 0.25
- w_down: bfloat16 [1536, 576], P('fsdp', 'ctx'), may hold values from -0.15625 to 0.15625
- cotangent: bfloat16 [4, 1024, 576], P('fsdp', 'ctx'), may hold values from -6 to 6
Outputs:
- output: bfloat16 [4, 1024, 576], P('fsdp', 'ctx')
- grad_input: float32 [4, 1024, 576], P('fsdp', 'ctx')
- grad_gain_attn: float32 [576], P('ctx')
- grad_w_query: float32 [576, 576], P('fsdp', 'ctx')
- grad_w_key: float32 [576, 192], P('fsdp', 'ctx')
- grad_w_value: float32 [576, 192], P('fsdp', 'ctx')
- grad_w_out: float32 [576, 576], P('fsdp', 'ctx')
- grad_gain_ffn: float32 [576], P('ctx')
- grad_w_gate: float32 [576, 1536], P('fsdp', 'ctx')
- grad_w_up: float32 [576, 1536], P('fsdp', 'ctx')
- grad_w_down: float32 [1536, 576], P('fsdp', 'ctx')
Inputs may be any that keep to these rules, and one draw needn't show every extreme that they name: Each row of pair_of holds every number from 0 to 7 once.
All inputs are finite; a program needn't handle non-finite values.
Results may differ from a plain program's by a relative error of at most 0.02.
Values may be sent and summed in bfloat16 or wider, within the bound.
No kernel may reach another device: no remote copies, remote signals or barrier semaphores. Data moves between devices by JAX's collectives and lax.ppermute only.
A program may use at most 128 MiB of HBM per device.

v0:
```python
import math

import jax
import jax.numpy as jnp
from jax import lax
from jax.sharding import PartitionSpec as P

QUERY_HEADS = 9
KEY_VALUE_HEADS = 3
HEAD_DIM = 64


theta_base = 100000.0
norm_eps = 1e-05
masked_fill = -1e30
group_shards = 4


def inverse_root(values):
    return lax.rsqrt(jnp.mean(values * values, axis=-1, keepdims=True) + norm_eps)


def rotary_tables(positions):
    half_dim = HEAD_DIM // 2
    frequency = theta_base ** (-jnp.arange(half_dim, dtype=jnp.float32) * 2.0 / HEAD_DIM)
    angles = positions.astype(jnp.float32)[:, None] * frequency[None, :]
    return (jnp.cos(angles), jnp.sin(angles))


def apply_rotary(values, cosine_table, sine_values):
    half_dim = values.shape[-1] // 2
    first_half = values[..., :half_dim]
    second_half = values[..., half_dim:]
    cos_rows = cosine_table[:, None, :]
    sin_rows = sine_values[:, None, :]
    return jnp.concatenate(
        [
            first_half * cos_rows - second_half * sin_rows,
            second_half * cos_rows + first_half * sin_rows,
        ],
        axis=-1,
    )


def unapply_rotary(grad_values, cosine_table, sine_values):
    half_dim = grad_values.shape[-1] // 2
    first_half = grad_values[..., :half_dim]
    second_half = grad_values[..., half_dim:]
    cos_rows = cosine_table[:, None, :]
    sin_rows = sine_values[:, None, :]
    return jnp.concatenate(
        [
            first_half * cos_rows + second_half * sin_rows,
            second_half * cos_rows - first_half * sin_rows,
        ],
        axis=-1,
    )


def norm_back(values, root_rows, gain, grad_out):
    normed = values * root_rows
    grad_normed = grad_out * gain
    grad_rows = root_rows * (
        grad_normed - normed * jnp.mean(grad_normed * normed, axis=-1, keepdims=True)
    )
    return (grad_rows, jnp.sum(grad_out * normed, axis=0))


def choose_by(flags, high_value, low_value):
    rank = max(high_value.ndim, low_value.ndim)
    shaped = flags.reshape(flags.shape + (1,) * (rank - 1))
    return jnp.where(shaped, high_value, low_value)


def split_piece(key_value_portion, first_row, pair_table, rows_per_block, shards):
    partition_count = key_value_portion.shape[0] // (2 * rows_per_block)
    first_shard = first_row // (2 * rows_per_block)
    pair_ids = lax.dynamic_slice_in_dim(pair_table, first_shard, partition_count)
    portions = key_value_portion.reshape(
        partition_count, 2, rows_per_block, 2, KEY_VALUE_HEADS, HEAD_DIM
    )
    offsets = jnp.arange(rows_per_block, dtype=jnp.int32)
    low_pos = pair_ids[:, None] * rows_per_block + offsets[None, :]
    high_pos = (2 * shards - 1 - pair_ids[:, None]) * rows_per_block + offsets[None, :]
    return (pair_ids, portions[:, :, :, 0], portions[:, :, :, 1], low_pos, high_pos)


def on_device(
    tokens,
    pair_of,
    gain_attn,
    w_query,
    key_weight,
    value_weight,
    w_out,
    gain_ffn,
    w_gate,
    w_up,
    w_down,
    cotangent,
):
    rows_per_block = tokens.shape[1] // 2
    rows_of_token = 2 * rows_per_block
    model_width = tokens.shape[2]
    shards = lax.axis_size("ctx")
    fsdp_size = lax.axis_size("fsdp")
    my_index = lax.axis_index("ctx")
    query_group_width = QUERY_HEADS // KEY_VALUE_HEADS
    key_value_width = KEY_VALUE_HEADS * HEAD_DIM
    score_scale = 1.0 / math.sqrt(HEAD_DIM)
    groups = shards // group_shards
    piece_rows = group_shards * rows_of_token
    offsets = jnp.arange(rows_per_block, dtype=jnp.int32)
    diagonal_mask = offsets[None, :] <= offsets[:, None]
    sliced = (
        lax.all_gather(w_query, "ctx", axis=1, tiled=True),
        lax.all_gather(key_weight, "ctx", axis=1, tiled=True),
        lax.all_gather(value_weight, "ctx", axis=1, tiled=True),
        lax.all_gather(w_out, "ctx", axis=1, tiled=True),
        lax.all_gather(w_gate, "ctx", axis=1, tiled=True),
        lax.all_gather(w_up, "ctx", axis=1, tiled=True),
        lax.all_gather(w_down, "ctx", axis=1, tiled=True),
        lax.all_gather(gain_attn, "ctx", axis=0, tiled=True),
        lax.all_gather(gain_ffn, "ctx", axis=0, tiled=True),
    )
    wq_full, wk_full, wv_full, wo_full, wg_full, wu_full, wd_full = (
        lax.all_gather(sliced[0], "fsdp", axis=0, tiled=True),
        lax.all_gather(sliced[1], "fsdp", axis=0, tiled=True),
        lax.all_gather(sliced[2], "fsdp", axis=0, tiled=True),
        lax.all_gather(sliced[3], "fsdp", axis=0, tiled=True),
        lax.all_gather(sliced[4], "fsdp", axis=0, tiled=True),
        lax.all_gather(sliced[5], "fsdp", axis=0, tiled=True),
        lax.all_gather(sliced[6], "fsdp", axis=0, tiled=True),
    )
    gain_first = sliced[7].astype(jnp.float32)
    gain_second = sliced[8].astype(jnp.float32)
    totals = None
    pair_table = pair_of[0]
    my_pair = pair_table[my_index]
    my_pos = jnp.stack(
        [my_pair * rows_per_block + offsets, (2 * shards - 1 - my_pair) * rows_per_block + offsets]
    )
    cosine_table, sine_values = rotary_tables(my_pos.reshape(-1))
    inputs = tokens[0].astype(jnp.float32)
    first_root = inverse_root(inputs)
    normed_attn = (inputs * first_root * gain_first).astype(jnp.bfloat16)
    query_pre = jnp.dot(normed_attn, wq_full, preferred_element_type=jnp.float32)
    key_unrotated = jnp.dot(normed_attn, wk_full, preferred_element_type=jnp.float32)
    values_low = jnp.dot(normed_attn, wv_full, preferred_element_type=jnp.float32).astype(
        jnp.bfloat16
    )
    query_matrix = apply_rotary(
        query_pre.reshape(rows_of_token, QUERY_HEADS, HEAD_DIM), cosine_table, sine_values
    ).astype(jnp.bfloat16)
    rotated_key_rows = apply_rotary(
        key_unrotated.reshape(rows_of_token, KEY_VALUE_HEADS, HEAD_DIM), cosine_table, sine_values
    ).astype(jnp.bfloat16)
    local_key_value = jnp.concatenate(
        [rotated_key_rows.reshape(rows_of_token, key_value_width), values_low], axis=1
    )
    blocks_of_query = query_matrix.reshape(
        2, rows_per_block, KEY_VALUE_HEADS, query_group_width, HEAD_DIM
    )
    local_lower = local_key_value[:rows_per_block].reshape(
        rows_per_block, 2, KEY_VALUE_HEADS, HEAD_DIM
    )
    own_keys = local_lower[:, 0]
    own_values = local_lower[:, 1]

    def second_visibility(upper_flags, low_pos, high_pos):
        chosen_qpos = choose_by(upper_flags, my_pos[1][None], my_pos[0][None])
        chosen_kpos = choose_by(upper_flags, high_pos, low_pos)
        return chosen_kpos[:, None, None, None, :] <= chosen_qpos[:, None, None, :, None]

    own_scores = (
        jnp.einsum(
            "rgjd,kgd->gjrk", blocks_of_query[0], own_keys, preferred_element_type=jnp.float32
        )
        * score_scale
    )
    own_scores = jnp.where(diagonal_mask, own_scores, masked_fill)
    own_max = jnp.max(own_scores, axis=-1)
    own_weights = jnp.exp(own_scores - own_max[..., None])
    own_out = jnp.einsum(
        "gjrk,kgd->gjrd",
        own_weights.astype(jnp.bfloat16),
        own_values,
        preferred_element_type=jnp.float32,
    )
    maxima = jnp.stack([own_max, jnp.full_like(own_max, masked_fill)])
    totals = jnp.stack([jnp.sum(own_weights, axis=-1), jnp.zeros_like(own_max)])
    sums_out = jnp.stack([own_out, jnp.zeros_like(own_out)])
    pair_ids, key_portion, value_portion, low_pos, high_pos = split_piece(
        lax.all_gather(local_key_value, "ctx", axis=0, tiled=True),
        jnp.int32(0),
        pair_table,
        rows_per_block,
        shards,
    )
    partition_count = pair_ids.shape[0]
    upper_flags = pair_ids >= my_pair
    flag_rows = upper_flags[:, None, None, None]
    flag_outs = upper_flags[:, None, None, None, None]
    lower_keys = key_portion[:, 0].reshape(
        partition_count * rows_per_block, KEY_VALUE_HEADS, HEAD_DIM
    )
    lower_values = value_portion[:, 0].reshape(
        partition_count * rows_per_block, KEY_VALUE_HEADS, HEAD_DIM
    )
    first_scores = (
        jnp.einsum(
            "rgjd,kgd->gjrk", blocks_of_query[1], lower_keys, preferred_element_type=jnp.float32
        )
        * score_scale
    )
    chosen_queries = choose_by(upper_flags, blocks_of_query[1][None], blocks_of_query[0][None])
    chosen_keys = choose_by(upper_flags, key_portion[:, 1], key_portion[:, 0])
    chosen_values = choose_by(upper_flags, value_portion[:, 1], value_portion[:, 0])
    visible = second_visibility(upper_flags, low_pos, high_pos)
    second_scores = (
        jnp.einsum(
            "nrgjd,nkgd->ngjrk", chosen_queries, chosen_keys, preferred_element_type=jnp.float32
        )
        * score_scale
    )
    second_scores = jnp.where(visible, second_scores, masked_fill)
    second_max = jnp.max(second_scores, axis=-1)
    low_block_max = jnp.max(jnp.where(flag_rows, masked_fill, second_max), axis=0)
    high_block_max = jnp.maximum(
        jnp.max(jnp.where(flag_rows, second_max, masked_fill), axis=0),
        jnp.max(first_scores, axis=-1),
    )
    new_max = jnp.maximum(maxima, jnp.stack([low_block_max, high_block_max]))
    rescale = jnp.exp(maxima - new_max)
    first_weights = jnp.exp(first_scores - new_max[1][..., None])
    chosen_max = jnp.where(flag_rows, new_max[1][None], new_max[0][None])
    second_weights = jnp.exp(second_scores - chosen_max[..., None])
    second_sums = jnp.sum(second_weights, axis=-1)
    low_add = jnp.sum(jnp.where(flag_rows, 0.0, second_sums), axis=0)
    high_add = jnp.sum(jnp.where(flag_rows, second_sums, 0.0), axis=0) + jnp.sum(
        first_weights, axis=-1
    )
    new_totals = totals * rescale + jnp.stack([low_add, high_add])
    first_out = jnp.einsum(
        "gjrk,kgd->gjrd",
        first_weights.astype(jnp.bfloat16),
        lower_values,
        preferred_element_type=jnp.float32,
    )
    second_out = jnp.einsum(
        "ngjrk,nkgd->ngjrd",
        second_weights.astype(jnp.bfloat16),
        chosen_values,
        preferred_element_type=jnp.float32,
    )
    low_out = jnp.sum(jnp.where(flag_outs, 0.0, second_out), axis=0)
    high_out = jnp.sum(jnp.where(flag_outs, second_out, 0.0), axis=0) + first_out
    new_sums = sums_out * rescale[..., None] + jnp.stack([low_out, high_out])
    log_totals = new_max + jnp.log(new_totals)
    attended_f32 = (
        (new_sums / new_totals[..., None])
        .transpose(0, 3, 1, 2, 4)
        .reshape(rows_of_token, QUERY_HEADS * HEAD_DIM)
    )
    attended = attended_f32.astype(jnp.bfloat16)
    middle = inputs + jnp.dot(attended, wo_full, preferred_element_type=jnp.float32)
    second_root = inverse_root(middle)
    normed_ffn = (middle * second_root * gain_second).astype(jnp.bfloat16)
    gate = jnp.dot(normed_ffn, wg_full, preferred_element_type=jnp.float32)
    up_part = jnp.dot(normed_ffn, wu_full, preferred_element_type=jnp.float32)
    hidden = (jax.nn.silu(gate) * up_part).astype(jnp.bfloat16)
    output = (middle + jnp.dot(hidden, wd_full, preferred_element_type=jnp.float32)).astype(
        jnp.bfloat16
    )
    grad_out_low = cotangent[0]
    grad_out = grad_out_low.astype(jnp.float32)
    grad_wd = jnp.einsum("rf,rd->fd", hidden, grad_out_low, preferred_element_type=jnp.float32)
    grad_hidden = jnp.einsum("rd,fd->rf", grad_out_low, wd_full, preferred_element_type=jnp.float32)
    sigmoid_gate = jax.nn.sigmoid(gate)
    grad_gate = (grad_hidden * up_part * sigmoid_gate * (1.0 + gate * (1.0 - sigmoid_gate))).astype(
        jnp.bfloat16
    )
    grad_up = (grad_hidden * jax.nn.silu(gate)).astype(jnp.bfloat16)
    grad_wg = jnp.einsum("rd,rf->df", normed_ffn, grad_gate, preferred_element_type=jnp.float32)
    grad_wu = jnp.einsum("rd,rf->df", normed_ffn, grad_up, preferred_element_type=jnp.float32)
    grad_normed_ffn = jnp.einsum(
        "rf,df->rd", grad_gate, wg_full, preferred_element_type=jnp.float32
    ) + jnp.einsum("rf,df->rd", grad_up, wu_full, preferred_element_type=jnp.float32)
    grad_norm_mid, grad_gain_second = norm_back(middle, second_root, gain_second, grad_normed_ffn)
    grad_middle = grad_out + grad_norm_mid
    grad_branch = grad_middle.astype(jnp.bfloat16)
    grad_wo = jnp.einsum("rq,rd->qd", attended, grad_branch, preferred_element_type=jnp.float32)
    attended_gradient = jnp.einsum(
        "rd,qd->rq", grad_branch, wo_full, preferred_element_type=jnp.float32
    ).astype(jnp.bfloat16)
    row_delta = jnp.sum(
        (attended_gradient.astype(jnp.float32) * attended_f32).reshape(
            2, rows_per_block, KEY_VALUE_HEADS, query_group_width, HEAD_DIM
        ),
        axis=-1,
    ).transpose(0, 2, 3, 1)
    gradient_blocks = attended_gradient.reshape(
        2, rows_per_block, KEY_VALUE_HEADS, query_group_width, HEAD_DIM
    )

    def backward_step(key_value_portion, first_row):
        pair_ids, key_portion, value_portion, low_pos, high_pos = split_piece(
            key_value_portion, first_row, pair_table, rows_per_block, shards
        )
        partition_count = pair_ids.shape[0]
        upper_flags = pair_ids >= my_pair
        flag_rows = upper_flags[:, None, None, None]
        flag_query = upper_flags[:, None, None, None, None]
        lower_keys = key_portion[:, 0].reshape(
            partition_count * rows_per_block, KEY_VALUE_HEADS, HEAD_DIM
        )
        lower_values = value_portion[:, 0].reshape(
            partition_count * rows_per_block, KEY_VALUE_HEADS, HEAD_DIM
        )
        first_scores = (
            jnp.einsum(
                "rgjd,kgd->gjrk", blocks_of_query[1], lower_keys, preferred_element_type=jnp.float32
            )
            * score_scale
        )
        first_probs = jnp.exp(first_scores - log_totals[1][..., None])
        first_dprob = jnp.einsum(
            "rgjd,kgd->gjrk", gradient_blocks[1], lower_values, preferred_element_type=jnp.float32
        )
        first_dscore = (first_probs * (first_dprob - row_delta[1][..., None]) * score_scale).astype(
            jnp.bfloat16
        )
        lower_value_gradient = jnp.einsum(
            "gjrk,rgjd->kgd",
            first_probs.astype(jnp.bfloat16),
            gradient_blocks[1],
            preferred_element_type=jnp.float32,
        )
        lower_key_gradient = jnp.einsum(
            "gjrk,rgjd->kgd", first_dscore, blocks_of_query[1], preferred_element_type=jnp.float32
        )
        high_query_grad = jnp.einsum(
            "gjrk,kgd->rgjd", first_dscore, lower_keys, preferred_element_type=jnp.float32
        )
        chosen_queries = choose_by(upper_flags, blocks_of_query[1][None], blocks_of_query[0][None])
        chosen_grads = choose_by(upper_flags, gradient_blocks[1][None], gradient_blocks[0][None])
        chosen_keys = choose_by(upper_flags, key_portion[:, 1], key_portion[:, 0])
        chosen_values = choose_by(upper_flags, value_portion[:, 1], value_portion[:, 0])
        visible = second_visibility(upper_flags, low_pos, high_pos)
        second_scores = (
            jnp.einsum(
                "nrgjd,nkgd->ngjrk", chosen_queries, chosen_keys, preferred_element_type=jnp.float32
            )
            * score_scale
        )
        second_scores = jnp.where(visible, second_scores, masked_fill)
        chosen_totals = jnp.where(flag_rows, log_totals[1][None], log_totals[0][None])
        chosen_delta = jnp.where(flag_rows, row_delta[1][None], row_delta[0][None])
        second_probs = jnp.exp(second_scores - chosen_totals[..., None])
        second_dprob = jnp.einsum(
            "nrgjd,nkgd->ngjrk", chosen_grads, chosen_values, preferred_element_type=jnp.float32
        )
        second_dscore = (
            second_probs * (second_dprob - chosen_delta[..., None]) * score_scale
        ).astype(jnp.bfloat16)
        chosen_value_grad = jnp.einsum(
            "ngjrk,nrgjd->nkgd",
            second_probs.astype(jnp.bfloat16),
            chosen_grads,
            preferred_element_type=jnp.float32,
        )
        chosen_key_grad = jnp.einsum(
            "ngjrk,nrgjd->nkgd", second_dscore, chosen_queries, preferred_element_type=jnp.float32
        )
        chosen_query_grad = jnp.einsum(
            "ngjrk,nkgd->nrgjd", second_dscore, chosen_keys, preferred_element_type=jnp.float32
        )
        low_query_grad = jnp.sum(jnp.where(flag_query, 0.0, chosen_query_grad), axis=0)
        high_query_grad = high_query_grad + jnp.sum(
            jnp.where(flag_query, chosen_query_grad, 0.0), axis=0
        )
        lower_key_part = lower_key_gradient.reshape(
            partition_count, rows_per_block, KEY_VALUE_HEADS, HEAD_DIM
        ) + jnp.where(flag_rows, 0.0, chosen_key_grad)
        key_high_part = jnp.where(flag_rows, chosen_key_grad, 0.0)
        lower_value_part = lower_value_gradient.reshape(
            partition_count, rows_per_block, KEY_VALUE_HEADS, HEAD_DIM
        ) + jnp.where(flag_rows, 0.0, chosen_value_grad)
        value_high_part = jnp.where(flag_rows, chosen_value_grad, 0.0)
        key_grads = jnp.stack([lower_key_part, key_high_part], axis=1)
        value_grads = jnp.stack([lower_value_part, value_high_part], axis=1)
        joined = jnp.stack([key_grads, value_grads], axis=3)
        return (
            joined.reshape(partition_count * rows_of_token, 2 * key_value_width),
            jnp.stack([low_query_grad, high_query_grad]),
        )

    kv_whole = lax.all_gather(local_key_value, "ctx", axis=0, tiled=True)

    def grad_loop(step_index, state):
        grad_whole, grad_query = state
        first_row = step_index * piece_rows
        key_value_portion = lax.dynamic_slice_in_dim(kv_whole, first_row, piece_rows)
        kv_grad, query_grad = backward_step(key_value_portion, first_row)
        grad_whole = lax.dynamic_update_slice_in_dim(grad_whole, kv_grad, first_row, 0)
        return (grad_whole, grad_query + query_grad)

    empty_whole = jnp.zeros((shards * rows_of_token, 2 * key_value_width), jnp.float32)
    blank_query = jnp.zeros(
        (2, rows_per_block, KEY_VALUE_HEADS, query_group_width, HEAD_DIM), jnp.float32
    )
    grad_whole, grad_query = lax.fori_loop(0, groups, grad_loop, (empty_whole, blank_query))
    own_probs = jnp.exp(own_scores - log_totals[0][..., None])
    own_dprob = jnp.einsum(
        "rgjd,kgd->gjrk", gradient_blocks[0], own_values, preferred_element_type=jnp.float32
    )
    own_dscore = (own_probs * (own_dprob - row_delta[0][..., None]) * score_scale).astype(
        jnp.bfloat16
    )
    own_value_grad = jnp.einsum(
        "gjrk,rgjd->kgd",
        own_probs.astype(jnp.bfloat16),
        gradient_blocks[0],
        preferred_element_type=jnp.float32,
    )
    own_key_grad = jnp.einsum(
        "gjrk,rgjd->kgd", own_dscore, blocks_of_query[0], preferred_element_type=jnp.float32
    )
    own_query_grad = jnp.einsum(
        "gjrk,kgd->rgjd", own_dscore, own_keys, preferred_element_type=jnp.float32
    )
    grad_query = grad_query + jnp.stack([own_query_grad, jnp.zeros_like(own_query_grad)])
    summed_key_value = lax.psum_scatter(grad_whole, "ctx", scatter_dimension=0, tiled=True)
    own_rows = jnp.concatenate(
        [
            own_key_grad.reshape(rows_per_block, key_value_width),
            own_value_grad.reshape(rows_per_block, key_value_width),
        ],
        axis=1,
    )
    summed_key_value = summed_key_value + jnp.concatenate(
        [own_rows, jnp.zeros_like(own_rows)], axis=0
    )
    grad_key_pre = (
        unapply_rotary(
            summed_key_value[:, :key_value_width].reshape(rows_of_token, KEY_VALUE_HEADS, HEAD_DIM),
            cosine_table,
            sine_values,
        )
        .reshape(rows_of_token, key_value_width)
        .astype(jnp.bfloat16)
    )
    grad_values = summed_key_value[:, key_value_width:].astype(jnp.bfloat16)
    grad_query_pre = (
        unapply_rotary(
            grad_query.reshape(rows_of_token, QUERY_HEADS, HEAD_DIM), cosine_table, sine_values
        )
        .reshape(rows_of_token, QUERY_HEADS * HEAD_DIM)
        .astype(jnp.bfloat16)
    )
    grad_wq = jnp.einsum(
        "rd,re->de", normed_attn, grad_query_pre, preferred_element_type=jnp.float32
    )
    grad_wk = jnp.einsum("rd,re->de", normed_attn, grad_key_pre, preferred_element_type=jnp.float32)
    grad_wv = jnp.einsum("rd,re->de", normed_attn, grad_values, preferred_element_type=jnp.float32)
    grad_normed_attn = jnp.einsum(
        "re,de->rd", grad_query_pre, wq_full, preferred_element_type=jnp.float32
    )
    grad_normed_attn = grad_normed_attn + jnp.einsum(
        "re,de->rd", grad_key_pre, wk_full, preferred_element_type=jnp.float32
    )
    grad_normed_attn = grad_normed_attn + jnp.einsum(
        "re,de->rd", grad_values, wv_full, preferred_element_type=jnp.float32
    )
    grad_norm_in, grad_gain_first = norm_back(inputs, first_root, gain_first, grad_normed_attn)
    grad_input = grad_middle + grad_norm_in
    weight_terms = (
        grad_wq,
        grad_wk,
        grad_wv,
        grad_wo,
        grad_wg,
        grad_wu,
        grad_wd,
        grad_gain_first,
        grad_gain_second,
    )
    outputs_list = [output]
    inputs_list = [grad_input]
    (
        grad_wq,
        grad_wk,
        grad_wv,
        grad_wo,
        grad_wg,
        grad_wu,
        grad_wd,
        grad_gain_first,
        grad_gain_second,
    ) = weight_terms
    tiled_first = jnp.broadcast_to(grad_gain_first[None], (fsdp_size, model_width))
    tiled_second = jnp.broadcast_to(grad_gain_second[None], (fsdp_size, model_width))
    parted = (
        lax.psum_scatter(
            grad_wq.astype(jnp.bfloat16), "fsdp", scatter_dimension=0, tiled=True
        ).astype(jnp.float32),
        lax.psum_scatter(
            grad_wk.astype(jnp.bfloat16), "fsdp", scatter_dimension=0, tiled=True
        ).astype(jnp.float32),
        lax.psum_scatter(
            grad_wv.astype(jnp.bfloat16), "fsdp", scatter_dimension=0, tiled=True
        ).astype(jnp.float32),
        lax.psum_scatter(
            grad_wo.astype(jnp.bfloat16), "fsdp", scatter_dimension=0, tiled=True
        ).astype(jnp.float32),
        lax.psum_scatter(
            grad_wg.astype(jnp.bfloat16), "fsdp", scatter_dimension=0, tiled=True
        ).astype(jnp.float32),
        lax.psum_scatter(
            grad_wu.astype(jnp.bfloat16), "fsdp", scatter_dimension=0, tiled=True
        ).astype(jnp.float32),
        lax.psum_scatter(
            grad_wd.astype(jnp.bfloat16), "fsdp", scatter_dimension=0, tiled=True
        ).astype(jnp.float32),
        lax.psum_scatter(
            tiled_first.astype(jnp.bfloat16), "fsdp", scatter_dimension=0, tiled=True
        ).astype(jnp.float32),
        lax.psum_scatter(
            tiled_second.astype(jnp.bfloat16), "fsdp", scatter_dimension=0, tiled=True
        ).astype(jnp.float32),
    )
    owned = (
        lax.psum_scatter(parted[0], "ctx", scatter_dimension=1, tiled=True),
        lax.psum_scatter(parted[1], "ctx", scatter_dimension=1, tiled=True),
        lax.psum_scatter(parted[2], "ctx", scatter_dimension=1, tiled=True),
        lax.psum_scatter(parted[3], "ctx", scatter_dimension=1, tiled=True),
        lax.psum_scatter(parted[4], "ctx", scatter_dimension=1, tiled=True),
        lax.psum_scatter(parted[5], "ctx", scatter_dimension=1, tiled=True),
        lax.psum_scatter(parted[6], "ctx", scatter_dimension=1, tiled=True),
        lax.psum_scatter(parted[7][0], "ctx", scatter_dimension=0, tiled=True),
        lax.psum_scatter(parted[8][0], "ctx", scatter_dimension=0, tiled=True),
    )
    gain_first_out = owned[7]
    gain_second_out = owned[8]
    return (
        jnp.stack(outputs_list),
        jnp.stack(inputs_list),
        gain_first_out,
        owned[0],
        owned[1],
        owned[2],
        owned[3],
        gain_second_out,
        owned[4],
        owned[5],
        owned[6],
    )


def solution(mesh):
    in_specs = (
        P("fsdp", "ctx", None),
        P("fsdp", None),
        P("ctx"),
        P("fsdp", "ctx"),
        P("fsdp", "ctx"),
        P("fsdp", "ctx"),
        P("fsdp", "ctx"),
        P("ctx"),
        P("fsdp", "ctx"),
        P("fsdp", "ctx"),
        P("fsdp", "ctx"),
        P("fsdp", "ctx", None),
    )
    out_specs = (
        P("fsdp", "ctx", None),
        P("fsdp", "ctx", None),
        P("ctx"),
        P("fsdp", "ctx"),
        P("fsdp", "ctx"),
        P("fsdp", "ctx"),
        P("fsdp", "ctx"),
        P("ctx"),
        P("fsdp", "ctx"),
        P("fsdp", "ctx"),
        P("fsdp", "ctx"),
    )
    return jax.shard_map(
        on_device, mesh=mesh, in_specs=in_specs, out_specs=out_specs, check_vma=False
    )
```

profile of v0, /device:TPU:0, one launch (start us, length us, event | category | flops | bytes accessed | tf_op | source)
XLA Modules:
  0.0 1132.9 jit_solution(2677370847967831493)
XLA Ops:
  7.2 33.6 %all-gather = bf16[8,192,144]{1,2,0:T(8,128)(2,1)S(1)} all-gather(bf16[1,192,144]{1,2,0:T(8,128)(2,1)} %bitcast.609), channel_id=1, replica_groups=mesh['ctx'=8,'fsdp'=4] {'ctx'}, dimensions={0}, use_global_device_ids=true | all-gather | bytes 497664 | tf_op jit(solution)/shard_map/all_gather | solution.py:120
  42.3 31.5 %all-gather.1 = bf16[8,192,144]{1,2,0:T(8,128)(2,1)S(1)} all-gather(bf16[1,192,144]{1,2,0:T(8,128)(2,1)S(1)} %bitcast.610), channel_id=1, replica_groups=mesh['ctx'=8,'fsdp'=4] {'ctx'}, dimensions={0}, use_global_device_ids=true | all-gather | bytes 497664 | tf_op jit(solution)/shard_map/all_gather | solution.py:121
  75.4 33.1 %all_gather.67 = bf16[384,576]{0,1:T(8,128)(2,1)} all-gather(bf16[384,72]{0,1:T(8,128)(2,1)S(1)} %copy-done.66), channel_id=1, replica_groups=mesh['ctx'=8,'fsdp'=4] {'ctx'}, dimensions={1}, use_global_device_ids=true | all-gather | bytes 497664 | tf_op jit(solution)/shard_map/all_gather | solution.py:122
  112.2 30.6 %all_gather.55 = bf16[144,192]{0,1:T(8,128)(2,1)S(1)} all-gather(bf16[144,24]{0,1:T(8,128)(2,1)S(1)} %copy-done.75), channel_id=1, replica_groups=mesh['ctx'=8,'fsdp'=4] {'ctx'}, dimensions={1}, use_global_device_ids=true | all-gather | bytes 62208 | tf_op jit(solution)/shard_map/all_gather | solution.py:118
  150.6 22.4 %all-reduce.13 = (bf16[576]{0:T(1024)(128)(2,1)S(1)}, bf16[576]{0:T(1024)(128)(2,1)}) all-reduce(bf16[576]{0:T(1024)(128)(2,1)S(1)} %dynamic-update-slice, bf16[576]{0:T(1024)(128)(2,1)S(1)} %dynamic-update-slice.1), channel_id=1, replica_groups=mesh['ctx'=8,'fsdp'=4] {'ctx'}, use_global_device_ids=true, to_apply=%add.5 | all-reduce | flops 1152 | bytes 4608
  173.1 30.6 %all_gather.53 = bf16[144,192]{0,1:T(8,128)(2,1)S(1)} all-gather(bf16[144,24]{0,1:T(8,128)(2,1)S(1)} %copy-done.76), channel_id=1, replica_groups=mesh['ctx'=8,'fsdp'=4] {'ctx'}, dimensions={1}, use_global_device_ids=true | all-gather | bytes 62208 | tf_op jit(solution)/shard_map/all_gather | solution.py:117
  211.7 30.8 %all_gather.57 = bf16[144,576]{0,1:T(8,128)(2,1)S(1)} all-gather(bf16[144,72]{0,1:T(8,128)(2,1)S(1)} %copy.379), channel_id=1, replica_groups=mesh['ctx'=8,'fsdp'=4] {'ctx'}, dimensions={1}, use_global_device_ids=true | all-gather | bytes 186624 | tf_op jit(solution)/shard_map/all_gather | solution.py:116
  254.9 30.0 %all_gather.59 = bf16[1024,384]{0,1:T(8,128)(2,1)} all-gather(bf16[128,384]{0,1:T(8,128)(2,1)S(1)} %pad_maximum_fusion.3), channel_id=1, replica_groups=mesh['ctx'=8,'fsdp'=4] {'ctx'}, dimensions={0}, use_global_device_ids=true | all-gather | bytes 884736 | tf_op jit(solution)/shard_map/all_gather | solution.py:194
  299.7 30.9 %all_gather.60 = bf16[144,576]{0,1:T(8,128)(2,1)S(1)} all-gather(bf16[144,72]{0,1:T(8,128)(2,1)S(1)} %copy-done.62), channel_id=1, replica_groups=mesh['ctx'=8,'fsdp'=4] {'ctx'}, dimensions={1}, use_global_device_ids=true | all-gather | bytes 186624 | tf_op jit(solution)/shard_map/all_gather | solution.py:119
  362.8 49.9 %while.18 = (s32[]{:T(128)}, f32[1024,384]{0,1:T(8,128)}, f32[2,64,3,3,64]{1,4,3,2,0:T(8,128)}, bf16[1024,384]{0,1:T(8,128)(2,1)}, bf16[2,64,3,3,64]{4,1,3,2,0:T...) while((s32[]{:T(128)}, f32[1024,384]{0,1:T(8,128)}, ...), condition=%wide.region_19.20_spmd.clone, body=%wide.region_16.19_spmd.clone.sunk | while | flops 193177248 | bytes 32036296 | solution.py:412
  423.5 52.3 %reduce-scatter.32.cloned.1.call-done = f32[128,384]{0,1:T(8,128)} async-done(((f32[1024,384]{0,1:T(8,128)}), f32[128,384]{0,1:T(8,128)}) %reduce-scatter.32.cloned.1.call-update) | async-done | bytes 196624 | tf_op jit(solution)/shard_map/reduce_scatter | solution.py:433
  502.3 23.4 %reduce-scatter.40.cloned.1.call-done = bf16[144,576]{1,0:T(8,128)(2,1)} async-done(((bf16[576,576]{1,0:T(8,128)(2,1)}), bf16[144,576]{1,0:T(8,128)(2,1)}) %reduce-scatter.40.cloned.1.call-update) | async-done | bytes 165904 | tf_op jit(solution)/shard_map/reduce_scatter | solution.py:513
  527.7 30.2 %reduce-scatter.42.cloned.1.call-done = bf16[144,1536]{1,0:T(8,128)(2,1)} async-done(((bf16[576,1536]{1,0:T(8,128)(2,1)}), bf16[144,1536]{1,0:T(8,128)(2,1)}) %reduce-scatter.42.cloned.1.call-update) | async-done | bytes 442384 | tf_op jit(solution)/shard_map/reduce_scatter | solution.py:516
  560.4 29.5 %reduce-scatter.44.cloned.1.call-done = bf16[144,1536]{1,0:T(8,128)(2,1)} async-done(((bf16[576,1536]{1,0:T(8,128)(2,1)}), bf16[144,1536]{1,0:T(8,128)(2,1)}) %reduce-scatter.44.cloned.1.call-update) | async-done | bytes 442384 | tf_op jit(solution)/shard_map/reduce_scatter | solution.py:519
  592.5 20.4 %reduce-scatter.36.cloned.1.call-done = bf16[144,192]{1,0:T(8,128)(2,1)} async-done(((bf16[576,192]{1,0:T(8,128)(2,1)}), bf16[144,192]{1,0:T(8,128)(2,1)}) %reduce-scatter.36.cloned.1.call-update) | async-done | bytes 55312 | tf_op jit(solution)/shard_map/reduce_scatter | solution.py:507
  614.6 20.9 %reduce-scatter.38.cloned.1.call-done = bf16[144,192]{1,0:T(8,128)(2,1)} async-done(((bf16[576,192]{1,0:T(8,128)(2,1)}), bf16[144,192]{1,0:T(8,128)(2,1)}) %reduce-scatter.38.cloned.1.call-update) | async-done | bytes 55312 | tf_op jit(solution)/shard_map/reduce_scatter | solution.py:510
  637.3 31.6 %reduce-scatter.58.cloned.1.call-done = bf16[384,576]{1,0:T(8,128)(2,1)} async-done(((bf16[1536,576]{1,0:T(8,128)(2,1)}), bf16[384,576]{1,0:T(8,128)(2,1)}) %reduce-scatter.58.cloned.1.call-update) | async-done | bytes 442384
  675.7 58.5 %reduce-scatter.46.cloned.1.call-done = f32[72,144]{1,0:T(8,128)} async-done(((f32[576,144]{1,0:T(8,128)}), f32[72,144]{1,0:T(8,128)}) %reduce-scatter.46.cloned.1.call-update) | async-done | bytes 41488
  735.8 63.2 %reduce-scatter.52.cloned.1.call-done = f32[72,144]{1,0:T(8,128)} async-done(((f32[576,144]{1,0:T(8,128)}), f32[72,144]{1,0:T(8,128)}) %reduce-scatter.52.cloned.1.call-update) | async-done | bytes 41488
  834.6 31.8 %reduce-scatter.54.cloned.1.call-done = f32[192,144]{1,0:T(8,128)} async-done(((f32[1536,144]{1,0:T(8,128)}), f32[192,144]{1,0:T(8,128)}) %reduce-scatter.54.cloned.1.call-update) | async-done | bytes 110608
  868.2 65.7 %reduce-scatter.56.cloned.1.call-done = f32[192,144]{1,0:T(8,128)} async-done(((f32[1536,144]{1,0:T(8,128)}), f32[192,144]{1,0:T(8,128)}) %reduce-scatter.56.cloned.1.call-update) | async-done | bytes 110608
  935.6 62.1 %reduce-scatter.48.cloned.1.call-done = f32[24,144]{1,0:T(8,128)} async-done(((f32[192,144]{1,0:T(8,128)}), f32[24,144]{1,0:T(8,128)}) %reduce-scatter.48.cloned.1.call-update) | async-done | bytes 13840
  997.7 63.8 %reduce-scatter.50.cloned.1.call-done = f32[24,144]{1,0:T(8,128)} async-done(((f32[192,144]{1,0:T(8,128)}), f32[24,144]{1,0:T(8,128)}) %reduce-scatter.50.cloned.1.call-update) | async-done | bytes 13840
  1061.5 64.1 %reduce-scatter.60.cloned.1.call-done = f32[384,72]{0,1:T(8,128)} async-done(((f32[384,576]{0,1:T(8,128)}), f32[384,72]{0,1:T(8,128)}) %reduce-scatter.60.cloned.1.call-update) | async-done | bytes 110608
  (486 shorter events, 222.2 us)
Async XLA Ops:
  7.2 340.3 %all-gather.6.cloned.1.call-start = ((), (), s32[]{:S(2)}) async-start(), calls=%async_computation.15 | async-start | bytes 2211840 | tf_op jit(solution)/shard_map/all_gather | solution.py:131
  42.3 308.1 %all-gather.8.cloned.1.call-start = ((), (), s32[]{:S(2)}) async-start(), calls=%async_computation.16 | async-start | bytes 2211840 | tf_op jit(solution)/shard_map/all_gather | solution.py:132
  74.0 99.0 %copy-start.6 = (bf16[1,128,576]{1,2,0:T(8,128)(2,1)S(1)}, bf16[1,128,576]{1,2,0:T(8,128)(2,1)}, u32[]{:S(2)}) copy-start(bf16[1,128,576]{1,2,0:T(8,128)(2,1)} %param.14) | copy-start | bytes 442372
  74.0 99.1 %copy-start.76 = (bf16[144,24]{0,1:T(8,128)(2,1)S(1)}, bf16[144,24]{0,1:T(8,128)(2,1)}, u32[]{:S(2)}) copy-start(bf16[144,24]{0,1:T(8,128)(2,1)} %param.18) | copy-start | bytes 20740
  75.3 278.0 %all-gather.10.cloned.1.call-start = ((), (), s32[]{:S(2)}) async-start(), calls=%async_computation.17 | async-start | bytes 2211840 | tf_op jit(solution)/shard_map/all_gather | solution.py:133
  108.5 367.3 %reduce-scatter.32.cloned.1.call-start = ((), (), s32[]{:S(2)}) async-start(), calls=%async_computation.18 | async-start | bytes 1769472 | tf_op jit(solution)/shard_map/reduce_scatter | solution.py:433
  210.9 122.0 %copy-start.40 = (bf16[64,384]{0,1:T(8,128)(2,1)}, bf16[64,384]{0,1:T(8,128)(2,1)S(1)}, u32[]{:S(2)}) copy-start(bf16[64,384]{0,1:T(8,128)(2,1)S(1)} %fusion.126) | copy-start | bytes 147460
  412.8 87.5 %reduce-scatter.34.cloned.1.call-start = ((), (), s32[]{:S(2)}) async-start(), calls=%async_computation.19 | async-start | bytes 921600 | tf_op jit(solution)/shard_map/reduce_scatter | solution.py:504
  417.8 108.0 %reduce-scatter.40.cloned.1.call-start = ((), (), s32[]{:S(2)}) async-start(), calls=%async_computation.22 | async-start | bytes 921600 | tf_op jit(solution)/shard_map/reduce_scatter | solution.py:513
  419.1 138.8 %reduce-scatter.42.cloned.1.call-start = ((), (), s32[]{:S(2)}) async-start(), calls=%async_computation.23 | async-start | bytes 2211840 | tf_op jit(solution)/shard_map/reduce_scatter | solution.py:516
  421.0 168.9 %reduce-scatter.44.cloned.1.call-start = ((), (), s32[]{:S(2)}) async-start(), calls=%async_computation.24 | async-start | bytes 2211840 | tf_op jit(solution)/shard_map/reduce_scatter | solution.py:519
  423.0 189.9 %reduce-scatter.36.cloned.1.call-start = ((), (), s32[]{:S(2)}) async-start(), calls=%async_computation.20 | async-start | bytes 368640 | tf_op jit(solution)/shard_map/reduce_scatter | solution.py:507
  477.8 157.7 %reduce-scatter.38.cloned.1.call-start = ((), (), s32[]{:S(2)}) async-start(), calls=%async_computation.21 | async-start | bytes 368640 | tf_op jit(solution)/shard_map/reduce_scatter | solution.py:510
  478.9 190.0 %reduce-scatter.58.cloned.1.call-start = ((), (), s32[]{:S(2)}) async-start(), calls=%async_computation.31 | async-start | bytes 2457600
  481.9 252.3 %reduce-scatter.46.cloned.1.call-start = ((), (), s32[]{:S(2)}) async-start(), calls=%async_computation.25 | async-start | bytes 663552
  502.3 296.7 %reduce-scatter.52.cloned.1.call-start = ((), (), s32[]{:S(2)}) async-start(), calls=%async_computation.28 | async-start | bytes 663552
  527.6 338.8 %reduce-scatter.54.cloned.1.call-start = ((), (), s32[]{:S(2)}) async-start(), calls=%async_computation.29 | async-start | bytes 1769472
  560.4 373.5 %reduce-scatter.56.cloned.1.call-start = ((), (), s32[]{:S(2)}) async-start(), calls=%async_computation.30 | async-start | bytes 1769472
  592.4 405.3 %reduce-scatter.48.cloned.1.call-start = ((), (), s32[]{:S(2)}) async-start(), calls=%async_computation.26 | async-start | bytes 221184
  614.6 447.0 %reduce-scatter.50.cloned.1.call-start = ((), (), s32[]{:S(2)}) async-start(), calls=%async_computation.27 | async-start | bytes 221184
  637.2 488.4 %reduce-scatter.60.cloned.1.call-start = ((), (), s32[]{:S(2)}) async-start(), calls=%async_computation.32 | async-start | bytes 995328
  672.5 128.1 %copy-start.27 = (bf16[576,192]{1,0:T(8,128)(2,1)S(1)}, bf16[576,192]{1,0:T(8,128)(2,1)}, u32[]{:S(2)}) copy-start(bf16[576,192]{1,0:T(8,128)(2,1)} %copy-done.26) | copy-start | bytes 663556
  675.3 125.5 %copy-start.39 = (bf16[576,192]{1,0:T(8,128)(2,1)S(1)}, bf16[576,192]{1,0:T(8,128)(2,1)}, u32[]{:S(2)}) copy-start(bf16[576,192]{1,0:T(8,128)(2,1)} %copy-done.38) | copy-start | bytes 663556
  675.3 125.9 %copy-start.77 = (bf16[576]{0:T(1024)(128)(2,1)S(1)}, bf16[576]{0:T(1024)(128)(2,1)}, u32[]{:S(2)}) copy-start(bf16[576]{0:T(1024)(128)(2,1)} %get-tuple-element.534) | copy-start | bytes 3460
  (98 other events, 1252.0 us)
Sparse Core Ops, SparseCore 0:
  42.4 21.7 all-gather.5
  75.4 22.0 all-gather.7
  108.6 22.1 all-gather.9
  413.0 62.7 reduce-scatter.31
  478.3 21.9 reduce-scatter.33
  502.7 22.9 reduce-scatter.39
  528.5 29.3 reduce-scatter.41
  560.5 29.3 reduce-scatter.43
  592.5 20.2 reduce-scatter.35
  615.2 20.2 reduce-scatter.37
  638.3 30.6 reduce-scatter.57
  672.1 62.1 reduce-scatter.45
  737.8 61.0 reduce-scatter.51
  802.3 64.1 reduce-scatter.53
  870.1 63.7 reduce-scatter.55
  937.6 60.0 reduce-scatter.47
  1001.4 60.1 reduce-scatter.49
  1065.4 60.2 reduce-scatter.59
where the time goes:
time: 1140 us; the launch traced here: 1130 us
  waiting for transfers between devices  636 us (56%)
  blocking collectives  331 us (29%)
  local copies, waits for them, and re-layouts  77.7 us (7%)
  matrix products  43.6 us (4%)
  other arithmetic  23.6 us (2%)
  between operations  18.7 us (2%)
    unnamed x26, waiting for transfers between devices  441 us
    unnamed x3, blocking collectives  52.4 us
    reduce_scatter x1, waiting for transfers between devices, on_device(): lax.psum_scatter(grad_whole, 'ctx', scatter_dimension=0, tiled=True)  52.3 us
    all_gather x1, blocking collectives, on_device(): lax.all_gather(w_gate, 'ctx', axis=1, tiled=True)  33.6 us
    all_gather x1, blocking collectives, on_device(): lax.all_gather(w_down, 'ctx', axis=1, tiled=True)  33.1 us
    unnamed x169, local copies, waits for them, and re-layouts  32.9 us
    all_gather x1, blocking collectives, on_device(): lax.all_gather(w_up, 'ctx', axis=1, tiled=True)  31.5 us
    all_gather x1, blocking collectives, on_device(): lax.all_gather(w_out, 'ctx', axis=1, tiled=True)  30.9 us
  transfers between devices with their start and end apart: 18, of which 15 were waited for; matrix products, arithmetic and copies ran while one was open for 7% of the time, Pallas kernels for 0%

commit v1 on v0

v1 whole, which is shorter than its diff:
```python
import functools
import math

import jax
import jax.numpy as jnp
from jax import lax
from jax.experimental import pallas as pl
from jax.experimental.pallas import tpu as pltpu
from jax.sharding import PartitionSpec as P

QUERY_HEADS = 9
KEY_VALUE_HEADS = 3
HEAD_DIM = 64
GROUP = QUERY_HEADS // KEY_VALUE_HEADS

THETA = 100000.0
EPS = 1e-05
MASKED = -1e30
SCALE = 1.0 / math.sqrt(HEAD_DIM)
F32 = jnp.float32
BF16 = jnp.bfloat16
VMEM_BYTES = 56 * 1024 * 1024

K_TILE, K_HALF = (0, 0, 1), (0, 1, 0)
V_TILE, V_HALF = (1, 2, 2), (1, 0, 1)


def round_up(n, m):
    return -(-n // m) * m


def swap(x, axis, mask):
    size = lax.axis_size(axis)
    return lax.ppermute(x, axis, [(i, i ^ mask) for i in range(size)])


def add_low(a, b):
    return (a.astype(F32) + b.astype(F32)).astype(BF16)


def outer_digits(shards):
    bits = list(range(1, shards.bit_length() - 1))
    return [tuple(bits[i : i + 2]) for i in range(0, len(bits), 2)]


def masks_of(digit):
    return [sum(1 << b for k, b in enumerate(digit) if n >> k & 1) for n in range(1 << len(digit))]


def gather_outer(x, shards):
    for digit in outer_digits(shards):
        x = jnp.concatenate([x] + [swap(x, "ctx", m) for m in masks_of(digit)[1:]], 0)
    return x


def scatter_outer(x, shards):
    digits = outer_digits(shards)[::-1]
    for at, digit in enumerate(digits):
        masks = masks_of(digit)
        parts = x.reshape((len(masks), -1) + x.shape[1:])
        total = parts[0].astype(F32)
        for n, m in enumerate(masks[1:]):
            total = total + swap(parts[n + 1], "ctx", m).astype(F32)
        x = total if at == len(digits) - 1 else total.astype(BF16)
    return x


def both(x, axis, mask):
    return jnp.concatenate([x, swap(x, axis, mask)], 0)


def gather_tree(x, rows, shards):
    z = gather_outer(x[None], shards)
    a, b = z[:, :rows], z[:, rows:]
    a, b = both(a, "ctx", 1), both(b, "fsdp", 2)
    a, b = both(a, "fsdp", 2), both(b, "ctx", 1)
    return both(a, "fsdp", 1), both(b, "fsdp", 1)


def scatter_tree(g, rows, shards):
    s = add_low(g[: 2 * shards], swap(g[2 * shards :], "fsdp", 1))
    a, b = s[:, :rows], s[:, rows:]
    a = add_low(a[:shards], swap(a[shards:], "fsdp", 2))
    b = b.reshape((2, 2, shards // 2) + b.shape[1:])
    b = add_low(b[:, 0], swap(b[:, 1], "ctx", 1))
    a = add_low(a[: shards // 2], swap(a[shards // 2 :], "ctx", 1))
    b = add_low(b[0], swap(b[1], "fsdp", 2))
    return scatter_outer(jnp.concatenate([a, b], 1), shards)[0]


def ctx_place(mask, shards):
    return (mask >> 1) + (shards // 2) * (mask & 1)


def place_yx(cm, fm, shards):
    return ctx_place(cm, shards) + shards * (fm >> 1) + 2 * shards * (fm & 1)


def place_xy(cm, fm, shards):
    half = shards // 2
    return (cm >> 1) + half * (fm >> 1) + shards * (cm & 1) + 2 * shards * (fm & 1)


def dot(a, b):
    return lax.dot_general(a, b, (((1,), (0,)), ((), ())), preferred_element_type=F32)


def dot_nt(a, b):
    return lax.dot_general(a, b, (((1,), (1,)), ((), ())), preferred_element_type=F32)


def dot_tn(a, b):
    return lax.dot_general(a, b, (((0,), (0,)), ((), ())), preferred_element_type=F32)


def lane_ids():
    return lax.broadcasted_iota(jnp.int32, (1, 128), 1)


def turned(u):
    lane = lane_ids()
    first = (lane & (HEAD_DIM - 1)) < HEAD_DIM // 2
    return jnp.where(first, pltpu.roll(u, 96, 1), pltpu.roll(u, 32, 1))


def to_half(tile, source, target):
    return tile if source == target else pltpu.roll(tile, 64, 1)


def only_half(tile, half):
    lane = lane_ids()
    keep = lane >= 64 if half else lane < 64
    return jnp.where(keep, tile, 0.0)


def head_rows(h):
    return slice(h * 128, (h + 1) * 128)


def qkv_kernel(dims, meta, x_ref, a1_ref, a2_ref, cos_ref, sin_ref, qp_ref, kv_ref, an_ref, gain_ref, q_s, kv_s):
    shards, fsdp, cq, ck, split, feat = dims
    mc, mf = meta[shards], meta[shards + 1]
    kvw = KEY_VALUE_HEADS * HEAD_DIM
    for c in range(shards):
        tail = a2_ref[place_xy(c ^ mc, mf ^ mf, shards)]
        row = tail[feat - split :, :].astype(F32)
        gain_ref[:, c * cq : (c + 1) * cq] = row[:, :cq]
        gain_ref[:, 640 + c * cq : 640 + (c + 1) * cq] = row[:, 128 : 128 + cq]
    x = x_ref[...].astype(F32)
    width = x.shape[1]
    rr = lax.rsqrt(jnp.mean(x * x, axis=-1, keepdims=True) + EPS)
    normed = (x * rr * gain_ref[0:1, :width]).astype(BF16)
    for c in range(shards):
        pieces = []
        for f in range(fsdp):
            pieces.append(a1_ref[place_yx(c ^ mc, f ^ mf, shards)])
            pieces.append(a2_ref[place_xy(c ^ mc, f ^ mf, shards)][: feat - split])
        w = jnp.concatenate(pieces, 0)
        an_ref[c] = w
        y = dot(normed, w[:, :128])
        q_s[:, c * cq : (c + 1) * cq] = y[:, :cq]
        kv_s[:, c * ck : (c + 1) * ck] = y[:, cq : cq + ck]
        kv_s[:, kvw + c * ck : kvw + (c + 1) * ck] = y[:, cq + ck : cq + 2 * ck]
    cos, sin = cos_ref[...], sin_ref[...]
    for t in range(5):
        u = q_s[:, t * 128 : (t + 1) * 128]
        u = u * cos + turned(u) * sin
        for h in (2 * t, 2 * t + 1):
            if h < QUERY_HEADS:
                half = K_HALF[h // GROUP]
                qp_ref[head_rows(h), :] = only_half(to_half(u, h % 2, half), half).astype(BF16)
    for t in range(3):
        u = kv_s[:, t * 128 : (t + 1) * 128]
        if t < 2:
            r = u * cos + turned(u) * sin
            u = r if t == 0 else jnp.where(lane_ids() < 64, r, u)
        kv_ref[:, t * 128 : (t + 1) * 128] = u.astype(BF16)


def score_mask(meta, shards, block, chunks, blk):
    mc = meta[shards]
    mine = meta[mc]
    r = lax.broadcasted_iota(jnp.int32, (blk, GROUP * 2 * blk), 1) & (2 * blk - 1)
    qpos = jnp.where(r < blk, mine * blk + r, (2 * shards - 1 - mine) * blk + r - blk)
    gap = qpos - lax.broadcasted_iota(jnp.int32, qpos.shape, 0)
    out = []
    half = shards // 2
    for i in range(chunks):
        place = block * chunks + i
        mask = 2 * lax.rem(place, half) + lax.div(place, half)
        pair = meta[mc ^ mask]
        out.append(gap >= pair * blk)
        out.append(gap >= (2 * shards - 1 - pair) * blk)
    return out


def masked(s, mask, blk):
    return jnp.concatenate(
        [jnp.where(m, s[i * blk : (i + 1) * blk], MASKED) for i, m in enumerate(mask)], 0
    )


def attend_kernel(dims, meta, qp_ref, kv_ref, att_ref, ot_ref, lse_ref, m_s, l_s):
    shards, chunks, blk = dims
    blocks = shards // chunks
    rows = chunks * 2 * blk
    span = GROUP * 2 * blk

    def block_step(b, first):
        mask = score_mask(meta, shards, b, chunks, blk)
        kv = kv_ref[pl.ds(b * chunks, chunks)].reshape(rows, -1)
        for g in range(KEY_VALUE_HEADS):
            keys = kv[:, K_TILE[g] * 128 : (K_TILE[g] + 1) * 128]
            vals = kv[:, V_TILE[g] * 128 : (V_TILE[g] + 1) * 128]
            s = masked(dot_nt(keys, qp_ref[g * span : (g + 1) * span, :]) * SCALE, mask, blk)
            top = jnp.max(s, axis=0, keepdims=True)
            if not first:
                top = jnp.maximum(top, m_s[g : g + 1, :])
            p = jnp.exp(s - top)
            total = jnp.sum(p, axis=0, keepdims=True)
            out = dot_tn(vals, p.astype(BF16))
            if not first:
                fade = jnp.exp(m_s[g : g + 1, :] - top)
                total = total + l_s[g : g + 1, :] * fade
                out = out + ot_ref[g] * fade
            m_s[g : g + 1, :] = top
            l_s[g : g + 1, :] = total
            ot_ref[g] = out

    block_step(0, True)
    if blocks > 1:

        @pl.loop(1, blocks)
        def _(b):
            block_step(b, False)

    tiles = {}
    for g in range(KEY_VALUE_HEADS):
        o = ot_ref[g] / l_s[g : g + 1, :]
        ot_ref[g] = o
        lse_ref[g : g + 1, :] = m_s[g : g + 1, :] + jnp.log(l_s[g : g + 1, :])
        for j in range(GROUP):
            h = g * GROUP + j
            tile = jnp.transpose(o[:, j * 128 : (j + 1) * 128])
            tiles[h] = to_half(tile, V_HALF[g], h % 2)
    for t in range(5):
        if 2 * t + 1 < QUERY_HEADS:
            tile = jnp.where(lane_ids() < 64, tiles[2 * t], tiles[2 * t + 1])
            att_ref[:, t * 128 : (t + 1) * 128] = tile.astype(BF16)
        else:
            att_ref[:, t * 128 : t * 128 + 64] = tiles[2 * t][:, :64].astype(BF16)


def ffn_kernel(
    dims, meta, att_ref, x_ref, dy_ref, wo_ref, gain_ref, gu_ref, dt_ref,
    out_ref, gout_ref, dmid_ref, ggain_ref, gp_ref, gu_s, hid_s, dh_s, dgu_s, ga_s,
):
    shards, fsdp, cq, cg, feat, ffr = dims
    mc, mf = meta[shards], meta[shards + 1]
    att = att_ref[...]
    x = x_ref[...].astype(F32)
    width = x.shape[1]
    dyl = dy_ref[...]
    gain = gain_ref[0:1, :width]
    mid = x + dot(att, wo_ref[...])
    rr = lax.rsqrt(jnp.mean(mid * mid, axis=-1, keepdims=True) + EPS)
    z = mid * rr
    normed = (z * gain).astype(BF16)

    def weights(c):
        return jnp.concatenate([gu_ref[c * fsdp + f, :feat, :] for f in range(fsdp)], 0)

    for c in range(shards):
        gu = dot(normed, weights(c))
        gu_s[c] = gu
        gate, up = gu[:, :cg], gu[:, cg : 2 * cg]
        hid_s[:, c * cg : (c + 1) * cg] = gate * jax.nn.sigmoid(gate) * up
    out = mid
    for f in range(fsdp):
        hid = hid_s[:, f * ffr : (f + 1) * ffr].astype(BF16)
        out = out + dot_nt(hid, dt_ref[f])
        dh_s[:, f * ffr : (f + 1) * ffr] = dot(dyl, dt_ref[f])
        g = dot_tn(dyl, hid)
        for c in range(shards):
            piece = g[c * cq : (c + 1) * cq, :].astype(BF16)
            gout_ref[place_yx(c ^ mc, f ^ mf, shards), feat : feat + cq, :] = piece
    out_ref[...] = out.astype(BF16)
    dn = jnp.zeros_like(mid)
    for c in range(shards):
        gu = gu_s[c]
        gate, up = gu[:, :cg], gu[:, cg : 2 * cg]
        dh = dh_s[:, c * cg : (c + 1) * cg]
        sg = jax.nn.sigmoid(gate)
        if 2 * cg < dgu_s.shape[1]:
            dgu_s[...] = jnp.zeros_like(dgu_s)
        dgu_s[:, :cg] = dh * up * sg * (1.0 + gate * (1.0 - sg))
        dgu_s[:, cg : 2 * cg] = dh * gate * sg
        dgu = dgu_s[...].astype(BF16)
        g = dot_tn(normed, dgu)
        for f in range(fsdp):
            piece = g[f * feat : (f + 1) * feat, :].astype(BF16)
            gout_ref[place_yx(c ^ mc, f ^ mf, shards), :feat, : dgu.shape[1]] = piece
        dn = dn + dot_nt(dgu, weights(c))
    e = dn * gain
    dmid = dyl.astype(F32) + rr * (e - z * jnp.mean(e * z, axis=-1, keepdims=True))
    dmid_ref[...] = dmid
    ggain_ref[...] = jnp.broadcast_to(jnp.sum(dn * z, axis=0, keepdims=True), ggain_ref.shape)
    ga_s[:, :width] = dot_nt(dmid.astype(BF16), wo_ref[...])
    for h in range(QUERY_HEADS):
        half = V_HALF[h // GROUP]
        tile = ga_s[:, (h // 2) * 128 : (h // 2 + 1) * 128]
        gp_ref[head_rows(h), :] = only_half(to_half(tile, h % 2, half), half).astype(BF16)


def attend_back_kernel(
    dims, meta, qp_ref, gp_ref, kv_ref, ot_ref, lse_ref, cos_ref, sin_ref, dq_ref, dkv_ref, dq_s
):
    shards, chunks, blk = dims
    blocks = shards // chunks
    rows = chunks * 2 * blk
    span = GROUP * 2 * blk
    deltas = []
    for g in range(KEY_VALUE_HEADS):
        gt = jnp.transpose(gp_ref[g * span : (g + 1) * span, :].astype(F32))
        deltas.append(jnp.sum(gt * ot_ref[g], axis=0, keepdims=True))

    def block_step(b, first):
        mask = score_mask(meta, shards, b, chunks, blk)
        kv = kv_ref[pl.ds(b * chunks, chunks)].reshape(rows, -1)
        tiles = [None, None, None]

        def put(t, value):
            tiles[t] = value if tiles[t] is None else tiles[t] + value

        for g in range(KEY_VALUE_HEADS):
            keys = kv[:, K_TILE[g] * 128 : (K_TILE[g] + 1) * 128]
            vals = kv[:, V_TILE[g] * 128 : (V_TILE[g] + 1) * 128]
            qg = qp_ref[g * span : (g + 1) * span, :]
            gg = gp_ref[g * span : (g + 1) * span, :]
            s = masked(dot_nt(keys, qg) * SCALE, mask, blk)
            p = jnp.exp(s - lse_ref[g : g + 1, :])
            ds = (p * (dot_nt(vals, gg) - deltas[g]) * SCALE).astype(BF16)
            put(V_TILE[g], dot(p.astype(BF16), gg))
            put(K_TILE[g], dot(ds, qg))
            dq = dot_tn(ds, keys)
            if first:
                dq_s[g * span : (g + 1) * span, :] = dq
            else:
                dq_s[g * span : (g + 1) * span, :] += dq
        for t in range(3):
            dkv_ref[pl.ds(b * chunks, chunks), :, t * 128 : (t + 1) * 128] = (
                tiles[t].astype(BF16).reshape(chunks, 2 * blk, 128)
            )

    block_step(0, True)
    if blocks > 1:

        @pl.loop(1, blocks)
        def _(b):
            block_step(b, False)

    cos, sin = cos_ref[...], sin_ref[...]
    tiles = {}
    for h in range(QUERY_HEADS):
        u = dq_s[head_rows(h), :]
        tiles[h] = to_half(u * cos - turned(u) * sin, K_HALF[h // GROUP], h % 2)
    for t in range(5):
        if 2 * t + 1 < QUERY_HEADS:
            tile = jnp.where(lane_ids() < 64, tiles[2 * t], tiles[2 * t + 1])
            dq_ref[:, t * 128 : (t + 1) * 128] = tile.astype(BF16)
        else:
            dq_ref[:, t * 128 : t * 128 + 64] = tiles[2 * t][:, :64].astype(BF16)


def qkv_back_kernel(
    dims, meta, x_ref, dq_ref, dkv_ref, att_ref, dmid_ref, wq_ref, wkv_ref, gain_ref, gg_ref,
    cos_ref, sin_ref, gin_ref, gout_ref, dq_s, dkv_s, gb_s, d_s, gg_s,
):
    shards, fsdp, cq, ck, feat = dims
    mc, mf = meta[shards], meta[shards + 1]
    kvw = KEY_VALUE_HEADS * HEAD_DIM
    x = x_ref[...].astype(F32)
    width = x.shape[1]
    gain = gain_ref[0:1, :width]
    rr = lax.rsqrt(jnp.mean(x * x, axis=-1, keepdims=True) + EPS)
    z = x * rr
    normed = (z * gain).astype(BF16)
    cos, sin = cos_ref[...], sin_ref[...]
    for t in range(3):
        u = dkv_ref[:, t * 128 : (t + 1) * 128]
        if t < 2:
            r = u * cos - turned(u) * sin
            u = r if t == 0 else jnp.where(lane_ids() < 64, r, u)
        dkv_s[:, t * 128 : (t + 1) * 128] = u
    dq_s[...] = dq_ref[...].astype(F32)
    dmid = dmid_ref[...]
    gb_s[...] = dmid
    dn = dot_nt(dq_ref[...], wq_ref[...]) + dot_nt(dkv_s[...].astype(BF16), wkv_ref[...])
    e = dn * gain
    gin_ref[...] = dmid + rr * (e - z * jnp.mean(e * z, axis=-1, keepdims=True))
    gg_s[...] = jnp.broadcast_to(jnp.sum(dn * z, axis=0, keepdims=True), gg_s.shape)
    att = att_ref[...]
    d_s[...] = jnp.zeros_like(d_s)
    for c in range(shards):
        d_s[:, :cq] = dq_s[:, c * cq : (c + 1) * cq]
        d_s[:, cq : cq + ck] = dkv_s[:, c * ck : (c + 1) * ck]
        d_s[:, cq + ck : cq + 2 * ck] = dkv_s[:, kvw + c * ck : kvw + (c + 1) * ck]
        d_s[:, 128 : 128 + cq] = gb_s[:, c * cq : (c + 1) * cq]
        g = jnp.concatenate(
            [dot_tn(normed, d_s[:, :128].astype(BF16)), dot_tn(att, d_s[:, 128:].astype(BF16))], 1
        )
        d_s[0:8, 0:cq] = gg_s[:, c * cq : (c + 1) * cq]
        d_s[0:8, 128 : 128 + cq] = gg_ref[:, c * cq : (c + 1) * cq]
        gains = d_s[0:8, :].astype(BF16)
        for f in range(fsdp):
            at = place_yx(c ^ mc, f ^ mf, shards)
            gout_ref[at, :feat, :] = g[f * feat : (f + 1) * feat, :].astype(BF16)
            gout_ref[at, feat : feat + 8, :] = gains


def call(kernel, outs, scratch, flops, moved, *args):
    smem = pl.BlockSpec(memory_space=pltpu.SMEM)
    vmem = pl.BlockSpec(memory_space=pltpu.VMEM)
    return pl.pallas_call(
        kernel,
        out_shape=outs,
        in_specs=[smem] + [vmem] * (len(args) - 1),
        out_specs=[vmem] * len(outs),
        scratch_shapes=scratch,
        cost_estimate=pl.CostEstimate(flops=flops, bytes_accessed=moved, transcendentals=0),
        compiler_params=pltpu.CompilerParams(vmem_limit_bytes=VMEM_BYTES),
    )(*args)


def arr(shape, dtype):
    return jax.ShapeDtypeStruct(shape, dtype)


def on_device(
    tokens, pair_of, gain_attn, w_query, key_weight, value_weight, w_out, gain_ffn,
    w_gate, w_up, w_down, cotangent,
):
    rows, width = tokens.shape[1:]
    blk = rows // 2
    shards, fsdp = lax.axis_size("ctx"), lax.axis_size("fsdp")
    feat, cq = w_query.shape
    ck, cg, ffr = key_weight.shape[1], w_gate.shape[1], w_down.shape[0]
    ff = cg * shards
    x, dy = tokens[0], cotangent[0]
    meta = jnp.concatenate(
        [pair_of[0], jnp.stack([lax.axis_index("ctx"), lax.axis_index("fsdp")]).astype(jnp.int32)]
    )

    def fill(parts, total):
        used = sum(p.shape[1] for p in parts)
        return parts + [jnp.zeros((parts[0].shape[0], total - used), BF16)]

    lanes = 256
    body = jnp.concatenate(
        fill([w_query, key_weight, value_weight], 128) + fill([w_out], 128), 1
    )
    gains_row = jnp.concatenate(fill([gain_attn[None]], 128) + fill([gain_ffn[None]], 128), 1)
    own = jnp.concatenate([body, jnp.broadcast_to(gains_row, (8, lanes))], 0)
    split = 80

    cgl = round_up(2 * cg, 128)
    gu_own = jnp.concatenate(fill([w_gate, w_up], cgl), 1)
    dt_own = w_down.T
    if cgl == ffr:
        ffn_all = lax.all_gather(jnp.concatenate([gu_own, dt_own], 0), ("ctx", "fsdp"), axis=0)
        gu_all, dt_all = ffn_all, ffn_all[:, feat:]
    else:
        gu_all = lax.all_gather(gu_own, ("ctx", "fsdp"), axis=0)
        dt_all = lax.all_gather(dt_own, ("ctx", "fsdp"), axis=0)
    dt_all = dt_all.reshape(shards, fsdp, cq, ffr).transpose(1, 0, 2, 3).reshape(fsdp, width, ffr)

    a1, a2 = gather_tree(own, split, shards)

    my_pair = pair_of[0, lax.axis_index("ctx")]
    offsets = jnp.arange(blk, dtype=jnp.int32)
    pos = jnp.concatenate([my_pair * blk + offsets, (2 * shards - 1 - my_pair) * blk + offsets])
    freq = THETA ** (-jnp.arange(HEAD_DIM // 2, dtype=F32) * 2.0 / HEAD_DIM)
    angles = pos.astype(F32)[:, None] * freq[None, :]
    cos, sin = jnp.cos(angles), jnp.sin(angles)
    cos_t = jnp.concatenate([cos] * 4, 1)
    sin_t = jnp.concatenate([-sin, sin] * 2, 1)

    kvl = 2 * KEY_VALUE_HEADS * HEAD_DIM
    hrows = QUERY_HEADS * rows
    qp, kv, a_nat, gains = call(
        functools.partial(qkv_kernel, (shards, fsdp, cq, ck, split, feat)),
        [
            arr((hrows, 128), BF16), arr((rows, kvl), BF16),
            arr((shards, width, lanes), BF16), arr((8, 1280), F32),
        ],
        [pltpu.VMEM((rows, 640), F32), pltpu.VMEM((rows, kvl), F32)],
        2 * rows * width * 128 * shards, 6_000_000,
        meta, x, a1, a2, cos_t, sin_t,
    )
    gain_first, gain_second = gains[:, :640], gains[:, 640:]

    def natural(lo, n):
        return a_nat[:, :, lo : lo + n].transpose(1, 0, 2).reshape(width, n * shards)

    wq_n = natural(0, cq)
    wkv_n = jnp.concatenate([natural(cq, ck), natural(cq + ck, ck)], 1)
    wo_n = natural(128, cq)

    kv_all = both(gather_outer(kv[None], shards), "ctx", 1)
    chunks = min(8, shards)
    span = GROUP * rows
    att, ot, lse = call(
        functools.partial(attend_kernel, (shards, chunks, blk)),
        [arr((rows, width), BF16), arr((KEY_VALUE_HEADS, 128, span), F32), arr((8, span), F32)],
        [pltpu.VMEM((8, span), F32), pltpu.VMEM((8, span), F32)],
        4 * hrows * shards * rows * 128, 3_000_000,
        meta, qp, kv_all,
    )

    grows = feat + cq
    glanes = max(cgl, ffr)
    out, g_ffn, dmid, ggain, gp = call(
        functools.partial(ffn_kernel, (shards, fsdp, cq, cg, feat, ffr)),
        [
            arr((rows, width), BF16), arr((fsdp * shards, grows, glanes), BF16),
            arr((rows, width), F32), arr((8, width), F32), arr((hrows, 128), BF16),
        ],
        [
            pltpu.VMEM((shards, rows, cgl), F32), pltpu.VMEM((rows, ff), F32),
            pltpu.VMEM((rows, ff), F32), pltpu.VMEM((rows, cgl), F32), pltpu.VMEM((rows, 640), F32),
        ],
        18 * rows * width * ff, 14_000_000,
        meta, att, x, dy, wo_n, gain_second, gu_all, dt_all,
    )
    ffn_own = scatter_tree(g_ffn, 112, shards)

    dq, dkv = call(
        functools.partial(attend_back_kernel, (shards, chunks, blk)),
        [arr((rows, width), BF16), arr((shards, rows, kvl), BF16)],
        [pltpu.VMEM((hrows, 128), F32)],
        10 * hrows * shards * rows * 128, 5_000_000,
        meta, qp, gp, kv_all, ot, lse, cos_t, sin_t,
    )
    half = shards // 2
    dkv = scatter_outer(add_low(dkv[:half], swap(dkv[half:], "ctx", 1)), shards)[0]

    grad_input, g_attn = call(
        functools.partial(qkv_back_kernel, (shards, fsdp, cq, ck, feat)),
        [arr((rows, width), F32), arr((fsdp * shards, feat + 8, lanes), BF16)],
        [
            pltpu.VMEM((rows, width), F32), pltpu.VMEM((rows, kvl), F32),
            pltpu.VMEM((rows, width), F32), pltpu.VMEM((rows, lanes), F32),
            pltpu.VMEM((8, width), F32),
        ],
        6 * rows * width * 256 * shards, 6_000_000,
        meta, x, dq, dkv, att, dmid, wq_n, wkv_n, gain_first, ggain, cos_t, sin_t,
    )
    attn_own = scatter_tree(g_attn, split, shards)
    return (
        out[None],
        grad_input[None],
        attn_own[feat, :cq],
        attn_own[:feat, :cq],
        attn_own[:feat, cq : cq + ck],
        attn_own[:feat, cq + ck : cq + 2 * ck],
        attn_own[:feat, 128 : 128 + cq],
        attn_own[feat, 128 : 128 + cq],
        ffn_own[:feat, :cg],
        ffn_own[:feat, cg : 2 * cg],
        ffn_own[feat:, :ffr].T,
    )


def solution(mesh):
    weights = (P("fsdp", "ctx"),) * 4
    data = P("fsdp", "ctx", None)
    in_specs = (
        (data, P("fsdp", None), P("ctx")) + weights + (P("ctx"),) + weights[:3] + (data,)
    )
    out_specs = (data, data, P("ctx")) + weights + (P("ctx"),) + weights[:3]
    return jax.shard_map(
        on_device, mesh=mesh, in_specs=in_specs, out_specs=out_specs, check_vma=False
    )
```

time: 1140 us -> 224 us (0.20)
  waiting for transfers between devices: 636 us -> 87 us
  blocking collectives: 331 us -> 0 us
  matrix products: 43.6 us -> 0 us
  local copies, waits for them, and re-layouts: 77.7 us -> 34.5 us
  starting transfers between devices: 1 us -> 38.2 us
  Pallas kernels: 0 us -> 30.3 us
    unnamed x26 -> x1, waiting for transfers between devices: 441 us -> 0.02 us
    all_gather x12 -> x0, blocking collectives: 279 us -> none  [the longest x1 33.6 us: on_device(): lax.all_gather(w_gate, 'ctx', axis=1, tiled=True)]
    reduce_scatter x7 -> x0, waiting for transfers between devices: 195 us -> none  [the longest x1 52.3 us: on_device(): lax.psum_scatter(grad_whole, 'ctx', scatter_dimension=0, tiled=True)]
    ppermute x0 -> x33, waiting for transfers between devices: none -> 83.5 us  [swap(): return lax.ppermute(x, axis, [(i, i ^ mask) for i in range(size)])]
    unnamed x3 -> x0, blocking collectives: 52.4 us -> none
    dot_general x51 -> x0, matrix products: 43.6 us -> none  [the longest x1 3.53 us: on_device(): jnp.einsum('rd,fd->rf', grad_out_low, wd_full, preferred_element_type=jnp...]
    ppermute x0 -> x33, starting transfers between devices: none -> 38.2 us  [swap(): return lax.ppermute(x, axis, [(i, i ^ mask) for i in range(size)])]
    pallas_call x0 -> x5, Pallas kernels: none -> 30.3 us  [call(): pl.pallas_call(kernel, out_shape=outs, in_specs=[smem] + [vmem] * (len(ar...]
  transfers between devices with their start and end apart: 18 -> 34, of which waited for: 15 -> 26; matrix products, arithmetic and copies ran while one was open for 7% -> 16% of each run, Pallas kernels for 0% -> 4%
where the time goes in v1:
time: 224 us; the launch traced here: 223 us
  waiting for transfers between devices  87 us (39%)
  starting transfers between devices  38.2 us (17%)
  local copies, waits for them, and re-layouts  34.5 us (15%)
  Pallas kernels  30.3 us (14%)
  other arithmetic  17.6 us (8%)
  between operations  15.9 us (7%)
    ppermute x33, waiting for transfers between devices, swap(): return lax.ppermute(x, axis, [(i, i ^ mask) for i in range(size)])  83.5 us
    ppermute x33, starting transfers between devices, swap(): return lax.ppermute(x, axis, [(i, i ^ mask) for i in range(size)])  38.2 us
    pallas_call x5, Pallas kernels, call(): pl.pallas_call(kernel, out_shape=outs, in_specs=[smem] + [vmem] * (len(ar...  30.3 us
    transpose x6, local copies, waits for them, and re-layouts, natural(): return a_nat[:, :, lo:lo + n].transpose(1, 0, 2).reshape(width, n * shards)  9.7 us
    unnamed x52, local copies, waits for them, and re-layouts  9.02 us
    convert_element_type x11, other arithmetic, add_low(): return (a.astype(F32) + b.astype(F32)).astype(BF16)  5.18 us
  transfers between devices with their start and end apart: 34, of which 26 were waited for; matrix products, arithmetic and copies ran while one was open for 16% of the time, Pallas kernels for 4%

profile of v1, /device:TPU:0, one launch (start us, length us, event | category | flops | bytes accessed | tf_op | source)
XLA Modules:
  0.0 223.5 jit_solution(14570696601571980588)
XLA Ops:
  12.4 5.1 %collective-permute-start.2 = (bf16[1,152,256]{2,1,0:T(8,128)(2,1)S(1)}, bf16[1,152,256]{2,1,0:T(8,128)(2,1)S(1)}, u32[]{:S(2)}, u32[]{:S(2)}) collective-permute-start(bf16[1,152,256]{2,1,0:T(8,128)(2,1)S(1)} %maximum_bitcast_fusion), channel_id=1, source_target_pairs={{0,24},{4,28},{8,16},{12,20},{16,8},{20,12},{24,0},{28,4},{1,25},{... | collective-permute-start | bytes 233480 | tf_op jit(solution)/shard_map/ppermute | solution.py:34
  20.7 3.3 %collective-permute-done.1 = bf16[1,152,256]{2,1,0:T(8,128)(2,1)S(1)} collective-permute-done((bf16[1,152,256]{2,1,0:T(8,128)(2,1)S(1)}, bf16[1,152,256]{2,1,0:T(8,128)(2,1)S(1)}, u32[]{:S(2)}, u32[]{:S(2)}) %collective-permute-start.1) | collective-permute-done | bytes 77856 | tf_op jit(solution)/shard_map/ppermute | solution.py:34
  32.8 4.7 %collective-permute-done.7 = bf16[8,72,256]{2,1,0:T(8,128)(2,1)S(1)} collective-permute-done((bf16[8,72,256]{2,1,0:T(8,128)(2,1)S(1)}, bf16[8,72,256]{2,1,0:T(8,128)(2,1)S(1)}, u32[]{:S(2)}, u32[]{:S(2)}) %collective-permute-start.7) | collective-permute-done | bytes 294944 | tf_op jit(solution)/shard_map/ppermute | solution.py:34
  44.2 4.6 %shard_map.203 = (bf16[1152,128]{1,0:T(8,128)(2,1)}, bf16[128,384]{1,0:T(8,128)(2,1)}, bf16[8,576,256]{2,1,0:T(8,128)(2,1)}, f32[8,1280]{1,0:T(8,128)}) custom-call(s32[10]{0:T(128)} %pad_add_fusion.meta, bf16[128,576]{1,0:T(8,128)(2,1)} %bitcast.99, bf16[32,80,256]{2,1,0:T(8,128)(2,1)} %pad_maximum_fusion.a1_ref, ...), custom_call_target="tpu_custom_call" | custom-call | flops 150994944 | bytes 6000000 | tf_op jit(solution)/shard_map/pallas_call | solution.py:424
  48.8 3.1 %collective-permute-start.11 = (bf16[1,128,384]{2,1,0:T(8,128)(2,1)}, bf16[1,128,384]{2,1,0:T(8,128)(2,1)S(1)}, u32[]{:S(2)}, u32[]{:S(2)}) collective-permute-start(bf16[1,128,384]{2,1,0:T(8,128)(2,1)} %bitcast.105), channel_id=1, source_target_pairs={{0,24},{4,28},{8,16},{12,20},{16,8},{20,12},{24,0},{28,4},{1,25},{... | collective-permute-start | bytes 294920 | tf_op jit(solution)/shard_map/ppermute | solution.py:34
  53.2 2.9 %slice_bitcast_fusion.2 = (bf16[576,8,72]{2,0,1:T(8,128)(2,1)}, bf16[576,8,72]{2,0,1:T(8,128)(2,1)S(1)}) fusion(bf16[8,576,256]{2,1,0:T(8,128)(2,1)} %get-tuple-element.30), kind=kLoop, calls=%fused_computation.9 | loop fusion | bytes 2654208 | tf_op jit(solution)/shard_map/transpose | solution.py:503
  56.7 4.9 %collective-permute-done.10 = bf16[1,128,384]{2,1,0:T(8,128)(2,1)S(1)} collective-permute-done((bf16[1,128,384]{2,1,0:T(8,128)(2,1)}, bf16[1,128,384]{2,1,0:T(8,128)(2,1)S(1)}, u32[]{:S(2)}, u32[]{:S(2)}) %collective-permute-start.10) | collective-permute-done | bytes 98336 | tf_op jit(solution)/shard_map/ppermute | solution.py:34
  65.5 15.4 %collective-permute-done.12 = bf16[4,128,384]{2,1,0:T(8,128)(2,1)S(1)} collective-permute-done((bf16[4,128,384]{2,1,0:T(8,128)(2,1)S(1)}, bf16[4,128,384]{2,1,0:T(8,128)(2,1)S(1)}, u32[]{:S(2)}, u32[]{:S(2)}) %collective-permute-start.12) | collective-permute-done | bytes 393248 | tf_op jit(solution)/shard_map/ppermute | solution.py:34
  81.9 4.3 %shard_map.204 = (bf16[128,576]{1,0:T(8,128)(2,1)}, f32[3,128,384]{2,1,0:T(8,128)}, f32[8,384]{1,0:T(8,128)}) custom-call(s32[10]{0:T(128)} %pad_add_fusion.meta, bf16[1152,128]{1,0:T(8,128)(2,1)} %get-tuple-element.27.qp_ref, bf16[8,128,384]{2,1,0:T(8,128)(2,1)} %copy-done.14), custom_call_target="tpu_custom_call" | custom-call | flops 603979776 | bytes 3000000 | tf_op jit(solution)/shard_map/pallas_call | solution.py:424
  86.2 3.5 %all-gather.3.cloned.1.call-done = bf16[6912,384]{1,0:T(8,128)(2,1)} async-done(((bf16[216,384]{1,0:T(8,128)(2,1)}), bf16[6912,384]{1,0:T(8,128)(2,1)}) %all-gather.3.cloned.1.call-update) | async-done | bytes 5308432 | tf_op jit(solution)/shard_map/all_gather | solution.py:470
  92.8 10.4 %shard_map.205 = (bf16[128,576]{1,0:T(8,128)(2,1)}, bf16[32,216,384]{2,1,0:T(8,128)(2,1)}, f32[128,576]{1,0:T(8,128)}, f32[8,576]{1,0:T(8,128)}, bf16[1152,128]{1,0:T(8,128)(2,1)}) custom-call(s32[10]{0:T(128)} %pad_add_fusion.meta, bf16[128,576]{1,0:T(8,128)(2,1)} %get-tuple-element.29.att_ref, bf16[128,576]{1,0:T(8,128)(2,1)} %bitcast.100, ...), custom_call_target="tpu_custom_call" | custom-call | flops 2038431744 | bytes 14000000 | tf_op jit(solution)/shard_map/pallas_call | solution.py:424
  103.2 6.4 %shard_map.206 = (bf16[128,576]{1,0:T(8,128)(2,1)}, bf16[8,128,384]{2,1,0:T(8,128)(2,1)}) custom-call(s32[10]{0:T(128)} %pad_add_fusion.meta, bf16[1152,128]{1,0:T(8,128)(2,1)} %get-tuple-element.27.qp_ref, bf16[1152,128]{1,0:T(8,128)(2,1)} %get-tuple-element.33.gp_ref, bf16[8,128,384]{2,1,0:T(8,128)(2,1)} %copy-done.14, ...), custom_call_target="tpu_custom_call" | custom-call | flops 1509949440 | bytes 5000000 | tf_op jit(solution)/shard_map/pallas_call | solution.py:424
  120.1 2.9 %collective-permute-done.13 = bf16[4,128,384]{2,1,0:T(8,128)(2,1)} collective-permute-done((bf16[4,128,384]{2,1,0:T(8,128)(2,1)}, bf16[4,128,384]{2,1,0:T(8,128)(2,1)}, u32[]{:S(2)}, u32[]{:S(2)}) %collective-permute-start.13) | collective-permute-done | bytes 393248 | tf_op jit(solution)/shard_map/ppermute | solution.py:34
  124.2 2.4 %collective-permute-start.14 = (bf16[1,128,384]{2,1,0:T(8,128)(2,1)S(1)}, bf16[1,128,384]{2,1,0:T(8,128)(2,1)S(1)}, u32[]{:S(2)}, u32[]{:S(2)}) collective-permute-start(bf16[1,128,384]{2,1,0:T(8,128)(2,1)S(1)} %get-tuple-element.83), channel_id=1, source_target_pairs={{0,8},{4,12},{8,0},{12,4},{16,24},{20,28},{24,16},{28,20},{1,9},{5... | collective-permute-start | bytes 294920 | tf_op jit(solution)/shard_map/ppermute | solution.py:34
  129.6 4.7 %collective-permute-done.16 = bf16[1,128,384]{2,1,0:T(8,128)(2,1)S(1)} collective-permute-done((bf16[1,128,384]{2,1,0:T(8,128)(2,1)S(1)}, bf16[1,128,384]{2,1,0:T(8,128)(2,1)S(1)}, u32[]{:S(2)}, u32[]{:S(2)}) %collective-permute-start.16) | collective-permute-done | bytes 98336 | tf_op jit(solution)/shard_map/ppermute | solution.py:34
  134.4 2.7 %collective-permute-done.15 = bf16[1,128,384]{2,1,0:T(8,128)(2,1)S(1)} collective-permute-done((bf16[1,128,384]{2,1,0:T(8,128)(2,1)S(1)}, bf16[1,128,384]{2,1,0:T(8,128)(2,1)S(1)}, u32[]{:S(2)}, u32[]{:S(2)}) %collective-permute-start.15) | collective-permute-done | bytes 98336 | tf_op jit(solution)/shard_map/ppermute | solution.py:34
  137.7 4.6 %shard_map.207 = (f32[128,576]{1,0:T(8,128)}, bf16[32,152,256]{2,1,0:T(8,128)(2,1)}) custom-call(s32[10]{0:T(128)} %pad_add_fusion.meta, bf16[128,576]{1,0:T(8,128)(2,1)} %bitcast.101, bf16[128,576]{1,0:T(8,128)(2,1)} %get-tuple-element.36.dq_ref, f32[128,384]{1,0:T(8,128)} %add_bitcast_fusion.dkv_ref, bf16[128,576]{1,0:T(8,128)(2,1)} %get-tuple-element.29.att_ref, ...), custom_call_target="tpu_custom_call" | custom-call | flops 905969664 | bytes 6000000 | tf_op jit(solution)/shard_map/pallas_call | solution.py:424
  149.5 7.0 %collective-permute-done.20 = bf16[2,4,72,256]{3,2,1,0:T(8,128)(2,1)S(1)} collective-permute-done((bf16[2,4,72,256]{3,2,1,0:T(8,128)(2,1)S(1)}, bf16[2,4,72,256]{3,2,1,0:T(8,128)(2,1)S(1)}, u32[]{:S(2)}, u32[]{:S(2)}) %collective-permute-start.20) | collective-permute-done | bytes 294944 | tf_op jit(solution)/shard_map/ppermute | solution.py:34
  159.2 2.6 %collective-permute-done.21 = bf16[4,72,256]{2,1,0:T(8,128)(2,1)S(1)} collective-permute-done((bf16[4,72,256]{2,1,0:T(8,128)(2,1)S(1)}, bf16[4,72,256]{2,1,0:T(8,128)(2,1)S(1)}, u32[]{:S(2)}, u32[]{:S(2)}) %collective-permute-start.21) | collective-permute-done | bytes 147488 | tf_op jit(solution)/shard_map/ppermute | solution.py:34
  168.1 2.1 collective-permute-start.24
  184.2 11.0 %collective-permute-done.26 = bf16[8,112,384]{2,1,0:T(8,128)(2,1)S(1)} collective-permute-done((bf16[8,112,384]{2,1,0:T(8,128)(2,1)S(1)}, bf16[8,112,384]{2,1,0:T(8,128)(2,1)S(1)}, u32[]{:S(2)}, u32[]{:S(2)}) %collective-permute-start.26) | collective-permute-done | bytes 688160 | tf_op jit(solution)/shard_map/ppermute | solution.py:34
  199.9 2.9 %collective-permute-done.27 = bf16[4,112,384]{2,1,0:T(8,128)(2,1)S(1)} collective-permute-done((bf16[4,112,384]{2,1,0:T(8,128)(2,1)S(1)}, bf16[4,112,384]{2,1,0:T(8,128)(2,1)S(1)}, u32[]{:S(2)}, u32[]{:S(2)}) %collective-permute-start.27) | collective-permute-done | bytes 344096 | tf_op jit(solution)/shard_map/ppermute | solution.py:34
  208.3 2.3 %collective-permute-done.32 = bf16[1,216,384]{2,1,0:T(8,128)(2,1)S(1)} collective-permute-done((bf16[1,216,384]{2,1,0:T(8,128)(2,1)S(1)}, bf16[1,216,384]{2,1,0:T(8,128)(2,1)S(1)}, u32[]{:S(2)}, u32[]{:S(2)}) %collective-permute-start.32) | collective-permute-done | bytes 165920 | tf_op jit(solution)/shard_map/ppermute | solution.py:34
  210.7 4.5 %collective-permute-done.31 = bf16[1,216,384]{2,1,0:T(8,128)(2,1)S(1)} collective-permute-done((bf16[1,216,384]{2,1,0:T(8,128)(2,1)S(1)}, bf16[1,216,384]{2,1,0:T(8,128)(2,1)S(1)}, u32[]{:S(2)}, u32[]{:S(2)}) %collective-permute-start.31) | collective-permute-done | bytes 165920 | tf_op jit(solution)/shard_map/ppermute | solution.py:34
  (180 shorter events, 89.4 us)
Async XLA Ops:
  7.2 82.5 %all-gather.3.cloned.1.call-start = ((), (), s32[]{:S(2)}) async-start(), calls=%async_computation | async-start | bytes 5474304 | tf_op jit(solution)/shard_map/all_gather | solution.py:470
  12.4 8.3 %collective-permute-start.2 = (bf16[1,152,256]{2,1,0:T(8,128)(2,1)S(1)}, bf16[1,152,256]{2,1,0:T(8,128)(2,1)S(1)}, u32[]{:S(2)}, u32[]{:S(2)}) collective-permute-start(bf16[1,152,256]{2,1,0:T(8,128)(2,1)S(1)} %maximum_bitcast_fusion), channel_id=1, source_target_pairs={{0,24},{4,28},{8,16},{12,20},{16,8},{20,12},{24,0},{28,4},{1,25},{... | collective-permute-start | bytes 233480 | tf_op jit(solution)/shard_map/ppermute | solution.py:34
  17.6 6.5 %collective-permute-start.1 = (bf16[1,152,256]{2,1,0:T(8,128)(2,1)S(1)}, bf16[1,152,256]{2,1,0:T(8,128)(2,1)S(1)}, u32[]{:S(2)}, u32[]{:S(2)}) collective-permute-start(bf16[1,152,256]{2,1,0:T(8,128)(2,1)S(1)} %maximum_bitcast_fusion), channel_id=1, source_target_pairs={{0,16},{4,20},{8,24},{12,28},{16,0},{20,4},{24,8},{28,12},{1,17},{... | collective-permute-start | bytes 233480 | tf_op jit(solution)/shard_map/ppermute | solution.py:34
  17.6 6.5 %collective-permute-start = (bf16[1,152,256]{2,1,0:T(8,128)(2,1)S(1)}, bf16[1,152,256]{2,1,0:T(8,128)(2,1)S(1)}, u32[]{:S(2)}, u32[]{:S(2)}) collective-permute-start(bf16[1,152,256]{2,1,0:T(8,128)(2,1)S(1)} %maximum_bitcast_fusion), channel_id=1, source_target_pairs={{0,8},{4,12},{8,0},{12,4},{16,24},{20,28},{24,16},{28,20},{1,9},{5... | collective-permute-start | bytes 233480 | tf_op jit(solution)/shard_map/ppermute | solution.py:34
  29.3 8.2 %collective-permute-start.7 = (bf16[8,72,256]{2,1,0:T(8,128)(2,1)S(1)}, bf16[8,72,256]{2,1,0:T(8,128)(2,1)S(1)}, u32[]{:S(2)}, u32[]{:S(2)}) collective-permute-start(bf16[8,72,256]{2,1,0:T(8,128)(2,1)S(1)} %pad_maximum_fusion.8), channel_id=1, source_target_pairs={{0,4},{4,0},{8,12},{12,8},{16,20},{20,16},{24,28},{28,24},{1,5},{5... | collective-permute-start | bytes 884744 | tf_op jit(solution)/shard_map/ppermute | solution.py:34
  31.7 7.5 %collective-permute-start.4 = (bf16[8,80,256]{2,1,0:T(8,128)(2,1)S(1)}, bf16[8,80,256]{2,1,0:T(8,128)(2,1)S(1)}, u32[]{:S(2)}, u32[]{:S(2)}) collective-permute-start(bf16[8,80,256]{2,1,0:T(8,128)(2,1)S(1)} %pad_maximum_fusion.6), channel_id=1, source_target_pairs={{0,2},{1,3},{2,0},{3,1},{4,6},{5,7},{6,4},{7,5},{8,10},{9,11},{10,... | collective-permute-start | bytes 983048 | tf_op jit(solution)/shard_map/ppermute | solution.py:34
  48.8 7.9 %collective-permute-start.11 = (bf16[1,128,384]{2,1,0:T(8,128)(2,1)}, bf16[1,128,384]{2,1,0:T(8,128)(2,1)S(1)}, u32[]{:S(2)}, u32[]{:S(2)}) collective-permute-start(bf16[1,128,384]{2,1,0:T(8,128)(2,1)} %bitcast.105), channel_id=1, source_target_pairs={{0,24},{4,28},{8,16},{12,20},{16,8},{20,12},{24,0},{28,4},{1,25},{... | collective-permute-start | bytes 294920 | tf_op jit(solution)/shard_map/ppermute | solution.py:34
  51.8 9.8 %collective-permute-start.10 = (bf16[1,128,384]{2,1,0:T(8,128)(2,1)}, bf16[1,128,384]{2,1,0:T(8,128)(2,1)S(1)}, u32[]{:S(2)}, u32[]{:S(2)}) collective-permute-start(bf16[1,128,384]{2,1,0:T(8,128)(2,1)} %bitcast.106), channel_id=1, source_target_pairs={{0,16},{4,20},{8,24},{12,28},{16,0},{20,4},{24,8},{28,12},{1,17},{... | collective-permute-start | bytes 294920 | tf_op jit(solution)/shard_map/ppermute | solution.py:34
  51.8 9.8 %collective-permute-start.9 = (bf16[1,128,384]{2,1,0:T(8,128)(2,1)}, bf16[1,128,384]{2,1,0:T(8,128)(2,1)S(1)}, u32[]{:S(2)}, u32[]{:S(2)}) collective-permute-start(bf16[1,128,384]{2,1,0:T(8,128)(2,1)} %bitcast.107), channel_id=1, source_target_pairs={{0,8},{4,12},{8,0},{12,4},{16,24},{20,28},{24,16},{28,20},{1,9},{5... | collective-permute-start | bytes 294920 | tf_op jit(solution)/shard_map/ppermute | solution.py:34
  61.6 19.3 %collective-permute-start.12 = (bf16[4,128,384]{2,1,0:T(8,128)(2,1)S(1)}, bf16[4,128,384]{2,1,0:T(8,128)(2,1)S(1)}, u32[]{:S(2)}, u32[]{:S(2)}) collective-permute-start(bf16[4,128,384]{2,1,0:T(8,128)(2,1)S(1)} %pad_maximum_fusion.5), channel_id=1, source_target_pairs={{0,4},{4,0},{8,12},{12,8},{16,20},{20,16},{24,28},{28,24},{1,5},{5... | collective-permute-start | bytes 1179656 | tf_op jit(solution)/shard_map/ppermute | solution.py:34
  111.4 11.6 %collective-permute-start.13 = (bf16[4,128,384]{2,1,0:T(8,128)(2,1)}, bf16[4,128,384]{2,1,0:T(8,128)(2,1)}, u32[]{:S(2)}, u32[]{:S(2)}) collective-permute-start(bf16[4,128,384]{2,1,0:T(8,128)(2,1)} %slice.189), channel_id=1, source_target_pairs={{0,4},{4,0},{8,12},{12,8},{16,20},{20,16},{24,28},{28,24},{1,5},{5... | collective-permute-start | bytes 1179656 | tf_op jit(solution)/shard_map/ppermute | solution.py:34
  126.6 7.8 %collective-permute-start.16 = (bf16[1,128,384]{2,1,0:T(8,128)(2,1)S(1)}, bf16[1,128,384]{2,1,0:T(8,128)(2,1)S(1)}, u32[]{:S(2)}, u32[]{:S(2)}) collective-permute-start(bf16[1,128,384]{2,1,0:T(8,128)(2,1)S(1)} %get-tuple-element.84), channel_id=1, source_target_pairs={{0,24},{4,28},{8,16},{12,20},{16,8},{20,12},{24,0},{28,4},{1,25},{... | collective-permute-start | bytes 294920 | tf_op jit(solution)/shard_map/ppermute | solution.py:34
  128.7 8.3 %collective-permute-start.15 = (bf16[1,128,384]{2,1,0:T(8,128)(2,1)S(1)}, bf16[1,128,384]{2,1,0:T(8,128)(2,1)S(1)}, u32[]{:S(2)}, u32[]{:S(2)}) collective-permute-start(bf16[1,128,384]{2,1,0:T(8,128)(2,1)S(1)} %get-tuple-element.85), channel_id=1, source_target_pairs={{0,16},{4,20},{8,24},{12,28},{16,0},{20,4},{24,8},{28,12},{1,17},{... | collective-permute-start | bytes 294920 | tf_op jit(solution)/shard_map/ppermute | solution.py:34
  144.3 19.5 %collective-permute-start.25 = (bf16[16,216,384]{2,1,0:T(8,128)(2,1)S(1)}, bf16[16,216,384]{2,1,0:T(8,128)(2,1)S(1)}, u32[]{:S(2)}, u32[]{:S(2)}) collective-permute-start(bf16[16,216,384]{2,1,0:T(8,128)(2,1)S(1)} %slice.220), channel_id=1, source_target_pairs={{0,1},{1,0},{2,3},{3,2},{4,5},{5,4},{6,7},{7,6},{8,9},{9,8},{10,11... | collective-permute-start | bytes 7962632 | tf_op jit(solution)/shard_map/ppermute | solution.py:34
  147.4 9.1 %collective-permute-start.20 = (bf16[2,4,72,256]{3,2,1,0:T(8,128)(2,1)S(1)}, bf16[2,4,72,256]{3,2,1,0:T(8,128)(2,1)S(1)}, u32[]{:S(2)}, u32[]{:S(2)}) collective-permute-start(bf16[2,4,72,256]{3,2,1,0:T(8,128)(2,1)S(1)} %slice_bitcast_fusion.8), channel_id=1, source_target_pairs={{0,4},{4,0},{8,12},{12,8},{16,20},{20,16},{24,28},{28,24},{1,5},{5... | collective-permute-start | bytes 884744 | tf_op jit(solution)/shard_map/ppermute | solution.py:34
  148.8 9.5 %collective-permute-start.18 = (bf16[8,80,256]{2,1,0:T(8,128)(2,1)S(1)}, bf16[8,80,256]{2,1,0:T(8,128)(2,1)S(1)}, u32[]{:S(2)}, u32[]{:S(2)}) collective-permute-start(bf16[8,80,256]{2,1,0:T(8,128)(2,1)S(1)} %slice.245), channel_id=1, source_target_pairs={{0,2},{1,3},{2,0},{3,1},{4,6},{5,7},{6,4},{7,5},{8,10},{9,11},{10,... | collective-permute-start | bytes 983048 | tf_op jit(solution)/shard_map/ppermute | solution.py:34
  166.7 14.7 %collective-permute-start.28 = (bf16[2,4,104,384]{3,2,1,0:T(8,128)(2,1)}, bf16[2,4,104,384]{3,2,1,0:T(8,128)(2,1)}, u32[]{:S(2)}, u32[]{:S(2)}) collective-permute-start(bf16[2,4,104,384]{3,2,1,0:T(8,128)(2,1)} %slice_bitcast_fusion.4), channel_id=1, source_target_pairs={{0,4},{4,0},{8,12},{12,8},{16,20},{20,16},{24,28},{28,24},{1,5},{5... | collective-permute-start | bytes 1916936 | tf_op jit(solution)/shard_map/ppermute | solution.py:34
  168.1 6.6 %collective-permute-start.24 = (bf16[1,152,256]{2,1,0:T(8,128)(2,1)}, bf16[1,152,256]{2,1,0:T(8,128)(2,1)}, u32[]{:S(2)}, u32[]{:S(2)}) collective-permute-start(bf16[1,152,256]{2,1,0:T(8,128)(2,1)} %get-tuple-element.89), channel_id=1, source_target_pairs={{0,24},{4,28},{8,16},{12,20},{16,8},{20,12},{24,0},{28,4},{1,25},{... | collective-permute-start | bytes 233480 | tf_op jit(solution)/shard_map/ppermute | solution.py:34
  170.2 6.6 %collective-permute-start.23 = (bf16[1,152,256]{2,1,0:T(8,128)(2,1)}, bf16[1,152,256]{2,1,0:T(8,128)(2,1)}, u32[]{:S(2)}, u32[]{:S(2)}) collective-permute-start(bf16[1,152,256]{2,1,0:T(8,128)(2,1)} %get-tuple-element.90), channel_id=1, source_target_pairs={{0,16},{4,20},{8,24},{12,28},{16,0},{20,4},{24,8},{28,12},{1,17},{... | collective-permute-start | bytes 233480 | tf_op jit(solution)/shard_map/ppermute | solution.py:34
  177.9 17.3 %collective-permute-start.26 = (bf16[8,112,384]{2,1,0:T(8,128)(2,1)S(1)}, bf16[8,112,384]{2,1,0:T(8,128)(2,1)S(1)}, u32[]{:S(2)}, u32[]{:S(2)}) collective-permute-start(bf16[8,112,384]{2,1,0:T(8,128)(2,1)S(1)} %slice.266), channel_id=1, source_target_pairs={{0,2},{1,3},{2,0},{3,1},{4,6},{5,7},{6,4},{7,5},{8,10},{9,11},{10,... | collective-permute-start | bytes 2064392 | tf_op jit(solution)/shard_map/ppermute | solution.py:34
  183.5 15.2 %collective-permute-start.29 = (bf16[4,104,384]{2,1,0:T(8,128)(2,1)}, bf16[4,104,384]{2,1,0:T(8,128)(2,1)}, u32[]{:S(2)}, u32[]{:S(2)}) collective-permute-start(bf16[4,104,384]{2,1,0:T(8,128)(2,1)} %slice_bitcast_fusion.6), channel_id=1, source_target_pairs={{0,2},{1,3},{2,0},{3,1},{4,6},{5,7},{6,4},{7,5},{8,10},{9,11},{10,... | collective-permute-start | bytes 958472 | tf_op jit(solution)/shard_map/ppermute | solution.py:34
  195.5 7.3 %collective-permute-start.27 = (bf16[4,112,384]{2,1,0:T(8,128)(2,1)S(1)}, bf16[4,112,384]{2,1,0:T(8,128)(2,1)S(1)}, u32[]{:S(2)}, u32[]{:S(2)}) collective-permute-start(bf16[4,112,384]{2,1,0:T(8,128)(2,1)S(1)} %slice.268), channel_id=1, source_target_pairs={{0,4},{4,0},{8,12},{12,8},{16,20},{20,16},{24,28},{28,24},{1,5},{5... | collective-permute-start | bytes 1032200 | tf_op jit(solution)/shard_map/ppermute | solution.py:34
  203.4 7.2 %collective-permute-start.32 = (bf16[1,216,384]{2,1,0:T(8,128)(2,1)S(1)}, bf16[1,216,384]{2,1,0:T(8,128)(2,1)S(1)}, u32[]{:S(2)}, u32[]{:S(2)}) collective-permute-start(bf16[1,216,384]{2,1,0:T(8,128)(2,1)S(1)} %get-tuple-element.81), channel_id=1, source_target_pairs={{0,24},{4,28},{8,16},{12,20},{16,8},{20,12},{24,0},{28,4},{1,25},{... | collective-permute-start | bytes 497672 | tf_op jit(solution)/shard_map/ppermute | solution.py:34
  205.3 9.9 %collective-permute-start.31 = (bf16[1,216,384]{2,1,0:T(8,128)(2,1)S(1)}, bf16[1,216,384]{2,1,0:T(8,128)(2,1)S(1)}, u32[]{:S(2)}, u32[]{:S(2)}) collective-permute-start(bf16[1,216,384]{2,1,0:T(8,128)(2,1)S(1)} %get-tuple-element.82), channel_id=1, source_target_pairs={{0,16},{4,20},{8,24},{12,28},{16,0},{20,4},{24,8},{28,12},{1,17},{... | collective-permute-start | bytes 497672 | tf_op jit(solution)/shard_map/ppermute | solution.py:34
  (30 other events, 249.9 us)
Sparse Core Ops, SparseCore 0:
  10.9 78.7 all-gather.2

commit v2 on v1

--- a/solution.py
+++ b/solution.py
@@ -47,58 +47,115 @@
     return [sum(1 << b for k, b in enumerate(digit) if n >> k & 1) for n in range(1 << len(digit))]
 
 
+def join(pieces, *before):
+    held = lax.optimization_barrier((*pieces, *before))[: len(pieces)]
+    return jnp.concatenate(held, 0)
+
+
 def gather_outer(x, shards):
+    pieces = [x]
     for digit in outer_digits(shards):
-        x = jnp.concatenate([x] + [swap(x, "ctx", m) for m in masks_of(digit)[1:]], 0)
-    return x
+        x = jnp.concatenate(pieces, 0)
+        pieces = [x] + [swap(x, "ctx", m) for m in masks_of(digit)[1:]]
+    return pieces
 
 
 def scatter_outer(x, shards):
-    digits = outer_digits(shards)[::-1]
-    for at, digit in enumerate(digits):
+    for digit in outer_digits(shards)[::-1]:
         masks = masks_of(digit)
         parts = x.reshape((len(masks), -1) + x.shape[1:])
-        total = parts[0].astype(F32)
-        for n, m in enumerate(masks[1:]):
-            total = total + swap(parts[n + 1], "ctx", m).astype(F32)
-        x = total if at == len(digits) - 1 else total.astype(BF16)
-    return x
-
-
-def both(x, axis, mask):
-    return jnp.concatenate([x, swap(x, axis, mask)], 0)
-
-
-def gather_tree(x, rows, shards):
-    z = gather_outer(x[None], shards)
-    a, b = z[:, :rows], z[:, rows:]
-    a, b = both(a, "ctx", 1), both(b, "fsdp", 2)
-    a, b = both(a, "fsdp", 2), both(b, "ctx", 1)
-    return both(a, "fsdp", 1), both(b, "fsdp", 1)
-
-
-def scatter_tree(g, rows, shards):
-    s = add_low(g[: 2 * shards], swap(g[2 * shards :], "fsdp", 1))
-    a, b = s[:, :rows], s[:, rows:]
-    a = add_low(a[:shards], swap(a[shards:], "fsdp", 2))
-    b = b.reshape((2, 2, shards // 2) + b.shape[1:])
-    b = add_low(b[:, 0], swap(b[:, 1], "ctx", 1))
-    a = add_low(a[: shards // 2], swap(a[shards // 2 :], "ctx", 1))
-    b = add_low(b[0], swap(b[1], "fsdp", 2))
-    return scatter_outer(jnp.concatenate([a, b], 1), shards)[0]
+        terms = [parts[0]] + [swap(parts[n + 1], "ctx", m) for n, m in enumerate(masks[1:])]
+        x = add_terms(terms).astype(BF16)
+    return terms
+
+
+def add_terms(terms, *before):
+    held = lax.optimization_barrier((*terms, *before))[: len(terms)]
+    return functools.reduce(lambda a, b: a + b, [t.astype(F32) for t in held])
+
+
+def after(x, *before):
+    return lax.optimization_barrier((x, *before))[0]
+
+
+class Gather:
+    def __init__(self, block, rows, shards):
+        self.block, self.rows, self.shards = block, rows, shards
+
+    def outer(self, *before):
+        pieces = gather_outer(after(self.block[None], *before), self.shards)
+        self.a = [p[:, : self.rows] for p in pieces]
+        self.b = [p[:, self.rows :] for p in pieces]
+
+    def phase(self, axis_a, mask_a, axis_b, mask_b, *before):
+        a, b = join(self.a, *before), join(self.b, *before)
+        self.now = a, b
+        self.a, self.b = [a, swap(a, axis_a, mask_a)], [b, swap(b, axis_b, mask_b)]
+
+    def second(self, *before):
+        self.phase("ctx", 1, "fsdp", 2, *before)
+
+    def third(self, *before):
+        self.phase("fsdp", 2, "ctx", 1, *before)
+
+    def cores(self, *before):
+        self.phase("fsdp", 1, "fsdp", 1, *before)
+        return *self.a, *self.b
+
+
+class Scatter:
+    def __init__(self, keep_a, send_a, keep_b, send_b, shards, *before):
+        self.a, self.b, self.shards = keep_a, keep_b, shards
+        send_a, send_b = after(send_a, *before), after(send_b, *before)
+        self.got_a, self.got_b = swap(send_a, "fsdp", 1), swap(send_b, "fsdp", 1)
+
+    def fold(self, size, *before):
+        a, b, got_a, got_b = lax.optimization_barrier(
+            (self.a, self.b, self.got_a, self.got_b, *before)
+        )[:4]
+        self.a, self.b = add_low(a[:size], got_a[:size]), add_low(b[:size], got_b[:size])
+        self.out = add_low(a[size:], got_a[size:]), add_low(b[size:], got_b[size:])
+        return self.out
+
+    def second(self, *before):
+        a, b = self.fold(self.shards, *before)
+        self.got_a, self.got_b = swap(a, "fsdp", 2), swap(b, "ctx", 1)
+
+    def third(self, *before):
+        a, b = self.fold(self.shards // 2, *before)
+        self.got_a, self.got_b = swap(a, "ctx", 1), swap(b, "fsdp", 2)
+
+    def outer(self, *before):
+        a, b, got_a, got_b = lax.optimization_barrier(
+            (self.a, self.b, self.got_a, self.got_b, *before)
+        )[:4]
+        self.terms = scatter_outer(
+            jnp.concatenate([add_low(a, got_a), add_low(b, got_b)], 1), self.shards
+        )
+
+    def total(self, *before):
+        return add_terms(self.terms, *before)[0]
 
 
 def ctx_place(mask, shards):
     return (mask >> 1) + (shards // 2) * (mask & 1)
 
 
-def place_yx(cm, fm, shards):
-    return ctx_place(cm, shards) + shards * (fm >> 1) + 2 * shards * (fm & 1)
-
-
-def place_xy(cm, fm, shards):
-    half = shards // 2
-    return (cm >> 1) + half * (fm >> 1) + shards * (cm & 1) + 2 * shards * (fm & 1)
+def place_a(cm, x_bit, shards):
+    return ctx_place(cm, shards) + shards * x_bit
+
+
+def place_b(cm, x_bit, shards):
+    return (cm >> 1) + (shards // 2) * x_bit + shards * (cm & 1)
+
+
+def arrange(out_ref, value, mine, feat):
+    for k in range(value.shape[1] // feat):
+
+        @pl.when(mine == k)
+        def _():
+            for m in range(value.shape[1] // feat):
+                out_ref[:, m * feat : (m + 1) * feat] = value[:, (m ^ k) * feat : ((m ^ k) + 1) * feat]
 
 
 def dot(a, b):
@@ -137,27 +194,29 @@
     return slice(h * 128, (h + 1) * 128)
 
 
-def qkv_kernel(dims, meta, x_ref, a1_ref, a2_ref, cos_ref, sin_ref, qp_ref, kv_ref, an_ref, gain_ref, q_s, kv_s):
+def qkv_kernel(
+    dims, meta, x_ref, ao_ref, as_ref, bo_ref, bs_ref, cos_ref, sin_ref,
+    qp_ref, kv_ref, an_ref, gain_ref, q_s, kv_s, n_s,
+):
     shards, fsdp, cq, ck, split, feat = dims
     mc, mf = meta[shards], meta[shards + 1]
     kvw = KEY_VALUE_HEADS * HEAD_DIM
     for c in range(shards):
-        tail = a2_ref[place_xy(c ^ mc, mf ^ mf, shards)]
-        row = tail[feat - split :, :].astype(F32)
+        row = bo_ref[place_b(c ^ mc, 0, shards)][feat - split :, :].astype(F32)
         gain_ref[:, c * cq : (c + 1) * cq] = row[:, :cq]
         gain_ref[:, 640 + c * cq : 640 + (c + 1) * cq] = row[:, 128 : 128 + cq]
     x = x_ref[...].astype(F32)
     width = x.shape[1]
     rr = lax.rsqrt(jnp.mean(x * x, axis=-1, keepdims=True) + EPS)
-    normed = (x * rr * gain_ref[0:1, :width]).astype(BF16)
+    arrange(n_s, x * rr * gain_ref[0:1, :width], mf, feat)
+    normed = n_s[...].astype(BF16)
     for c in range(shards):
-        pieces = []
-        for f in range(fsdp):
-            pieces.append(a1_ref[place_yx(c ^ mc, f ^ mf, shards)])
-            pieces.append(a2_ref[place_xy(c ^ mc, f ^ mf, shards)][: feat - split])
-        w = jnp.concatenate(pieces, 0)
-        an_ref[c] = w
-        y = dot(normed, w[:, :128])
+        for m in range(fsdp):
+            a_ref, b_ref = ((ao_ref, bo_ref), (as_ref, bs_ref))[m & 1]
+            cut = m * feat + split
+            an_ref[c, m * feat : cut, :] = a_ref[place_a(c ^ mc, m >> 1, shards)]
+            an_ref[c, cut : (m + 1) * feat, :] = b_ref[place_b(c ^ mc, m >> 1, shards)][: feat - split]
+        y = dot(normed, an_ref[c, :, :128])
         q_s[:, c * cq : (c + 1) * cq] = y[:, :cq]
         kv_s[:, c * ck : (c + 1) * ck] = y[:, cq : cq + ck]
         kv_s[:, kvw + c * ck : kvw + (c + 1) * ck] = y[:, cq + ck : cq + 2 * ck]
@@ -184,23 +243,27 @@
     qpos = jnp.where(r < blk, mine * blk + r, (2 * shards - 1 - mine) * blk + r - blk)
     gap = qpos - lax.broadcasted_iota(jnp.int32, qpos.shape, 0)
     out = []
-    half = shards // 2
     for i in range(chunks):
-        place = block * chunks + i
-        mask = 2 * lax.rem(place, half) + lax.div(place, half)
-        pair = meta[mc ^ mask]
+        pair = meta[mc ^ (2 * (block * (chunks // 2) + i % (chunks // 2)) + i // (chunks // 2))]
         out.append(gap >= pair * blk)
         out.append(gap >= (2 * shards - 1 - pair) * blk)
     return out
 
 
+def block_rows(near_ref, far_ref, block, chunks):
+    here = pl.ds(block * (chunks // 2), chunks // 2)
+    return jnp.concatenate(
+        [r[here].reshape(-1, r.shape[2]) for r in (near_ref, far_ref)], 0
+    )
+
+
 def masked(s, mask, blk):
     return jnp.concatenate(
         [jnp.where(m, s[i * blk : (i + 1) * blk], MASKED) for i, m in enumerate(mask)], 0
     )
 
 
-def attend_kernel(dims, meta, qp_ref, kv_ref, att_ref, ot_ref, lse_ref, m_s, l_s):
+def attend_kernel(dims, meta, qp_ref, near_ref, far_ref, att_ref, ot_ref, lse_ref, m_s, l_s):
     shards, chunks, blk = dims
     blocks = shards // chunks
     rows = chunks * 2 * blk
@@ -208,7 +271,7 @@
 
     def block_step(b, first):
         mask = score_mask(meta, shards, b, chunks, blk)
-        kv = kv_ref[pl.ds(b * chunks, chunks)].reshape(rows, -1)
+        kv = block_rows(near_ref, far_ref, b, chunks)
         for g in range(KEY_VALUE_HEADS):
             keys = kv[:, K_TILE[g] * 128 : (K_TILE[g] + 1) * 128]
             vals = kv[:, V_TILE[g] * 128 : (V_TILE[g] + 1) * 128]
@@ -252,23 +315,61 @@
 
 
 def ffn_kernel(
-    dims, meta, att_ref, x_ref, dy_ref, wo_ref, gain_ref, gu_ref, dt_ref,
-    out_ref, gout_ref, dmid_ref, ggain_ref, gp_ref, gu_s, hid_s, dh_s, dgu_s, ga_s,
+    dims, meta, att_ref, x_ref, dy_ref, an_ref, gain_ref, *refs
 ):
-    shards, fsdp, cq, cg, feat, ffr = dims
+    shards, fsdp, cq, cg, feat, ffr, split, packed = dims
+    ins = refs[:4] if packed else refs[:2]
+    (
+        out_ref, ak_ref, as_ref, bk_ref, bs_ref, dmid_ref, ggain_ref, gp_ref,
+        gu_s, hid_s, dh_s, dgu_s, wide_s, p_s, w_s, dt_s,
+    ) = refs[len(ins) :]
     mc, mf = meta[shards], meta[shards + 1]
-    att = att_ref[...]
+    lanes = ak_ref.shape[2]
+    if packed:
+        for c in range(0, shards, 2):
+            for m in range(fsdp):
+                tails = []
+                for d in (c, c + 1):
+                    a_ref, b_ref = ins[m & 1], ins[2 + (m & 1)]
+                    w_s[d, m * feat : m * feat + split, :] = a_ref[place_a(d ^ mc, m >> 1, shards)]
+                    tail = b_ref[place_b(d ^ mc, m >> 1, shards)]
+                    w_s[d, m * feat + split : (m + 1) * feat, :] = tail[: feat - split]
+                    tails.append(tail[feat - split :].astype(F32))
+                dt_s[m, c * cq : (c + 2) * cq, :] = jnp.concatenate(tails, 0).astype(BF16)
+    else:
+        for m in range(fsdp):
+            dt_s[m] = ins[1][mf ^ m]
+
+    def weights(c):
+        if packed:
+            return w_s[c]
+        return jnp.concatenate([ins[0][c, mf ^ m] for m in range(fsdp)], 0)
+
     x = x_ref[...].astype(F32)
     width = x.shape[1]
     dyl = dy_ref[...]
     gain = gain_ref[0:1, :width]
-    mid = x + dot(att, wo_ref[...])
+    arrange(p_s, att_ref[...].astype(F32), mf, feat)
+    attp = p_s[...].astype(BF16)
+    for c in range(shards):
+        wide_s[:, c * cq : (c + 1) * cq] = dot(attp, an_ref[c, :, -128:])[:, :cq]
+    mid = x + wide_s[:, :width]
     rr = lax.rsqrt(jnp.mean(mid * mid, axis=-1, keepdims=True) + EPS)
     z = mid * rr
-    normed = (z * gain).astype(BF16)
-
-    def weights(c):
-        return jnp.concatenate([gu_ref[c * fsdp + f, :feat, :] for f in range(fsdp)], 0)
+    arrange(p_s, z * gain, mf, feat)
+    normed = p_s[...].astype(BF16)
+
+    def store_grad(c, m, row, value):
+        end = row + value.shape[0]
+        here = slice(0, value.shape[1])
+        if row < split:
+            stop = min(end, split)
+            ref = (ak_ref, as_ref)[m & 1]
+            ref[place_a(c ^ mc, m >> 1, shards), row:stop, here] = value[: stop - row]
+        if end > split:
+            start = max(row, split)
+            ref = (bk_ref, bs_ref)[m & 1]
+            ref[place_b(c ^ mc, m >> 1, shards), start - split : end - split, here] = value[start - row :]
 
     for c in range(shards):
         gu = dot(normed, weights(c))
@@ -276,14 +377,16 @@
         gate, up = gu[:, :cg], gu[:, cg : 2 * cg]
         hid_s[:, c * cg : (c + 1) * cg] = gate * jax.nn.sigmoid(gate) * up
     out = mid
-    for f in range(fsdp):
-        hid = hid_s[:, f * ffr : (f + 1) * ffr].astype(BF16)
-        out = out + dot_nt(hid, dt_ref[f])
-        dh_s[:, f * ffr : (f + 1) * ffr] = dot(dyl, dt_ref[f])
+    for m in range(fsdp):
+        here = pl.ds(pl.multiple_of((mf ^ m) * ffr, 128), ffr)
+        hid = hid_s[:, here].astype(BF16)
+        out = out + dot_nt(hid, dt_s[m])
+        dh_s[:, here] = dot(dyl, dt_s[m])
         g = dot_tn(dyl, hid)
         for c in range(shards):
             piece = g[c * cq : (c + 1) * cq, :].astype(BF16)
-            gout_ref[place_yx(c ^ mc, f ^ mf, shards), feat : feat + cq, :] = piece
+            for t in range(ffr // lanes):
+                store_grad(c, m, feat + t * cq, piece[:, t * lanes : (t + 1) * lanes])
     out_ref[...] = out.astype(BF16)
     dn = jnp.zeros_like(mid)
     for c in range(shards):
@@ -297,23 +400,32 @@
         dgu_s[:, cg : 2 * cg] = dh * gate * sg
         dgu = dgu_s[...].astype(BF16)
         g = dot_tn(normed, dgu)
-        for f in range(fsdp):
-            piece = g[f * feat : (f + 1) * feat, :].astype(BF16)
-            gout_ref[place_yx(c ^ mc, f ^ mf, shards), :feat, : dgu.shape[1]] = piece
+        for m in range(fsdp):
+            store_grad(c, m, 0, g[m * feat : (m + 1) * feat, :].astype(BF16))
         dn = dn + dot_nt(dgu, weights(c))
+    arrange(p_s, dn, mf, feat)
+    dn = p_s[...]
     e = dn * gain
     dmid = dyl.astype(F32) + rr * (e - z * jnp.mean(e * z, axis=-1, keepdims=True))
     dmid_ref[...] = dmid
     ggain_ref[...] = jnp.broadcast_to(jnp.sum(dn * z, axis=0, keepdims=True), ggain_ref.shape)
-    ga_s[:, :width] = dot_nt(dmid.astype(BF16), wo_ref[...])
+    wide_s[...] = jnp.zeros_like(wide_s)
+    wide_s[:, :width] = dmid
+    ga = jnp.zeros_like(mid)
+    for c in range(shards):
+        gb = wide_s[:, c * cq : c * cq + 128].astype(BF16)
+        ga = ga + dot_nt(gb, an_ref[c, :, -128:])
+    arrange(p_s, ga, mf, feat)
+    wide_s[:, :width] = p_s[...]
     for h in range(QUERY_HEADS):
         half = V_HALF[h // GROUP]
-        tile = ga_s[:, (h // 2) * 128 : (h // 2 + 1) * 128]
+        tile = wide_s[:, (h // 2) * 128 : (h // 2 + 1) * 128]
         gp_ref[head_rows(h), :] = only_half(to_half(tile, h % 2, half), half).astype(BF16)
 
 
 def attend_back_kernel(
-    dims, meta, qp_ref, gp_ref, kv_ref, ot_ref, lse_ref, cos_ref, sin_ref, dq_ref, dkv_ref, dq_s
+    dims, meta, qp_ref, gp_ref, near_ref, far_ref, ot_ref, lse_ref, cos_ref, sin_ref,
+    dq_ref, dnear_ref, dfar_ref, dq_s,
 ):
     shards, chunks, blk = dims
     blocks = shards // chunks
@@ -326,7 +438,7 @@
 
     def block_step(b, first):
         mask = score_mask(meta, shards, b, chunks, blk)
-        kv = kv_ref[pl.ds(b * chunks, chunks)].reshape(rows, -1)
+        kv = block_rows(near_ref, far_ref, b, chunks)
         tiles = [None, None, None]
 
         def put(t, value):
@@ -348,9 +460,9 @@
             else:
                 dq_s[g * span : (g + 1) * span, :] += dq
         for t in range(3):
-            dkv_ref[pl.ds(b * chunks, chunks), :, t * 128 : (t + 1) * 128] = (
-                tiles[t].astype(BF16).reshape(chunks, 2 * blk, 128)
-            )
+            tile = tiles[t].astype(BF16).reshape(2, chunks // 2, 2 * blk, 128)
+            for n, ref in enumerate((dnear_ref, dfar_ref)):
+                ref[pl.ds(b * (chunks // 2), chunks // 2), :, t * 128 : (t + 1) * 128] = tile[n]
 
     block_step(0, True)
     if blocks > 1:
@@ -373,10 +485,10 @@
 
 
 def qkv_back_kernel(
-    dims, meta, x_ref, dq_ref, dkv_ref, att_ref, dmid_ref, wq_ref, wkv_ref, gain_ref, gg_ref,
-    cos_ref, sin_ref, gin_ref, gout_ref, dq_s, dkv_s, gb_s, d_s, gg_s,
+    dims, meta, x_ref, dq_ref, dkv_ref, att_ref, dmid_ref, an_ref, gain_ref, gg_ref,
+    cos_ref, sin_ref, gin_ref, ak_ref, as_ref, bk_ref, bs_ref, dq_s, dkv_s, d_s, p_s, gg_s,
 ):
-    shards, fsdp, cq, ck, feat = dims
+    shards, fsdp, cq, ck, split, feat = dims
     mc, mf = meta[shards], meta[shards + 1]
     kvw = KEY_VALUE_HEADS * HEAD_DIM
     x = x_ref[...].astype(F32)
@@ -384,7 +496,10 @@
     gain = gain_ref[0:1, :width]
     rr = lax.rsqrt(jnp.mean(x * x, axis=-1, keepdims=True) + EPS)
     z = x * rr
-    normed = (z * gain).astype(BF16)
+    arrange(p_s, z * gain, mf, feat)
+    normed = p_s[...].astype(BF16)
+    arrange(p_s, att_ref[...].astype(F32), mf, feat)
+    att = p_s[...].astype(BF16)
     cos, sin = cos_ref[...], sin_ref[...]
     for t in range(3):
         u = dkv_ref[:, t * 128 : (t + 1) * 128]
@@ -393,29 +508,31 @@
             u = r if t == 0 else jnp.where(lane_ids() < 64, r, u)
         dkv_s[:, t * 128 : (t + 1) * 128] = u
     dq_s[...] = dq_ref[...].astype(F32)
-    dmid = dmid_ref[...]
-    gb_s[...] = dmid
-    dn = dot_nt(dq_ref[...], wq_ref[...]) + dot_nt(dkv_s[...].astype(BF16), wkv_ref[...])
-    e = dn * gain
-    gin_ref[...] = dmid + rr * (e - z * jnp.mean(e * z, axis=-1, keepdims=True))
-    gg_s[...] = jnp.broadcast_to(jnp.sum(dn * z, axis=0, keepdims=True), gg_s.shape)
-    att = att_ref[...]
     d_s[...] = jnp.zeros_like(d_s)
+    dn = jnp.zeros_like(x)
     for c in range(shards):
         d_s[:, :cq] = dq_s[:, c * cq : (c + 1) * cq]
         d_s[:, cq : cq + ck] = dkv_s[:, c * ck : (c + 1) * ck]
         d_s[:, cq + ck : cq + 2 * ck] = dkv_s[:, kvw + c * ck : kvw + (c + 1) * ck]
-        d_s[:, 128 : 128 + cq] = gb_s[:, c * cq : (c + 1) * cq]
-        g = jnp.concatenate(
-            [dot_tn(normed, d_s[:, :128].astype(BF16)), dot_tn(att, d_s[:, 128:].astype(BF16))], 1
-        )
+        d_s[:, 128 : 128 + cq] = dmid_ref[:, c * cq : (c + 1) * cq]
+        d = d_s[...].astype(BF16)
+        dn = dn + dot_nt(d[:, :128], an_ref[c, :, :128])
+        g = jnp.concatenate([dot_tn(normed, d[:, :128]), dot_tn(att, d[:, 128:])], 1).astype(BF16)
+        for m in range(fsdp):
+            part = g[m * feat : (m + 1) * feat, :]
+            (ak_ref, as_ref)[m & 1][place_a(c ^ mc, m >> 1, shards)] = part[:split]
+            (bk_ref, bs_ref)[m & 1][place_b(c ^ mc, m >> 1, shards), : feat - split] = part[split:]
+    arrange(p_s, dn, mf, feat)
+    dn = p_s[...]
+    e = dn * gain
+    gin_ref[...] = dmid_ref[...] + rr * (e - z * jnp.mean(e * z, axis=-1, keepdims=True))
+    gg_s[...] = jnp.broadcast_to(jnp.sum(dn * z, axis=0, keepdims=True), gg_s.shape)
+    for c in range(shards):
         d_s[0:8, 0:cq] = gg_s[:, c * cq : (c + 1) * cq]
         d_s[0:8, 128 : 128 + cq] = gg_ref[:, c * cq : (c + 1) * cq]
         gains = d_s[0:8, :].astype(BF16)
-        for f in range(fsdp):
-            at = place_yx(c ^ mc, f ^ mf, shards)
-            gout_ref[at, :feat, :] = g[f * feat : (f + 1) * feat, :].astype(BF16)
-            gout_ref[at, feat : feat + 8, :] = gains
+        for m in range(fsdp):
+            (bk_ref, bs_ref)[m & 1][place_b(c ^ mc, m >> 1, shards), feat - split :] = gains
 
 
 def call(kernel, outs, scratch, flops, moved, *args):
@@ -466,15 +583,26 @@
     cgl = round_up(2 * cg, 128)
     gu_own = jnp.concatenate(fill([w_gate, w_up], cgl), 1)
     dt_own = w_down.T
-    if cgl == ffr:
-        ffn_all = lax.all_gather(jnp.concatenate([gu_own, dt_own], 0), ("ctx", "fsdp"), axis=0)
-        gu_all, dt_all = ffn_all, ffn_all[:, feat:]
+    packed = cgl == ffr and cq % 8 == 0
+    ffn_split = 112
+    if packed:
+        ffn = Gather(jnp.concatenate([gu_own, dt_own], 0), ffn_split, shards)
     else:
-        gu_all = lax.all_gather(gu_own, ("ctx", "fsdp"), axis=0)
-        dt_all = lax.all_gather(dt_own, ("ctx", "fsdp"), axis=0)
-    dt_all = dt_all.reshape(shards, fsdp, cq, ffr).transpose(1, 0, 2, 3).reshape(fsdp, width, ffr)
-
-    a1, a2 = gather_tree(own, split, shards)
+        gu_all = lax.all_gather(gu_own, ("ctx", "fsdp"), axis=0).reshape(shards, fsdp, feat, cgl)
+        dt_all = lax.all_gather(dt_own, ("ctx", "fsdp"), axis=0).reshape(shards, fsdp, cq, ffr)
+        ffn_in = (gu_all, dt_all.transpose(1, 0, 2, 3).reshape(fsdp, width, ffr))
+
+    attn = Gather(own, split, shards)
+    attn.outer()
+    if packed:
+        ffn.outer(*attn.a, *attn.b)
+    attn.second()
+    attn.third()
+    if packed:
+        attn_in = attn.cores(*ffn.a, *ffn.b)
+        ffn.second()
+    else:
+        attn_in = attn.cores()
 
     my_pair = pair_of[0, lax.axis_index("ctx")]
     offsets = jnp.arange(blk, dtype=jnp.int32)
@@ -493,20 +621,16 @@
             arr((hrows, 128), BF16), arr((rows, kvl), BF16),
             arr((shards, width, lanes), BF16), arr((8, 1280), F32),
         ],
-        [pltpu.VMEM((rows, 640), F32), pltpu.VMEM((rows, kvl), F32)],
+        [pltpu.VMEM((rows, 640), F32), pltpu.VMEM((rows, kvl), F32), pltpu.VMEM((rows, width), F32)],
         2 * rows * width * 128 * shards, 6_000_000,
-        meta, x, a1, a2, cos_t, sin_t,
+        meta, x, *attn_in, cos_t, sin_t,
     )
     gain_first, gain_second = gains[:, :640], gains[:, 640:]
 
-    def natural(lo, n):
-        return a_nat[:, :, lo : lo + n].transpose(1, 0, 2).reshape(width, n * shards)
-
-    wq_n = natural(0, cq)
-    wkv_n = jnp.concatenate([natural(cq, ck), natural(cq + ck, ck)], 1)
-    wo_n = natural(128, cq)
-
-    kv_all = both(gather_outer(kv[None], shards), "ctx", 1)
+    kv_near = join(gather_outer(kv[None], shards))
+    kv_far = swap(kv_near, "ctx", 1)
+    if packed:
+        ffn.third(kv)
     chunks = min(8, shards)
     span = GROUP * rows
     att, ot, lse = call(
@@ -514,48 +638,65 @@
         [arr((rows, width), BF16), arr((KEY_VALUE_HEADS, 128, span), F32), arr((8, span), F32)],
         [pltpu.VMEM((8, span), F32), pltpu.VMEM((8, span), F32)],
         4 * hrows * shards * rows * 128, 3_000_000,
-        meta, qp, kv_all,
-    )
-
-    grows = feat + cq
-    glanes = max(cgl, ffr)
-    out, g_ffn, dmid, ggain, gp = call(
-        functools.partial(ffn_kernel, (shards, fsdp, cq, cg, feat, ffr)),
-        [
-            arr((rows, width), BF16), arr((fsdp * shards, grows, glanes), BF16),
-            arr((rows, width), F32), arr((8, width), F32), arr((hrows, 128), BF16),
-        ],
+        meta, qp, kv_near, kv_far,
+    )
+
+    if packed:
+        ffn_in = ffn.cores(kv_near)
+    glanes = cgl
+    tiles = ffr // glanes
+    parts = [arr((2 * shards, ffn_split, glanes), BF16)] * 2
+    parts += [arr((2 * shards, feat + tiles * cq - ffn_split, glanes), BF16)] * 2
+    out, *g_ffn, dmid, ggain, gp = call(
+        functools.partial(
+            ffn_kernel, (shards, fsdp, cq, cg, feat, ffr, ffn_split, packed)
+        ),
+        [arr((rows, width), BF16), *parts]
+        + [arr((rows, width), F32), arr((8, width), F32), arr((hrows, 128), BF16)],
         [
             pltpu.VMEM((shards, rows, cgl), F32), pltpu.VMEM((rows, ff), F32),
-            pltpu.VMEM((rows, ff), F32), pltpu.VMEM((rows, cgl), F32), pltpu.VMEM((rows, 640), F32),
+            pltpu.VMEM((rows, ff), F32), pltpu.VMEM((rows, cgl), F32), pltpu.VMEM((rows, 768), F32),
+            pltpu.VMEM((rows, width), F32), pltpu.VMEM((shards, width, cgl) if packed else (1, 16, 128), BF16),
+            pltpu.VMEM((fsdp, width, ffr), BF16),
         ],
         18 * rows * width * ff, 14_000_000,
-        meta, att, x, dy, wo_n, gain_second, gu_all, dt_all,
-    )
-    ffn_own = scatter_tree(g_ffn, 112, shards)
-
-    dq, dkv = call(
+        meta, att, x, dy, a_nat if packed else a_nat[:, :, 128:], gain_second, *ffn_in,
+    )
+    ffn_sum = Scatter(*g_ffn, shards)
+    ffn_sum.second()
+
+    dq, dkv_near, dkv_far = call(
         functools.partial(attend_back_kernel, (shards, chunks, blk)),
-        [arr((rows, width), BF16), arr((shards, rows, kvl), BF16)],
+        [arr((rows, width), BF16)] + [arr((shards // 2, rows, kvl), BF16)] * 2,
         [pltpu.VMEM((hrows, 128), F32)],
         10 * hrows * shards * rows * 128, 5_000_000,
-        meta, qp, gp, kv_all, ot, lse, cos_t, sin_t,
-    )
-    half = shards // 2
-    dkv = scatter_outer(add_low(dkv[:half], swap(dkv[half:], "ctx", 1)), shards)[0]
-
-    grad_input, g_attn = call(
-        functools.partial(qkv_back_kernel, (shards, fsdp, cq, ck, feat)),
-        [arr((rows, width), F32), arr((fsdp * shards, feat + 8, lanes), BF16)],
+        meta, qp, gp, kv_near, kv_far, ot, lse, cos_t, sin_t,
+    )
+    dkv_far = after(dkv_far, *ffn_sum.out)
+    dkv_terms = scatter_outer(add_low(dkv_near, swap(dkv_far, "ctx", 1)), shards)
+    ffn_sum.third()
+    dkv = add_terms(dkv_terms, *ffn_sum.out)[0]
+
+    grad_input, *g_attn = call(
+        functools.partial(qkv_back_kernel, (shards, fsdp, cq, ck, split, feat)),
+        [arr((rows, width), F32)]
+        + [arr((2 * shards, split, lanes), BF16)] * 2
+        + [arr((2 * shards, feat + 8 - split, lanes), BF16)] * 2,
         [
             pltpu.VMEM((rows, width), F32), pltpu.VMEM((rows, kvl), F32),
-            pltpu.VMEM((rows, width), F32), pltpu.VMEM((rows, lanes), F32),
+            pltpu.VMEM((rows, lanes), F32), pltpu.VMEM((rows, width), F32),
             pltpu.VMEM((8, width), F32),
         ],
         6 * rows * width * 256 * shards, 6_000_000,
-        meta, x, dq, dkv, att, dmid, wq_n, wkv_n, gain_first, ggain, cos_t, sin_t,
-    )
-    attn_own = scatter_tree(g_attn, split, shards)
+        meta, x, dq, dkv, att, dmid, a_nat, gain_first, ggain, cos_t, sin_t,
+    )
+    attn_sum = Scatter(*g_attn, shards, ffn_sum.got_a, ffn_sum.got_b)
+    ffn_sum.outer()
+    attn_sum.second()
+    attn_sum.third()
+    ffn_own = ffn_sum.total(*attn_sum.out)
+    attn_sum.outer()
+    attn_own = attn_sum.total()
     return (
         out[None],
         grad_input[None],
@@ -567,7 +708,7 @@
         attn_own[feat, 128 : 128 + cq],
         ffn_own[:feat, :cg],
         ffn_own[:feat, cg : 2 * cg],
-        ffn_own[feat:, :ffr].T,
+        jnp.concatenate([ffn_own[feat + t * cq : feat + (t + 1) * cq] for t in range(tiles)], 1).T,
     )
 
 

time: 224 us -> 177 us (0.79)
  waiting for transfers between devices: 87 us -> 66.9 us
  local copies, waits for them, and re-layouts: 34.5 us -> 16.2 us
  between operations: 15.9 us -> 2.78 us
  starting transfers between devices: 38.2 us -> 49.9 us
  other arithmetic: 17.6 us -> 7.39 us
  Pallas kernels: 30.3 us -> 33.7 us
    ppermute x33 -> x44, waiting for transfers between devices: 83.5 us -> 66.9 us  [swap(): return lax.ppermute(x, axis, [(i, i ^ mask) for i in range(size)])]
    ppermute x33 -> x44, starting transfers between devices: 38.2 us -> 49.9 us  [swap(): return lax.ppermute(x, axis, [(i, i ^ mask) for i in range(size)])]
    transpose x7 -> x1, local copies, waits for them, and re-layouts: 10.4 us -> 0.65 us  [on_device(): jnp.concatenate([ffn_own[feat + t * cq:feat + (t + 1) * cq] for t in rang...]
    concatenate x12 -> x2, other arithmetic: 6.07 us -> 0.09 us  [outer(): jnp.concatenate([add_low(a, got_a), add_low(b, got_b)], 1)]
    slice x12 -> x19, local copies, waits for them, and re-layouts: 5.6 us -> 0.15 us  [the longest x8 0.06 us: outer(): self.b = [p[:, self.rows:] for p in pieces]]
    reshape x5 -> x0, local copies, waits for them, and re-layouts: 4.14 us -> none  [the longest x4 2.76 us: natural(): return a_nat[:, :, lo:lo + n].transpose(1, 0, 2).reshape(width, n * shards)]
    all_gather x1 -> x0, waiting for transfers between devices: 3.52 us -> none  [on_device(): lax.all_gather(jnp.concatenate([gu_own, dt_own], 0), ('ctx', 'fsdp'), axi...]
    pallas_call x5, Pallas kernels: 30.3 us -> 33.7 us  [call(): pl.pallas_call(kernel, out_shape=outs, in_specs=[smem] + [vmem] * (len(ar...]
  transfers between devices with their start and end apart: 34 -> 44, of which waited for: 26 -> 20; matrix products, arithmetic and copies ran while one was open for 16% -> 8% of each run, Pallas kernels for 4% -> 12%
where the time goes in v2:
time: 177 us
  waiting for transfers between devices  66.9 us (38%)
  starting transfers between devices  49.9 us (28%)
  Pallas kernels  33.7 us (19%)
  local copies, waits for them, and re-layouts  16.2 us (9%)
  other arithmetic  7.39 us (4%)
  between operations  2.78 us (2%)
    ppermute x44, waiting for transfers between devices, swap(): return lax.ppermute(x, axis, [(i, i ^ mask) for i in range(size)])  66.9 us
    ppermute x44, starting transfers between devices, swap(): return lax.ppermute(x, axis, [(i, i ^ mask) for i in range(size)])  49.9 us
    pallas_call x5, Pallas kernels, call(): pl.pallas_call(kernel, out_shape=outs, in_specs=[smem] + [vmem] * (len(ar...  33.7 us
    unnamed x77, local copies, waits for them, and re-layouts  11.4 us
  transfers between devices with their start and end apart: 44, of which 20 were waited for; matrix products, arithmetic and copies ran while one was open for 8% of the time, Pallas kernels for 12%

profile of v2, /device:TPU:0, one launch (start us, length us, event | category | flops | bytes accessed | tf_op | source)
XLA Modules:
  0.0 176.9 jit_solution(9716420966088267980)
XLA Ops:
  4.1 5.1 %collective-permute-start.2 = (bf16[1,152,256]{2,1,0:T(8,128)(2,1)S(1)}, bf16[1,152,256]{2,1,0:T(8,128)(2,1)S(1)}, u32[]{:S(2)}, u32[]{:S(2)}) collective-permute-start(bf16[1,152,256]{2,1,0:T(8,128)(2,1)S(1)} %maximum_bitcast_fusion.1), channel_id=1, source_target_pairs={{0,24},{4,28},{8,16},{12,20},{16,8},{20,12},{24,0},{28,4},{1,25},{... | collective-permute-start | bytes 233480 | tf_op jit(solution)/shard_map/ppermute | solution.py:34
  15.8 2.8 %collective-permute-start.7 = (bf16[1,216,384]{2,1,0:T(8,128)(2,1)S(1)}, bf16[1,216,384]{2,1,0:T(8,128)(2,1)S(1)}, u32[]{:S(2)}, u32[]{:S(2)}) collective-permute-start(bf16[1,216,384]{2,1,0:T(8,128)(2,1)S(1)} %maximum_bitcast_fusion), channel_id=1, source_target_pairs={{0,24},{4,28},{8,16},{12,20},{16,8},{20,12},{24,0},{28,4},{1,25},{... | collective-permute-start | bytes 497672 | tf_op jit(solution)/shard_map/ppermute | solution.py:34
  28.9 3.2 %collective-permute-done.6 = bf16[1,216,384]{2,1,0:T(8,128)(2,1)S(1)} collective-permute-done((bf16[1,216,384]{2,1,0:T(8,128)(2,1)S(1)}, bf16[1,216,384]{2,1,0:T(8,128)(2,1)S(1)}, u32[]{:S(2)}, u32[]{:S(2)}) %collective-permute-start.6) | collective-permute-done | bytes 165920 | tf_op jit(solution)/shard_map/ppermute | solution.py:34
  34.3 4.3 %collective-permute-done.4 = bf16[8,80,256]{2,1,0:T(8,128)(2,1)S(1)} collective-permute-done((bf16[8,80,256]{2,1,0:T(8,128)(2,1)S(1)}, bf16[8,80,256]{2,1,0:T(8,128)(2,1)S(1)}, u32[]{:S(2)}, u32[]{:S(2)}) %collective-permute-start.4) | collective-permute-done | bytes 327712 | tf_op jit(solution)/shard_map/ppermute | solution.py:34
  42.8 4.5 %shard_map.203 = (bf16[1152,128]{1,0:T(8,128)(2,1)}, bf16[128,384]{1,0:T(8,128)(2,1)}, bf16[8,576,256]{2,1,0:T(8,128)(2,1)}, f32[8,1280]{1,0:T(8,128)}) custom-call(s32[10]{0:T(128)} %pad_add_fusion.meta, bf16[128,576]{1,0:T(8,128)(2,1)} %bitcast.30, bf16[16,80,256]{2,1,0:T(8,128)(2,1)} %copy-done.2, bf16[16,80,256]{2,1,0:T(8,128)(2,1)} %copy-done.7, ...), custom_call_target="tpu_custom_call" | custom-call | flops 150994944 | bytes 6000000 | tf_op jit(solution)/shard_map/pallas_call | solution.py:541
  47.3 2.1 %collective-permute-done.16 = bf16[4,112,384]{2,1,0:T(8,128)(2,1)S(1)} collective-permute-done((bf16[4,112,384]{2,1,0:T(8,128)(2,1)S(1)}, bf16[4,112,384]{2,1,0:T(8,128)(2,1)S(1)}, u32[]{:S(2)}, u32[]{:S(2)}) %collective-permute-start.16) | collective-permute-done | bytes 344096 | tf_op jit(solution)/shard_map/ppermute | solution.py:34
  50.5 4.4 %collective-permute-start.14 = (bf16[1,128,384]{2,1,0:T(8,128)(2,1)S(1)}, bf16[1,128,384]{2,1,0:T(8,128)(2,1)S(1)}, u32[]{:S(2)}, u32[]{:S(2)}) collective-permute-start(bf16[1,128,384]{2,1,0:T(8,128)(2,1)S(1)} %bitcast.37), channel_id=1, source_target_pairs={{0,24},{4,28},{8,16},{12,20},{16,8},{20,12},{24,0},{28,4},{1,25},{... | collective-permute-start | bytes 294920 | tf_op jit(solution)/shard_map/ppermute | solution.py:34
  55.6 3.0 %collective-permute-done.14 = bf16[1,128,384]{2,1,0:T(8,128)(2,1)S(1)} collective-permute-done((bf16[1,128,384]{2,1,0:T(8,128)(2,1)S(1)}, bf16[1,128,384]{2,1,0:T(8,128)(2,1)S(1)}, u32[]{:S(2)}, u32[]{:S(2)}) %collective-permute-start.14) | collective-permute-done | bytes 98336 | tf_op jit(solution)/shard_map/ppermute | solution.py:34
  58.6 4.0 %collective-permute-done.13 = bf16[1,128,384]{2,1,0:T(8,128)(2,1)S(1)} collective-permute-done((bf16[1,128,384]{2,1,0:T(8,128)(2,1)S(1)}, bf16[1,128,384]{2,1,0:T(8,128)(2,1)S(1)}, u32[]{:S(2)}, u32[]{:S(2)}) %collective-permute-start.13) | collective-permute-done | bytes 98336 | tf_op jit(solution)/shard_map/ppermute | solution.py:34
  62.7 2.9 %collective-permute-done.20 = bf16[8,104,384]{2,1,0:T(8,128)(2,1)S(1)} collective-permute-done((bf16[8,104,384]{2,1,0:T(8,128)(2,1)S(1)}, bf16[8,104,384]{2,1,0:T(8,128)(2,1)S(1)}, u32[]{:S(2)}, u32[]{:S(2)}) %collective-permute-start.20) | collective-permute-done | bytes 639008 | tf_op jit(solution)/shard_map/ppermute | solution.py:34
  70.9 8.5 %collective-permute-done.15.far_ref = bf16[4,128,384]{2,1,0:T(8,128)(2,1)} collective-permute-done((bf16[4,128,384]{2,1,0:T(8,128)(2,1)S(1)}, bf16[4,128,384]{2,1,0:T(8,128)(2,1)}, u32[]{:S(2)}, u32[]{:S(2)}) %collective-permute-start.15) | collective-permute-done | bytes 393248 | tf_op jit(solution)/shard_map/ppermute | solution.py:34
  79.4 4.3 %shard_map.204 = (bf16[128,576]{1,0:T(8,128)(2,1)}, f32[3,128,384]{2,1,0:T(8,128)}, f32[8,384]{1,0:T(8,128)}) custom-call(s32[10]{0:T(128)} %pad_add_fusion.meta, bf16[1152,128]{1,0:T(8,128)(2,1)} %get-tuple-element.127.qp_ref, bf16[4,128,384]{2,1,0:T(8,128)(2,1)} %copy-done.20, bf16[4,128,384]{2,1,0:T(8,128)(2,1)} %collective-permute-done.15.far_ref), custom_call_target="tpu_custom_call" | custom-call | flops 603979776 | bytes 3000000 | tf_op jit(solution)/shard_map/pallas_call | solution.py:541
  83.8 12.9 %shard_map.205 = (bf16[128,576]{1,0:T(8,128)(2,1)}, bf16[16,112,384]{2,1,0:T(8,128)(2,1)}, bf16[16,112,384]{2,1,0:T(8,128)(2,1)}, bf16[16,104,384]{2,1,0:T(8,128...) custom-call(s32[10]{0:T(128)} %pad_add_fusion.meta, ...), custom_call_target="tpu_custom_call" | custom-call | flops 2038431744 | bytes 14000000 | tf_op jit(solution)/shard_map/pallas_call | solution.py:541
  97.2 6.5 %shard_map.206 = (bf16[128,576]{1,0:T(8,128)(2,1)}, bf16[4,128,384]{2,1,0:T(8,128)(2,1)}, bf16[4,128,384]{2,1,0:T(8,128)(2,1)}) custom-call(s32[10]{0:T(128)} %pad_add_fusion.meta, bf16[1152,128]{1,0:T(8,128)(2,1)} %get-tuple-element.127.qp_ref, bf16[1152,128]{1,0:T(8,128)(2,1)} %get-tuple-element.153.gp_ref, bf16[4,128,384]{2,1,0:T(8,128)(2,1)} %copy-done.20, ...), custom_call_target="tpu_custom_call" | custom-call | flops 1509949440 | bytes 5000000 | tf_op jit(solution)/shard_map/pallas_call | solution.py:541
  108.8 9.2 %collective-permute-done.24 = bf16[4,128,384]{2,1,0:T(8,128)(2,1)S(1)} collective-permute-done((bf16[4,128,384]{2,1,0:T(8,128)(2,1)S(1)}, bf16[4,128,384]{2,1,0:T(8,128)(2,1)S(1)}, u32[]{:S(2)}, u32[]{:S(2)}) %collective-permute-start.24) | collective-permute-done | bytes 393248 | tf_op jit(solution)/shard_map/ppermute | solution.py:34
  118.2 4.4 %collective-permute-start.27 = (bf16[1,128,384]{2,1,0:T(8,128)(2,1)S(1)}, bf16[1,128,384]{2,1,0:T(8,128)(2,1)S(1)}, u32[]{:S(2)}, u32[]{:S(2)}) collective-permute-start(bf16[1,128,384]{2,1,0:T(8,128)(2,1)S(1)} %get-tuple-element.251), channel_id=1, source_target_pairs={{0,24},{4,28},{8,16},{12,20},{16,8},{20,12},{24,0},{28,4},{1,25},{... | collective-permute-start | bytes 294920 | tf_op jit(solution)/shard_map/ppermute | solution.py:34
  123.2 7.6 %collective-permute-done.29 = bf16[8,104,384]{2,1,0:T(8,128)(2,1)S(1)} collective-permute-done((bf16[8,104,384]{2,1,0:T(8,128)(2,1)S(1)}, bf16[8,104,384]{2,1,0:T(8,128)(2,1)S(1)}, u32[]{:S(2)}, u32[]{:S(2)}) %collective-permute-start.29) | collective-permute-done | bytes 639008 | tf_op jit(solution)/shard_map/ppermute | solution.py:34
  134.1 5.5 %shard_map.207 = (f32[128,576]{1,0:T(8,128)}, bf16[16,80,256]{2,1,0:T(8,128)(2,1)}, bf16[16,80,256]{2,1,0:T(8,128)(2,1)}, bf16[16,72,256]{2,1,0:T(8,128)(2,1)}, bf16[16,72,256]{2,1,0:T(8,128)(2,1)}) custom-call(s32[10]{0:T(128)} %pad_add_fusion.meta, bf16[128,576]{1,0:T(8,128)(2,1)} %bitcast.32, bf16[128,576]{1,0:T(8,128)(2,1)} %get-tuple-element.156.dq_ref, ...), custom_call_target="tpu_custom_call" | custom-call | flops 905969664 | bytes 6000000 | tf_op jit(solution)/shard_map/pallas_call | solution.py:541
  146.4 4.4 %collective-permute-start.43 = (bf16[1,216,384]{2,1,0:T(8,128)(2,1)S(1)}, bf16[1,216,384]{2,1,0:T(8,128)(2,1)S(1)}, u32[]{:S(2)}, u32[]{:S(2)}) collective-permute-start(bf16[1,216,384]{2,1,0:T(8,128)(2,1)S(1)} %get-tuple-element.243), channel_id=1, source_target_pairs={{0,24},{4,28},{8,16},{12,20},{16,8},{20,12},{24,0},{28,4},{1,25},{... | collective-permute-start | bytes 497672 | tf_op jit(solution)/shard_map/ppermute | solution.py:34
  151.5 2.8 %collective-permute-done.35 = bf16[8,72,256]{2,1,0:T(8,128)(2,1)S(1)} collective-permute-done((bf16[8,72,256]{2,1,0:T(8,128)(2,1)S(1)}, bf16[8,72,256]{2,1,0:T(8,128)(2,1)S(1)}, u32[]{:S(2)}, u32[]{:S(2)}) %collective-permute-start.35) | collective-permute-done | bytes 294944 | tf_op jit(solution)/shard_map/ppermute | solution.py:34
  156.4 3.8 %collective-permute-done.41 = bf16[1,216,384]{2,1,0:T(8,128)(2,1)S(1)} collective-permute-done((bf16[1,216,384]{2,1,0:T(8,128)(2,1)S(1)}, bf16[1,216,384]{2,1,0:T(8,128)(2,1)S(1)}, u32[]{:S(2)}, u32[]{:S(2)}) %collective-permute-start.41) | collective-permute-done | bytes 165920 | tf_op jit(solution)/shard_map/ppermute | solution.py:34
  160.2 3.9 %collective-permute-done.42 = bf16[1,216,384]{2,1,0:T(8,128)(2,1)S(1)} collective-permute-done((bf16[1,216,384]{2,1,0:T(8,128)(2,1)S(1)}, bf16[1,216,384]{2,1,0:T(8,128)(2,1)S(1)}, u32[]{:S(2)}, u32[]{:S(2)}) %collective-permute-start.42) | collective-permute-done | bytes 165920 | tf_op jit(solution)/shard_map/ppermute | solution.py:34
  165.0 2.1 %collective-permute-start.40 = (bf16[1,152,256]{2,1,0:T(8,128)(2,1)S(1)}, bf16[1,152,256]{2,1,0:T(8,128)(2,1)S(1)}, u32[]{:S(2)}, u32[]{:S(2)}) collective-permute-start(bf16[1,152,256]{2,1,0:T(8,128)(2,1)S(1)} %get-tuple-element.257), channel_id=1, source_target_pairs={{0,24},{4,28},{8,16},{12,20},{16,8},{20,12},{24,0},{28,4},{1,25},{... | collective-permute-start | bytes 233480 | tf_op jit(solution)/shard_map/ppermute | solution.py:34
  167.1 2.4 %collective-permute-start.39 = (bf16[1,152,256]{2,1,0:T(8,128)(2,1)S(1)}, bf16[1,152,256]{2,1,0:T(8,128)(2,1)S(1)}, u32[]{:S(2)}, u32[]{:S(2)}) collective-permute-start(bf16[1,152,256]{2,1,0:T(8,128)(2,1)S(1)} %get-tuple-element.260), channel_id=1, source_target_pairs={{0,16},{4,20},{8,24},{12,28},{16,0},{20,4},{24,8},{28,12},{1,17},{... | collective-permute-start | bytes 233480 | tf_op jit(solution)/shard_map/ppermute | solution.py:34
  (218 shorter events, 59.7 us)
Async XLA Ops:
  4.1 10.6 %collective-permute-start.2 = (bf16[1,152,256]{2,1,0:T(8,128)(2,1)S(1)}, bf16[1,152,256]{2,1,0:T(8,128)(2,1)S(1)}, u32[]{:S(2)}, u32[]{:S(2)}) collective-permute-start(bf16[1,152,256]{2,1,0:T(8,128)(2,1)S(1)} %maximum_bitcast_fusion.1), channel_id=1, source_target_pairs={{0,24},{4,28},{8,16},{12,20},{16,8},{20,12},{24,0},{28,4},{1,25},{... | collective-permute-start | bytes 233480 | tf_op jit(solution)/shard_map/ppermute | solution.py:34
  15.8 13.1 %collective-permute-start.7 = (bf16[1,216,384]{2,1,0:T(8,128)(2,1)S(1)}, bf16[1,216,384]{2,1,0:T(8,128)(2,1)S(1)}, u32[]{:S(2)}, u32[]{:S(2)}) collective-permute-start(bf16[1,216,384]{2,1,0:T(8,128)(2,1)S(1)} %maximum_bitcast_fusion), channel_id=1, source_target_pairs={{0,24},{4,28},{8,16},{12,20},{16,8},{20,12},{24,0},{28,4},{1,25},{... | collective-permute-start | bytes 497672 | tf_op jit(solution)/shard_map/ppermute | solution.py:34
  18.6 13.5 %collective-permute-start.6 = (bf16[1,216,384]{2,1,0:T(8,128)(2,1)S(1)}, bf16[1,216,384]{2,1,0:T(8,128)(2,1)S(1)}, u32[]{:S(2)}, u32[]{:S(2)}) collective-permute-start(bf16[1,216,384]{2,1,0:T(8,128)(2,1)S(1)} %maximum_bitcast_fusion), channel_id=1, source_target_pairs={{0,16},{4,20},{8,24},{12,28},{16,0},{20,4},{24,8},{28,12},{1,17},{... | collective-permute-start | bytes 497672 | tf_op jit(solution)/shard_map/ppermute | solution.py:34
  18.6 13.5 %collective-permute-start.5 = (bf16[1,216,384]{2,1,0:T(8,128)(2,1)S(1)}, bf16[1,216,384]{2,1,0:T(8,128)(2,1)S(1)}, u32[]{:S(2)}, u32[]{:S(2)}) collective-permute-start(bf16[1,216,384]{2,1,0:T(8,128)(2,1)S(1)} %maximum_bitcast_fusion), channel_id=1, source_target_pairs={{0,8},{4,12},{8,0},{12,4},{16,24},{20,28},{24,16},{28,20},{1,9},{5... | collective-permute-start | bytes 497672 | tf_op jit(solution)/shard_map/ppermute | solution.py:34
  28.8 9.8 %collective-permute-start.4 = (bf16[8,80,256]{2,1,0:T(8,128)(2,1)S(1)}, bf16[8,80,256]{2,1,0:T(8,128)(2,1)S(1)}, u32[]{:S(2)}, u32[]{:S(2)}) collective-permute-start(bf16[8,80,256]{2,1,0:T(8,128)(2,1)S(1)} %constant_dynamic-update-slice_fusion.4), channel_id=1, source_target_pairs={{0,2},{1,3},{2,0},{3,1},{4,6},{5,7},{6,4},{7,5},{8,10},{9,11},{10,... | collective-permute-start | bytes 983048 | tf_op jit(solution)/shard_map/ppermute | solution.py:34
  32.3 15.0 %collective-permute-start.19 = (bf16[4,104,384]{2,1,0:T(8,128)(2,1)S(1)}, bf16[4,104,384]{2,1,0:T(8,128)(2,1)S(1)}, u32[]{:S(2)}, u32[]{:S(2)}) collective-permute-start(bf16[4,104,384]{2,1,0:T(8,128)(2,1)S(1)} %constant_dynamic-update-slice_fusion.28), channel_id=1, source_target_pairs={{0,2},{1,3},{2,0},{3,1},{4,6},{5,7},{6,4},{7,5},{8,10},{9,11},{10,... | collective-permute-start | bytes 958472 | tf_op jit(solution)/shard_map/ppermute | solution.py:34
  38.8 10.5 %collective-permute-start.16 = (bf16[4,112,384]{2,1,0:T(8,128)(2,1)S(1)}, bf16[4,112,384]{2,1,0:T(8,128)(2,1)S(1)}, u32[]{:S(2)}, u32[]{:S(2)}) collective-permute-start(bf16[4,112,384]{2,1,0:T(8,128)(2,1)S(1)} %constant_dynamic-update-slice_fusion.20), channel_id=1, source_target_pairs={{0,4},{4,0},{8,12},{12,8},{16,20},{20,16},{24,28},{28,24},{1,5},{5... | collective-permute-start | bytes 1032200 | tf_op jit(solution)/shard_map/ppermute | solution.py:34
  49.5 16.1 %collective-permute-start.20 = (bf16[8,104,384]{2,1,0:T(8,128)(2,1)S(1)}, bf16[8,104,384]{2,1,0:T(8,128)(2,1)S(1)}, u32[]{:S(2)}, u32[]{:S(2)}) collective-permute-start(bf16[8,104,384]{2,1,0:T(8,128)(2,1)S(1)} %constant_dynamic-update-slice_fusion.32), channel_id=1, source_target_pairs={{0,4},{4,0},{8,12},{12,8},{16,20},{20,16},{24,28},{28,24},{1,5},{5... | collective-permute-start | bytes 1916936 | tf_op jit(solution)/shard_map/ppermute | solution.py:34
  50.4 16.8 %collective-permute-start.17 = (bf16[8,112,384]{2,1,0:T(8,128)(2,1)S(1)}, bf16[8,112,384]{2,1,0:T(8,128)(2,1)S(1)}, u32[]{:S(2)}, u32[]{:S(2)}) collective-permute-start(bf16[8,112,384]{2,1,0:T(8,128)(2,1)S(1)} %constant_dynamic-update-slice_fusion.24), channel_id=1, source_target_pairs={{0,2},{1,3},{2,0},{3,1},{4,6},{5,7},{6,4},{7,5},{8,10},{9,11},{10,... | collective-permute-start | bytes 2064392 | tf_op jit(solution)/shard_map/ppermute | solution.py:34
  67.5 16.3 %collective-permute-start.18 = (bf16[16,112,384]{2,1,0:T(8,128)(2,1)S(1)}, bf16[16,112,384]{2,1,0:T(8,128)(2,1)}, u32[]{:S(2)}, u32[]{:S(2)}) collective-permute-start(bf16[16,112,384]{2,1,0:T(8,128)(2,1)S(1)} %constant_dynamic-update-slice_fusion.26.refs_0_), channel_id=1, source_target_pairs={{0,1},{1,0},{2,3},{3,2},{4,5},{5,4},{6,7},{7,6},{8,9},{9,8},{10,11... | collective-permute-start | bytes 4128776 | tf_op jit(solution)/shard_map/ppermute | solution.py:34
  67.7 16.1 %collective-permute-start.21 = (bf16[16,104,384]{2,1,0:T(8,128)(2,1)S(1)}, bf16[16,104,384]{2,1,0:T(8,128)(2,1)}, u32[]{:S(2)}, u32[]{:S(2)}) collective-permute-start(bf16[16,104,384]{2,1,0:T(8,128)(2,1)S(1)} %constant_dynamic-update-slice_fusion.34.refs_2_), channel_id=1, source_target_pairs={{0,1},{1,0},{2,3},{3,2},{4,5},{5,4},{6,7},{7,6},{8,9},{9,8},{10,11... | collective-permute-start | bytes 3833864 | tf_op jit(solution)/shard_map/ppermute | solution.py:34
  68.2 11.2 %collective-permute-start.15 = (bf16[4,128,384]{2,1,0:T(8,128)(2,1)S(1)}, bf16[4,128,384]{2,1,0:T(8,128)(2,1)}, u32[]{:S(2)}, u32[]{:S(2)}) collective-permute-start(bf16[4,128,384]{2,1,0:T(8,128)(2,1)S(1)} %constant_dynamic-update-slice_fusion.16.near_ref), channel_id=1, source_target_pairs={{0,4},{4,0},{8,12},{12,8},{16,20},{20,16},{24,28},{28,24},{1,5},{5... | collective-permute-start | bytes 1179656 | tf_op jit(solution)/shard_map/ppermute | solution.py:34
  106.0 12.0 %collective-permute-start.24 = (bf16[4,128,384]{2,1,0:T(8,128)(2,1)S(1)}, bf16[4,128,384]{2,1,0:T(8,128)(2,1)S(1)}, u32[]{:S(2)}, u32[]{:S(2)}) collective-permute-start(bf16[4,128,384]{2,1,0:T(8,128)(2,1)S(1)} %copy-done.22), channel_id=1, source_target_pairs={{0,4},{4,0},{8,12},{12,8},{16,20},{20,16},{24,28},{28,24},{1,5},{5... | collective-permute-start | bytes 1179656 | tf_op jit(solution)/shard_map/ppermute | solution.py:34
  107.3 23.5 %collective-permute-start.28 = (bf16[8,112,384]{2,1,0:T(8,128)(2,1)S(1)}, bf16[8,112,384]{2,1,0:T(8,128)(2,1)S(1)}, u32[]{:S(2)}, u32[]{:S(2)}) collective-permute-start(bf16[8,112,384]{2,1,0:T(8,128)(2,1)S(1)} %get-tuple-element.232), channel_id=1, source_target_pairs={{0,2},{1,3},{2,0},{3,1},{4,6},{5,7},{6,4},{7,5},{8,10},{9,11},{10,... | collective-permute-start | bytes 2064392 | tf_op jit(solution)/shard_map/ppermute | solution.py:34
  108.1 22.7 %collective-permute-start.29 = (bf16[8,104,384]{2,1,0:T(8,128)(2,1)S(1)}, bf16[8,104,384]{2,1,0:T(8,128)(2,1)S(1)}, u32[]{:S(2)}, u32[]{:S(2)}) collective-permute-start(bf16[8,104,384]{2,1,0:T(8,128)(2,1)S(1)} %get-tuple-element.234), channel_id=1, source_target_pairs={{0,4},{4,0},{8,12},{12,8},{16,20},{20,16},{24,28},{28,24},{1,5},{5... | collective-permute-start | bytes 1916936 | tf_op jit(solution)/shard_map/ppermute | solution.py:34
  118.2 15.2 %collective-permute-start.27 = (bf16[1,128,384]{2,1,0:T(8,128)(2,1)S(1)}, bf16[1,128,384]{2,1,0:T(8,128)(2,1)S(1)}, u32[]{:S(2)}, u32[]{:S(2)}) collective-permute-start(bf16[1,128,384]{2,1,0:T(8,128)(2,1)S(1)} %get-tuple-element.251), channel_id=1, source_target_pairs={{0,24},{4,28},{8,16},{12,20},{16,8},{20,12},{24,0},{28,4},{1,25},{... | collective-permute-start | bytes 294920 | tf_op jit(solution)/shard_map/ppermute | solution.py:34
  122.6 10.8 %collective-permute-start.26 = (bf16[1,128,384]{2,1,0:T(8,128)(2,1)S(1)}, bf16[1,128,384]{2,1,0:T(8,128)(2,1)S(1)}, u32[]{:S(2)}, u32[]{:S(2)}) collective-permute-start(bf16[1,128,384]{2,1,0:T(8,128)(2,1)S(1)} %get-tuple-element.252), channel_id=1, source_target_pairs={{0,16},{4,20},{8,24},{12,28},{16,0},{20,4},{24,8},{28,12},{1,17},{... | collective-permute-start | bytes 294920 | tf_op jit(solution)/shard_map/ppermute | solution.py:34
  122.6 10.8 %collective-permute-start.25 = (bf16[1,128,384]{2,1,0:T(8,128)(2,1)S(1)}, bf16[1,128,384]{2,1,0:T(8,128)(2,1)S(1)}, u32[]{:S(2)}, u32[]{:S(2)}) collective-permute-start(bf16[1,128,384]{2,1,0:T(8,128)(2,1)S(1)} %get-tuple-element.253), channel_id=1, source_target_pairs={{0,8},{4,12},{8,0},{12,4},{16,24},{20,28},{24,16},{28,20},{1,9},{5... | collective-permute-start | bytes 294920 | tf_op jit(solution)/shard_map/ppermute | solution.py:34
  131.0 9.9 %collective-permute-start.30 = (bf16[4,112,384]{2,1,0:T(8,128)(2,1)S(1)}, bf16[4,112,384]{2,1,0:T(8,128)(2,1)S(1)}, u32[]{:S(2)}, u32[]{:S(2)}) collective-permute-start(bf16[4,112,384]{2,1,0:T(8,128)(2,1)S(1)} %get-tuple-element.236), channel_id=1, source_target_pairs={{0,4},{4,0},{8,12},{12,8},{16,20},{20,16},{24,28},{28,24},{1,5},{5... | collective-permute-start | bytes 1032200 | tf_op jit(solution)/shard_map/ppermute | solution.py:34
  144.4 9.9 %collective-permute-start.34 = (bf16[8,80,256]{2,1,0:T(8,128)(2,1)S(1)}, bf16[8,80,256]{2,1,0:T(8,128)(2,1)S(1)}, u32[]{:S(2)}, u32[]{:S(2)}) collective-permute-start(bf16[8,80,256]{2,1,0:T(8,128)(2,1)S(1)} %get-tuple-element.237), channel_id=1, source_target_pairs={{0,2},{1,3},{2,0},{3,1},{4,6},{5,7},{6,4},{7,5},{8,10},{9,11},{10,... | collective-permute-start | bytes 983048 | tf_op jit(solution)/shard_map/ppermute | solution.py:34
  146.4 10.0 %collective-permute-start.43 = (bf16[1,216,384]{2,1,0:T(8,128)(2,1)S(1)}, bf16[1,216,384]{2,1,0:T(8,128)(2,1)S(1)}, u32[]{:S(2)}, u32[]{:S(2)}) collective-permute-start(bf16[1,216,384]{2,1,0:T(8,128)(2,1)S(1)} %get-tuple-element.243), channel_id=1, source_target_pairs={{0,24},{4,28},{8,16},{12,20},{16,8},{20,12},{24,0},{28,4},{1,25},{... | collective-permute-start | bytes 497672 | tf_op jit(solution)/shard_map/ppermute | solution.py:34
  150.8 13.2 %collective-permute-start.42 = (bf16[1,216,384]{2,1,0:T(8,128)(2,1)S(1)}, bf16[1,216,384]{2,1,0:T(8,128)(2,1)S(1)}, u32[]{:S(2)}, u32[]{:S(2)}) collective-permute-start(bf16[1,216,384]{2,1,0:T(8,128)(2,1)S(1)} %get-tuple-element.246), channel_id=1, source_target_pairs={{0,16},{4,20},{8,24},{12,28},{16,0},{20,4},{24,8},{28,12},{1,17},{... | collective-permute-start | bytes 497672 | tf_op jit(solution)/shard_map/ppermute | solution.py:34
  154.4 10.5 %collective-permute-start.36 = (bf16[4,80,256]{2,1,0:T(8,128)(2,1)S(1)}, bf16[4,80,256]{2,1,0:T(8,128)(2,1)S(1)}, u32[]{:S(2)}, u32[]{:S(2)}) collective-permute-start(bf16[4,80,256]{2,1,0:T(8,128)(2,1)S(1)} %get-tuple-element.247), channel_id=1, source_target_pairs={{0,4},{4,0},{8,12},{12,8},{16,20},{20,16},{24,28},{28,24},{1,5},{5... | collective-permute-start | bytes 491528 | tf_op jit(solution)/shard_map/ppermute | solution.py:34
  155.3 9.6 %collective-permute-start.37 = (bf16[4,72,256]{2,1,0:T(8,128)(2,1)S(1)}, bf16[4,72,256]{2,1,0:T(8,128)(2,1)S(1)}, u32[]{:S(2)}, u32[]{:S(2)}) collective-permute-start(bf16[4,72,256]{2,1,0:T(8,128)(2,1)S(1)} %get-tuple-element.249), channel_id=1, source_target_pairs={{0,2},{1,3},{2,0},{3,1},{4,6},{5,7},{6,4},{7,5},{8,10},{9,11},{10,... | collective-permute-start | bytes 442376 | tf_op jit(solution)/shard_map/ppermute | solution.py:34
  (45 other events, 291.9 us)

commit v3 on v2

--- a/solution.py
+++ b/solution.py
@@ -20,6 +20,7 @@
 F32 = jnp.float32
 BF16 = jnp.bfloat16
 VMEM_BYTES = 56 * 1024 * 1024
+CHIP_BYTES = 24 * 1024 * 1024
 
 K_TILE, K_HALF = (0, 0, 1), (0, 1, 0)
 V_TILE, V_HALF = (1, 2, 2), (1, 0, 1)
@@ -98,6 +99,11 @@
     def third(self, *before):
         self.phase("fsdp", 2, "ctx", 1, *before)
 
+    def cores_apart(self, *before):
+        near, far = lax.optimization_barrier((*self.a, *before))[:2]
+        b = join(self.b, *before)
+        return near, far, swap(near, "fsdp", 1), swap(far, "fsdp", 1), b, swap(b, "fsdp", 1)
+
     def cores(self, *before):
         self.phase("fsdp", 1, "fsdp", 1, *before)
         return *self.a, *self.b
@@ -158,6 +164,15 @@
                 out_ref[:, m * feat : (m + 1) * feat] = value[:, (m ^ k) * feat : ((m ^ k) + 1) * feat]
 
 
+def chunk_rows(parts, c, mc, fsdp, split, feat, shards, lanes):
+    pieces = []
+    for m in range(fsdp):
+        a_ref, b_ref = parts[m & 1], parts[2 + (m & 1)]
+        pieces.append(a_ref[place_a(c ^ mc, m >> 1, shards), :, lanes])
+        pieces.append(b_ref[place_b(c ^ mc, m >> 1, shards), : feat - split, lanes])
+    return jnp.concatenate(pieces, 0)
+
+
 def dot(a, b):
     return lax.dot_general(a, b, (((1,), (0,)), ((), ())), preferred_element_type=F32)
 
@@ -196,10 +211,11 @@
 
 def qkv_kernel(
     dims, meta, x_ref, ao_ref, as_ref, bo_ref, bs_ref, cos_ref, sin_ref,
-    qp_ref, kv_ref, an_ref, gain_ref, q_s, kv_s, n_s,
+    qp_ref, kv_ref, gain_ref, q_s, kv_s, n_s,
 ):
     shards, fsdp, cq, ck, split, feat = dims
     mc, mf = meta[shards], meta[shards + 1]
+    parts = ao_ref, as_ref, bo_ref, bs_ref
     kvw = KEY_VALUE_HEADS * HEAD_DIM
     for c in range(shards):
         row = bo_ref[place_b(c ^ mc, 0, shards)][feat - split :, :].astype(F32)
@@ -211,12 +227,8 @@
     arrange(n_s, x * rr * gain_ref[0:1, :width], mf, feat)
     normed = n_s[...].astype(BF16)
     for c in range(shards):
-        for m in range(fsdp):
-            a_ref, b_ref = ((ao_ref, bo_ref), (as_ref, bs_ref))[m & 1]
-            cut = m * feat + split
-            an_ref[c, m * feat : cut, :] = a_ref[place_a(c ^ mc, m >> 1, shards)]
-            an_ref[c, cut : (m + 1) * feat, :] = b_ref[place_b(c ^ mc, m >> 1, shards)][: feat - split]
-        y = dot(normed, an_ref[c, :, :128])
+        w = chunk_rows(parts, c, mc, fsdp, split, feat, shards, slice(0, 128))
+        y = dot(normed, w)
         q_s[:, c * cq : (c + 1) * cq] = y[:, :cq]
         kv_s[:, c * ck : (c + 1) * ck] = y[:, cq : cq + ck]
         kv_s[:, kvw + c * ck : kvw + (c + 1) * ck] = y[:, cq + ck : cq + 2 * ck]
@@ -250,11 +262,12 @@
     return out
 
 
-def block_rows(near_ref, far_ref, block, chunks):
-    here = pl.ds(block * (chunks // 2), chunks // 2)
-    return jnp.concatenate(
-        [r[here].reshape(-1, r.shape[2]) for r in (near_ref, far_ref)], 0
-    )
+def block_rows(refs, block, chunks, blocks):
+    if blocks == 1:
+        values = [r[...] for r in refs]
+    else:
+        values = [r[pl.ds(block * (chunks // 2), chunks // 2)] for r in refs]
+    return jnp.concatenate([v.reshape(-1, v.shape[2]) for v in values], 0)
 
 
 def masked(s, mask, blk):
@@ -263,7 +276,8 @@
     )
 
 
-def attend_kernel(dims, meta, qp_ref, near_ref, far_ref, att_ref, ot_ref, lse_ref, m_s, l_s):
+def attend_kernel(dims, meta, qp_ref, *refs):
+    *kv_refs, att_ref, ot_ref, lse_ref, m_s, l_s = refs
     shards, chunks, blk = dims
     blocks = shards // chunks
     rows = chunks * 2 * blk
@@ -271,7 +285,7 @@
 
     def block_step(b, first):
         mask = score_mask(meta, shards, b, chunks, blk)
-        kv = block_rows(near_ref, far_ref, b, chunks)
+        kv = block_rows(kv_refs, b, chunks, blocks)
         for g in range(KEY_VALUE_HEADS):
             keys = kv[:, K_TILE[g] * 128 : (K_TILE[g] + 1) * 128]
             vals = kv[:, V_TILE[g] * 128 : (V_TILE[g] + 1) * 128]
@@ -315,49 +329,59 @@
 
 
 def ffn_kernel(
-    dims, meta, att_ref, x_ref, dy_ref, an_ref, gain_ref, *refs
+    dims, meta, att_ref, x_ref, dy_ref, gain_ref, *refs
 ):
-    shards, fsdp, cq, cg, feat, ffr, split, packed = dims
-    ins = refs[:4] if packed else refs[:2]
+    shards, fsdp, cq, cg, feat, ffr, fsplit, split, packed, asplit = dims
+    ins, refs = (refs[:6], refs[6:]) if packed else (refs[:2], refs[2:])
+    parts, refs = refs[:4], refs[4:]
     (
         out_ref, ak_ref, as_ref, bk_ref, bs_ref, dmid_ref, ggain_ref, gp_ref,
-        gu_s, hid_s, dh_s, dgu_s, wide_s, p_s, w_s, dt_s,
-    ) = refs[len(ins) :]
+        gu_s, hid_s, dh_s, dgu_s, wide_s, p_s, dt_s,
+    ) = refs
     mc, mf = meta[shards], meta[shards + 1]
     lanes = ak_ref.shape[2]
     if packed:
         for c in range(0, shards, 2):
             for m in range(fsdp):
-                tails = []
-                for d in (c, c + 1):
-                    a_ref, b_ref = ins[m & 1], ins[2 + (m & 1)]
-                    w_s[d, m * feat : m * feat + split, :] = a_ref[place_a(d ^ mc, m >> 1, shards)]
-                    tail = b_ref[place_b(d ^ mc, m >> 1, shards)]
-                    w_s[d, m * feat + split : (m + 1) * feat, :] = tail[: feat - split]
-                    tails.append(tail[feat - split :].astype(F32))
-                dt_s[m, c * cq : (c + 2) * cq, :] = jnp.concatenate(tails, 0).astype(BF16)
+                b_ref = ins[4 + (m & 1)]
+                pair = [b_ref[place_b(d ^ mc, m >> 1, shards)][feat - fsplit :] for d in (c, c + 1)]
+                dt_s[m, c * cq : (c + 2) * cq, :] = jnp.concatenate(
+                    [p.astype(F32) for p in pair], 0
+                ).astype(BF16)
     else:
         for m in range(fsdp):
             dt_s[m] = ins[1][mf ^ m]
 
     def weights(c):
         if packed:
-            return w_s[c]
+            pieces = []
+            for m in range(fsdp):
+                pieces.append(ins[2 * (m & 1) + (m >> 1)][ctx_place(c ^ mc, shards)])
+                if fsplit < feat:
+                    b_ref = ins[4 + (m & 1)]
+                    pieces.append(b_ref[place_b(c ^ mc, m >> 1, shards), : feat - fsplit, :])
+            return jnp.concatenate(pieces, 0)
         return jnp.concatenate([ins[0][c, mf ^ m] for m in range(fsdp)], 0)
+
+    def outer(c):
+        return chunk_rows(parts, c, mc, fsdp, asplit, feat, shards, slice(-128, None))
 
     x = x_ref[...].astype(F32)
     width = x.shape[1]
-    dyl = dy_ref[...]
-    gain = gain_ref[0:1, :width]
+    dy_t = dy_ref[...]
+    dyf = jnp.transpose(dy_t.astype(F32))
+    dyl = dyf.astype(BF16)
+    gain = gain_ref[0:1, 640 : 640 + width]
     arrange(p_s, att_ref[...].astype(F32), mf, feat)
     attp = p_s[...].astype(BF16)
     for c in range(shards):
-        wide_s[:, c * cq : (c + 1) * cq] = dot(attp, an_ref[c, :, -128:])[:, :cq]
+        wide_s[:, c * cq : (c + 1) * cq] = dot(attp, outer(c))[:, :cq]
     mid = x + wide_s[:, :width]
     rr = lax.rsqrt(jnp.mean(mid * mid, axis=-1, keepdims=True) + EPS)
     z = mid * rr
     arrange(p_s, z * gain, mf, feat)
     normed = p_s[...].astype(BF16)
+    normed_t = jnp.transpose(p_s[...]).astype(BF16)
 
     def store_grad(c, m, row, value):
         end = row + value.shape[0]
@@ -382,12 +406,12 @@
         hid = hid_s[:, here].astype(BF16)
         out = out + dot_nt(hid, dt_s[m])
         dh_s[:, here] = dot(dyl, dt_s[m])
-        g = dot_tn(dyl, hid)
+        g = dot(dy_t, hid)
         for c in range(shards):
             piece = g[c * cq : (c + 1) * cq, :].astype(BF16)
             for t in range(ffr // lanes):
                 store_grad(c, m, feat + t * cq, piece[:, t * lanes : (t + 1) * lanes])
-    out_ref[...] = out.astype(BF16)
+    out_ref[...] = jnp.transpose(out).astype(BF16)
     dn = jnp.zeros_like(mid)
     for c in range(shards):
         gu = gu_s[c]
@@ -399,14 +423,14 @@
         dgu_s[:, :cg] = dh * up * sg * (1.0 + gate * (1.0 - sg))
         dgu_s[:, cg : 2 * cg] = dh * gate * sg
         dgu = dgu_s[...].astype(BF16)
-        g = dot_tn(normed, dgu)
+        g = dot(normed_t, dgu)
         for m in range(fsdp):
             store_grad(c, m, 0, g[m * feat : (m + 1) * feat, :].astype(BF16))
         dn = dn + dot_nt(dgu, weights(c))
     arrange(p_s, dn, mf, feat)
     dn = p_s[...]
     e = dn * gain
-    dmid = dyl.astype(F32) + rr * (e - z * jnp.mean(e * z, axis=-1, keepdims=True))
+    dmid = dyf + rr * (e - z * jnp.mean(e * z, axis=-1, keepdims=True))
     dmid_ref[...] = dmid
     ggain_ref[...] = jnp.broadcast_to(jnp.sum(dn * z, axis=0, keepdims=True), ggain_ref.shape)
     wide_s[...] = jnp.zeros_like(wide_s)
@@ -414,7 +438,7 @@
     ga = jnp.zeros_like(mid)
     for c in range(shards):
         gb = wide_s[:, c * cq : c * cq + 128].astype(BF16)
-        ga = ga + dot_nt(gb, an_ref[c, :, -128:])
+        ga = ga + dot_nt(gb, outer(c))
     arrange(p_s, ga, mf, feat)
     wide_s[:, :width] = p_s[...]
     for h in range(QUERY_HEADS):
@@ -424,9 +448,9 @@
 
 
 def attend_back_kernel(
-    dims, meta, qp_ref, gp_ref, near_ref, far_ref, ot_ref, lse_ref, cos_ref, sin_ref,
-    dq_ref, dnear_ref, dfar_ref, dq_s,
+    dims, meta, qp_ref, gp_ref, ot_ref, lse_ref, cos_ref, sin_ref, *refs
 ):
+    *kv_refs, dq_ref, dnear_ref, dfar_ref, dq_s = refs
     shards, chunks, blk = dims
     blocks = shards // chunks
     rows = chunks * 2 * blk
@@ -438,7 +462,7 @@
 
     def block_step(b, first):
         mask = score_mask(meta, shards, b, chunks, blk)
-        kv = block_rows(near_ref, far_ref, b, chunks)
+        kv = block_rows(kv_refs, b, chunks, blocks)
         tiles = [None, None, None]
 
         def put(t, value):
@@ -485,11 +509,13 @@
 
 
 def qkv_back_kernel(
-    dims, meta, x_ref, dq_ref, dkv_ref, att_ref, dmid_ref, an_ref, gain_ref, gg_ref,
-    cos_ref, sin_ref, gin_ref, ak_ref, as_ref, bk_ref, bs_ref, dq_s, dkv_s, d_s, p_s, gg_s,
+    dims, meta, x_ref, dq_ref, dkv_ref, att_ref, dmid_ref, gain_ref, gg_ref,
+    cos_ref, sin_ref, ao_ref, as_in, bo_ref, bs_in, gin_ref, ak_ref, as_ref, bk_ref, bs_ref,
+    dq_s, dkv_s, d_s, p_s, gg_s,
 ):
     shards, fsdp, cq, ck, split, feat = dims
     mc, mf = meta[shards], meta[shards + 1]
+    parts = ao_ref, as_in, bo_ref, bs_in
     kvw = KEY_VALUE_HEADS * HEAD_DIM
     x = x_ref[...].astype(F32)
     width = x.shape[1]
@@ -497,9 +523,9 @@
     rr = lax.rsqrt(jnp.mean(x * x, axis=-1, keepdims=True) + EPS)
     z = x * rr
     arrange(p_s, z * gain, mf, feat)
-    normed = p_s[...].astype(BF16)
+    normed_t = jnp.transpose(p_s[...]).astype(BF16)
     arrange(p_s, att_ref[...].astype(F32), mf, feat)
-    att = p_s[...].astype(BF16)
+    att_t = jnp.transpose(p_s[...]).astype(BF16)
     cos, sin = cos_ref[...], sin_ref[...]
     for t in range(3):
         u = dkv_ref[:, t * 128 : (t + 1) * 128]
@@ -516,8 +542,9 @@
         d_s[:, cq + ck : cq + 2 * ck] = dkv_s[:, kvw + c * ck : kvw + (c + 1) * ck]
         d_s[:, 128 : 128 + cq] = dmid_ref[:, c * cq : (c + 1) * cq]
         d = d_s[...].astype(BF16)
-        dn = dn + dot_nt(d[:, :128], an_ref[c, :, :128])
-        g = jnp.concatenate([dot_tn(normed, d[:, :128]), dot_tn(att, d[:, 128:])], 1).astype(BF16)
+        w = chunk_rows(parts, c, mc, fsdp, split, feat, shards, slice(0, 128))
+        dn = dn + dot_nt(d[:, :128], w)
+        g = jnp.concatenate([dot(normed_t, d[:, :128]), dot(att_t, d[:, 128:])], 1).astype(BF16)
         for m in range(fsdp):
             part = g[m * feat : (m + 1) * feat, :]
             (ak_ref, as_ref)[m & 1][place_a(c ^ mc, m >> 1, shards)] = part[:split]
@@ -525,7 +552,8 @@
     arrange(p_s, dn, mf, feat)
     dn = p_s[...]
     e = dn * gain
-    gin_ref[...] = dmid_ref[...] + rr * (e - z * jnp.mean(e * z, axis=-1, keepdims=True))
+    gin = dmid_ref[...] + rr * (e - z * jnp.mean(e * z, axis=-1, keepdims=True))
+    gin_ref[...] = jnp.transpose(gin)
     gg_s[...] = jnp.broadcast_to(jnp.sum(dn * z, axis=0, keepdims=True), gg_s.shape)
     for c in range(shards):
         d_s[0:8, 0:cq] = gg_s[:, c * cq : (c + 1) * cq]
@@ -535,9 +563,14 @@
             (bk_ref, bs_ref)[m & 1][place_b(c ^ mc, m >> 1, shards), feat - split :] = gains
 
 
-def call(kernel, outs, scratch, flops, moved, *args):
+def call(kernel, outs, scratch, flops, moved, *args, on_chip=False, leave=()):
     smem = pl.BlockSpec(memory_space=pltpu.SMEM)
     vmem = pl.BlockSpec(memory_space=pltpu.VMEM)
+    if on_chip:
+        args = args[:1] + tuple(pltpu.with_memory_space_constraint(a, pltpu.VMEM) for a in args[1:])
+        outs = [
+            o if n in leave else pltpu.VMEM(o.shape, o.dtype) for n, o in enumerate(outs)
+        ]
     return pl.pallas_call(
         kernel,
         out_shape=outs,
@@ -545,7 +578,7 @@
         out_specs=[vmem] * len(outs),
         scratch_shapes=scratch,
         cost_estimate=pl.CostEstimate(flops=flops, bytes_accessed=moved, transcendentals=0),
-        compiler_params=pltpu.CompilerParams(vmem_limit_bytes=VMEM_BYTES),
+        compiler_params=pltpu.CompilerParams(vmem_limit_bytes=CHIP_BYTES if on_chip else VMEM_BYTES),
     )(*args)
 
 
@@ -584,7 +617,7 @@
     gu_own = jnp.concatenate(fill([w_gate, w_up], cgl), 1)
     dt_own = w_down.T
     packed = cgl == ffr and cq % 8 == 0
-    ffn_split = 112
+    ffn_split = feat
     if packed:
         ffn = Gather(jnp.concatenate([gu_own, dt_own], 0), ffn_split, shards)
     else:
@@ -615,22 +648,29 @@
 
     kvl = 2 * KEY_VALUE_HEADS * HEAD_DIM
     hrows = QUERY_HEADS * rows
-    qp, kv, a_nat, gains = call(
+    qp, kv, gains = call(
         functools.partial(qkv_kernel, (shards, fsdp, cq, ck, split, feat)),
         [
             arr((hrows, 128), BF16), arr((rows, kvl), BF16),
-            arr((shards, width, lanes), BF16), arr((8, 1280), F32),
+            arr((8, 1280), F32),
         ],
-        [pltpu.VMEM((rows, 640), F32), pltpu.VMEM((rows, kvl), F32), pltpu.VMEM((rows, width), F32)],
+        [
+            pltpu.VMEM((rows, 640), F32), pltpu.VMEM((rows, kvl), F32),
+            pltpu.VMEM((rows, width), F32),
+        ],
         2 * rows * width * 128 * shards, 6_000_000,
-        meta, x, *attn_in, cos_t, sin_t,
-    )
-    gain_first, gain_second = gains[:, :640], gains[:, 640:]
-
-    kv_near = join(gather_outer(kv[None], shards))
-    kv_far = swap(kv_near, "ctx", 1)
+        meta, x, *attn_in, cos_t, sin_t, on_chip=packed,
+    )
+
+    kv_pieces = gather_outer(kv[None], shards)
+    kv_near = join(kv_pieces)
     if packed:
-        ffn.third(kv)
+        cut = kv_near.shape[0] * 3 // 4
+        kv_far = [swap(kv_near[:cut], "ctx", 1), swap(kv_near[cut:], "ctx", 1)]
+        ffn.third(kv_pieces[1])
+        ffn_in = ffn.cores_apart(kv_far[0])
+    else:
+        kv_far = [swap(kv_near, "ctx", 1)]
     chunks = min(8, shards)
     span = GROUP * rows
     att, ot, lse = call(
@@ -638,29 +678,27 @@
         [arr((rows, width), BF16), arr((KEY_VALUE_HEADS, 128, span), F32), arr((8, span), F32)],
         [pltpu.VMEM((8, span), F32), pltpu.VMEM((8, span), F32)],
         4 * hrows * shards * rows * 128, 3_000_000,
-        meta, qp, kv_near, kv_far,
-    )
-
-    if packed:
-        ffn_in = ffn.cores(kv_near)
+        meta, qp, kv_near, *kv_far, on_chip=packed,
+    )
+
     glanes = cgl
     tiles = ffr // glanes
-    parts = [arr((2 * shards, ffn_split, glanes), BF16)] * 2
-    parts += [arr((2 * shards, feat + tiles * cq - ffn_split, glanes), BF16)] * 2
+    parts = [arr((2 * shards, feat, glanes), BF16)] * 2
+    parts += [arr((2 * shards, tiles * cq, glanes), BF16)] * 2
     out, *g_ffn, dmid, ggain, gp = call(
         functools.partial(
-            ffn_kernel, (shards, fsdp, cq, cg, feat, ffr, ffn_split, packed)
+            ffn_kernel, (shards, fsdp, cq, cg, feat, ffr, ffn_split, feat, packed, split)
         ),
-        [arr((rows, width), BF16), *parts]
+        [arr((width, rows), BF16), *parts]
         + [arr((rows, width), F32), arr((8, width), F32), arr((hrows, 128), BF16)],
         [
             pltpu.VMEM((shards, rows, cgl), F32), pltpu.VMEM((rows, ff), F32),
             pltpu.VMEM((rows, ff), F32), pltpu.VMEM((rows, cgl), F32), pltpu.VMEM((rows, 768), F32),
-            pltpu.VMEM((rows, width), F32), pltpu.VMEM((shards, width, cgl) if packed else (1, 16, 128), BF16),
-            pltpu.VMEM((fsdp, width, ffr), BF16),
+            pltpu.VMEM((rows, width), F32), pltpu.VMEM((fsdp, width, ffr), BF16),
         ],
         18 * rows * width * ff, 14_000_000,
-        meta, att, x, dy, a_nat if packed else a_nat[:, :, 128:], gain_second, *ffn_in,
+        meta, att, x, dy.T, gains, *ffn_in, *(attn_in if packed else [p[:, :, 128:] for p in attn_in]),
+        on_chip=packed, leave=(0,),
     )
     ffn_sum = Scatter(*g_ffn, shards)
     ffn_sum.second()
@@ -670,7 +708,7 @@
         [arr((rows, width), BF16)] + [arr((shards // 2, rows, kvl), BF16)] * 2,
         [pltpu.VMEM((hrows, 128), F32)],
         10 * hrows * shards * rows * 128, 5_000_000,
-        meta, qp, gp, kv_near, kv_far, ot, lse, cos_t, sin_t,
+        meta, qp, gp, ot, lse, cos_t, sin_t, kv_near, *kv_far, on_chip=packed,
     )
     dkv_far = after(dkv_far, *ffn_sum.out)
     dkv_terms = scatter_outer(add_low(dkv_near, swap(dkv_far, "ctx", 1)), shards)
@@ -679,7 +717,7 @@
 
     grad_input, *g_attn = call(
         functools.partial(qkv_back_kernel, (shards, fsdp, cq, ck, split, feat)),
-        [arr((rows, width), F32)]
+        [arr((width, rows), F32)]
         + [arr((2 * shards, split, lanes), BF16)] * 2
         + [arr((2 * shards, feat + 8 - split, lanes), BF16)] * 2,
         [
@@ -688,7 +726,8 @@
             pltpu.VMEM((8, width), F32),
         ],
         6 * rows * width * 256 * shards, 6_000_000,
-        meta, x, dq, dkv, att, dmid, a_nat, gain_first, ggain, cos_t, sin_t,
+        meta, x, dq, dkv, att, dmid, gains, ggain, cos_t, sin_t, *attn_in,
+        on_chip=packed, leave=(0,),
     )
     attn_sum = Scatter(*g_attn, shards, ffn_sum.got_a, ffn_sum.got_b)
     ffn_sum.outer()
@@ -698,8 +737,8 @@
     attn_sum.outer()
     attn_own = attn_sum.total()
     return (
-        out[None],
-        grad_input[None],
+        out.T[None],
+        grad_input.T[None],
         attn_own[feat, :cq],
         attn_own[:feat, :cq],
         attn_own[:feat, cq : cq + ck],

time: 177 us -> 160 us (0.904)
  Pallas kernels: 33.7 us -> 20.6 us
  local copies, waits for them, and re-layouts: 16.2 us -> 8.53 us
  waiting for transfers between devices: 66.9 us -> 71.6 us
    pallas_call x5, Pallas kernels: 33.7 us -> 20.6 us  [call(): pl.pallas_call(kernel, out_shape=outs, in_specs=[smem] + [vmem] * (len(ar...]
    unnamed x77 -> x31, local copies, waits for them, and re-layouts: 11.4 us -> 4.43 us
    ppermute x44 -> x46, waiting for transfers between devices: 66.9 us -> 71.6 us  [swap(): return lax.ppermute(x, axis, [(i, i ^ mask) for i in range(size)])]
    ppermute x44 -> x46, starting transfers between devices: 49.9 us -> 50.3 us  [swap(): return lax.ppermute(x, axis, [(i, i ^ mask) for i in range(size)])]
  transfers between devices with their start and end apart: 44 -> 46, of which waited for: 20 -> 25; matrix products, arithmetic and copies ran while one was open for 8% -> 5% of each run, Pallas kernels for 12% -> 8%
where the time goes in v3:
time: 160 us
  waiting for transfers between devices  71.6 us (45%)
  starting transfers between devices  50.3 us (31%)
  Pallas kernels  20.6 us (13%)
  local copies, waits for them, and re-layouts  8.53 us (5%)
  other arithmetic  5.94 us (4%)
  between operations  2.62 us (2%)
    ppermute x46, waiting for transfers between devices, swap(): return lax.ppermute(x, axis, [(i, i ^ mask) for i in range(size)])  71.6 us
    ppermute x46, starting transfers between devices, swap(): return lax.ppermute(x, axis, [(i, i ^ mask) for i in range(size)])  50.3 us
    pallas_call x5, Pallas kernels, call(): pl.pallas_call(kernel, out_shape=outs, in_specs=[smem] + [vmem] * (len(ar...  20.6 us
    unnamed x31, local copies, waits for them, and re-layouts  4.43 us
  transfers between devices with their start and end apart: 46, of which 25 were waited for; matrix products, arithmetic and copies ran while one was open for 5% of the time, Pallas kernels for 8%

profile of v3, /device:TPU:0, one launch (start us, length us, event | category | flops | bytes accessed | tf_op | source)
XLA Modules:
  0.0 159.7 jit_solution(6195690014562991319)
XLA Ops:
  4.0 5.1 %collective-permute-start.2 = (bf16[1,152,256]{2,1,0:T(8,128)(2,1)S(1)}, bf16[1,152,256]{2,1,0:T(8,128)(2,1)S(1)}, u32[]{:S(2)}, u32[]{:S(2)}) collective-permute-start(bf16[1,152,256]{2,1,0:T(8,128)(2,1)S(1)} %maximum_bitcast_fusion.1), channel_id=1, source_target_pairs={{0,24},{4,28},{8,16},{12,20},{16,8},{20,12},{24,0},{28,4},{1,25},{... | collective-permute-start | bytes 233480 | tf_op jit(solution)/shard_map/ppermute | solution.py:35
  15.8 3.3 %collective-permute-start.7 = (bf16[1,216,384]{2,1,0:T(8,128)(2,1)S(1)}, bf16[1,216,384]{2,1,0:T(8,128)(2,1)S(1)}, u32[]{:S(2)}, u32[]{:S(2)}) collective-permute-start(bf16[1,216,384]{2,1,0:T(8,128)(2,1)S(1)} %maximum_bitcast_fusion), channel_id=1, source_target_pairs={{0,24},{4,28},{8,16},{12,20},{16,8},{20,12},{24,0},{28,4},{1,25},{... | collective-permute-start | bytes 497672 | tf_op jit(solution)/shard_map/ppermute | solution.py:35
  28.9 3.4 %collective-permute-done.6 = bf16[1,216,384]{2,1,0:T(8,128)(2,1)S(1)} collective-permute-done((bf16[1,216,384]{2,1,0:T(8,128)(2,1)S(1)}, bf16[1,216,384]{2,1,0:T(8,128)(2,1)S(1)}, u32[]{:S(2)}, u32[]{:S(2)}) %collective-permute-start.6) | collective-permute-done | bytes 165920 | tf_op jit(solution)/shard_map/ppermute | solution.py:35
  33.7 2.2 %collective-permute-done.4 = bf16[8,80,256]{2,1,0:T(8,128)(2,1)S(1)} collective-permute-done((bf16[8,80,256]{2,1,0:T(8,128)(2,1)S(1)}, bf16[8,80,256]{2,1,0:T(8,128)(2,1)S(1)}, u32[]{:S(2)}, u32[]{:S(2)}) %collective-permute-start.4) | collective-permute-done | bytes 327712 | tf_op jit(solution)/shard_map/ppermute | solution.py:35
  41.0 2.5 %collective-permute-start.14 = (bf16[1,128,384]{2,1,0:T(8,128)(2,1)S(1)}, bf16[1,128,384]{2,1,0:T(8,128)(2,1)S(1)}, u32[]{:S(2)}, u32[]{:S(2)}) collective-permute-start(bf16[1,128,384]{2,1,0:T(8,128)(2,1)S(1)} %bitcast.40), channel_id=1, source_target_pairs={{0,24},{4,28},{8,16},{12,20},{16,8},{20,12},{24,0},{28,4},{1,25},{... | collective-permute-start | bytes 294920 | tf_op jit(solution)/shard_map/ppermute | solution.py:35
  45.1 3.6 %collective-permute-done.17 = bf16[4,144,384]{2,1,0:T(8,128)(2,1)S(1)} collective-permute-done((bf16[4,144,384]{2,1,0:T(8,128)(2,1)S(1)}, bf16[4,144,384]{2,1,0:T(8,128)(2,1)S(1)}, u32[]{:S(2)}, u32[]{:S(2)}) %collective-permute-start.17) | collective-permute-done | bytes 442400 | tf_op jit(solution)/shard_map/ppermute | solution.py:35
  50.3 2.9 %collective-permute-done.13 = bf16[1,128,384]{2,1,0:T(8,128)(2,1)S(1)} collective-permute-done((bf16[1,128,384]{2,1,0:T(8,128)(2,1)S(1)}, bf16[1,128,384]{2,1,0:T(8,128)(2,1)S(1)}, u32[]{:S(2)}, u32[]{:S(2)}) %collective-permute-start.13) | collective-permute-done | bytes 98336 | tf_op jit(solution)/shard_map/ppermute | solution.py:35
  54.9 12.3 %collective-permute-done.15.refs_1_ = bf16[3,128,384]{2,1,0:T(8,128)(2,1)S(1)} collective-permute-done((bf16[3,128,384]{2,1,0:T(8,128)(2,1)S(1)}, bf16[3,128,384]{2,1,0:T(8,128)(2,1)S(1)}, u32[]{:S(2)}, u32[]{:S(2)}) %collective-permute-start.15) | collective-permute-done | bytes 294944 | tf_op jit(solution)/shard_map/ppermute | solution.py:35
  67.4 2.8 %collective-permute-done.18.refs_1_ = bf16[8,144,384]{2,1,0:T(8,128)(2,1)S(1)} collective-permute-done((bf16[8,144,384]{2,1,0:T(8,128)(2,1)S(1)}, bf16[8,144,384]{2,1,0:T(8,128)(2,1)S(1)}, u32[]{:S(2)}, u32[]{:S(2)}) %collective-permute-start.18) | collective-permute-done | bytes 884768 | tf_op jit(solution)/shard_map/ppermute | solution.py:35
  72.0 3.3 %collective-permute-done.16.refs_2_ = bf16[1,128,384]{2,1,0:T(8,128)(2,1)S(1)} collective-permute-done((bf16[1,128,384]{2,1,0:T(8,128)(2,1)S(1)}, bf16[1,128,384]{2,1,0:T(8,128)(2,1)S(1)}, u32[]{:S(2)}, u32[]{:S(2)}) %collective-permute-start.16) | collective-permute-done | bytes 98336 | tf_op jit(solution)/shard_map/ppermute | solution.py:35
  75.4 2.9 %shard_map.204 = (bf16[128,576]{1,0:T(8,128)(2,1)S(1)}, f32[3,128,384]{2,1,0:T(8,128)S(1)}, f32[8,384]{1,0:T(8,128)S(1)}) custom-call(s32[10]{0:T(128)S(1)} %pad_add_fusion.meta, bf16[1152,128]{1,0:T(8,128)(2,1)S(1)} %get-tuple-element.126.qp_ref, bf16[4,128,384]{2,1,0:T(8,128)(2,1)S(1)} %constant_dynamic-update-slice_fusion.16.refs_0_, ...), custom_call_target="tpu_custom_call" | custom-call | flops 603979776 | bytes 3000000 | tf_op jit(solution)/shard_map/pallas_call | solution.py:574
  78.3 7.9 %shard_map.205 = (bf16[576,128]{1,0:T(8,128)(2,1)}, bf16[16,144,384]{2,1,0:T(8,128)(2,1)S(1)}, bf16[16,144,384]{2,1,0:T(8,128)(2,1)S(1)}, bf16[16,72,384]{2,1,0:...) custom-call(s32[10]{0:T(128)S(1)} %pad_add_fusion.meta, ...), custom_call_target="tpu_custom_call" | custom-call | flops 2038431744 | bytes 14000000 | tf_op jit(solution)/shard_map/pallas_call | solution.py:574
  86.8 4.6 %shard_map.206 = (bf16[128,576]{1,0:T(8,128)(2,1)S(1)}, bf16[4,128,384]{2,1,0:T(8,128)(2,1)S(1)}, bf16[4,128,384]{2,1,0:T(8,128)(2,1)S(1)}) custom-call(s32[10]{0:T(128)S(1)} %pad_add_fusion.meta, bf16[1152,128]{1,0:T(8,128)(2,1)S(1)} %get-tuple-element.126.qp_ref, bf16[1152,128]{1,0:T(8,128)(2,1)S(1)} %get-tuple-element.151.gp_ref, ...), custom_call_target="tpu_custom_call" | custom-call | flops 1509949440 | bytes 5000000 | tf_op jit(solution)/shard_map/pallas_call | solution.py:574
  95.1 10.0 %collective-permute-done.26 = bf16[4,128,384]{2,1,0:T(8,128)(2,1)S(1)} collective-permute-done((bf16[4,128,384]{2,1,0:T(8,128)(2,1)S(1)}, bf16[4,128,384]{2,1,0:T(8,128)(2,1)S(1)}, u32[]{:S(2)}, u32[]{:S(2)}) %collective-permute-start.26) | collective-permute-done | bytes 393248 | tf_op jit(solution)/shard_map/ppermute | solution.py:35
  105.2 3.6 %collective-permute-start.29 = (bf16[1,128,384]{2,1,0:T(8,128)(2,1)S(1)}, bf16[1,128,384]{2,1,0:T(8,128)(2,1)S(1)}, u32[]{:S(2)}, u32[]{:S(2)}) collective-permute-start(bf16[1,128,384]{2,1,0:T(8,128)(2,1)S(1)} %get-tuple-element.249), channel_id=1, source_target_pairs={{0,24},{4,28},{8,16},{12,20},{16,8},{20,12},{24,0},{28,4},{1,25},{... | collective-permute-start | bytes 294920 | tf_op jit(solution)/shard_map/ppermute | solution.py:35
  109.7 3.6 %collective-permute-done.31 = bf16[8,72,384]{2,1,0:T(8,128)(2,1)S(1)} collective-permute-done((bf16[8,72,384]{2,1,0:T(8,128)(2,1)S(1)}, bf16[8,72,384]{2,1,0:T(8,128)(2,1)S(1)}, u32[]{:S(2)}, u32[]{:S(2)}) %collective-permute-start.31) | collective-permute-done | bytes 442400 | tf_op jit(solution)/shard_map/ppermute | solution.py:35
  116.3 3.5 %shard_map.207 = (f32[576,128]{1,0:T(8,128)}, bf16[16,80,256]{2,1,0:T(8,128)(2,1)S(1)}, bf16[16,80,256]{2,1,0:T(8,128)(2,1)S(1)}, bf16[16,72,256]{2,1,0:T(8,128)(2,1)S(1)}, bf16[16,72,256]{2,1,0:T(8,128)(2,1)S(1)}) custom-call(s32[10]{0:T(128)S(1)} %pad_add_fusion.meta, bf16[128,576]{1,0:T(8,128)(2,1)S(1)} %bitcast.38, ...), custom_call_target="tpu_custom_call" | custom-call | flops 905969664 | bytes 6000000 | tf_op jit(solution)/shard_map/pallas_call | solution.py:574
  121.5 3.5 %collective-permute-done.32 = bf16[4,144,384]{2,1,0:T(8,128)(2,1)S(1)} collective-permute-done((bf16[4,144,384]{2,1,0:T(8,128)(2,1)S(1)}, bf16[4,144,384]{2,1,0:T(8,128)(2,1)S(1)}, u32[]{:S(2)}, u32[]{:S(2)}) %collective-permute-start.32) | collective-permute-done | bytes 442400 | tf_op jit(solution)/shard_map/ppermute | solution.py:35
  125.6 2.3 %collective-permute-done.35 = bf16[16,72,256]{2,1,0:T(8,128)(2,1)S(1)} collective-permute-done((bf16[16,72,256]{2,1,0:T(8,128)(2,1)S(1)}, bf16[16,72,256]{2,1,0:T(8,128)(2,1)S(1)}, u32[]{:S(2)}, u32[]{:S(2)}) %collective-permute-start.35) | collective-permute-done | bytes 589856 | tf_op jit(solution)/shard_map/ppermute | solution.py:35
  130.6 3.8 %collective-permute-start.45 = (bf16[1,216,384]{2,1,0:T(8,128)(2,1)S(1)}, bf16[1,216,384]{2,1,0:T(8,128)(2,1)S(1)}, u32[]{:S(2)}, u32[]{:S(2)}) collective-permute-start(bf16[1,216,384]{2,1,0:T(8,128)(2,1)S(1)} %get-tuple-element.241), channel_id=1, source_target_pairs={{0,24},{4,28},{8,16},{12,20},{16,8},{20,12},{24,0},{28,4},{1,25},{... | collective-permute-start | bytes 497672 | tf_op jit(solution)/shard_map/ppermute | solution.py:35
  135.1 2.9 %collective-permute-done.37 = bf16[8,72,256]{2,1,0:T(8,128)(2,1)S(1)} collective-permute-done((bf16[8,72,256]{2,1,0:T(8,128)(2,1)S(1)}, bf16[8,72,256]{2,1,0:T(8,128)(2,1)S(1)}, u32[]{:S(2)}, u32[]{:S(2)}) %collective-permute-start.37) | collective-permute-done | bytes 294944 | tf_op jit(solution)/shard_map/ppermute | solution.py:35
  140.8 2.9 %collective-permute-done.43 = bf16[1,216,384]{2,1,0:T(8,128)(2,1)S(1)} collective-permute-done((bf16[1,216,384]{2,1,0:T(8,128)(2,1)S(1)}, bf16[1,216,384]{2,1,0:T(8,128)(2,1)S(1)}, u32[]{:S(2)}, u32[]{:S(2)}) %collective-permute-start.43) | collective-permute-done | bytes 165920 | tf_op jit(solution)/shard_map/ppermute | solution.py:35
  143.7 4.0 %collective-permute-done.44 = bf16[1,216,384]{2,1,0:T(8,128)(2,1)S(1)} collective-permute-done((bf16[1,216,384]{2,1,0:T(8,128)(2,1)S(1)}, bf16[1,216,384]{2,1,0:T(8,128)(2,1)S(1)}, u32[]{:S(2)}, u32[]{:S(2)}) %collective-permute-start.44) | collective-permute-done | bytes 165920 | tf_op jit(solution)/shard_map/ppermute | solution.py:35
  148.7 2.4 %collective-permute-start.42 = (bf16[1,152,256]{2,1,0:T(8,128)(2,1)S(1)}, bf16[1,152,256]{2,1,0:T(8,128)(2,1)S(1)}, u32[]{:S(2)}, u32[]{:S(2)}) collective-permute-start(bf16[1,152,256]{2,1,0:T(8,128)(2,1)S(1)} %get-tuple-element.255), channel_id=1, source_target_pairs={{0,24},{4,28},{8,16},{12,20},{16,8},{20,12},{24,0},{28,4},{1,25},{... | collective-permute-start | bytes 233480 | tf_op jit(solution)/shard_map/ppermute | solution.py:35
  (173 shorter events, 57.7 us)
Async XLA Ops:
  4.0 11.1 %collective-permute-start.2 = (bf16[1,152,256]{2,1,0:T(8,128)(2,1)S(1)}, bf16[1,152,256]{2,1,0:T(8,128)(2,1)S(1)}, u32[]{:S(2)}, u32[]{:S(2)}) collective-permute-start(bf16[1,152,256]{2,1,0:T(8,128)(2,1)S(1)} %maximum_bitcast_fusion.1), channel_id=1, source_target_pairs={{0,24},{4,28},{8,16},{12,20},{16,8},{20,12},{24,0},{28,4},{1,25},{... | collective-permute-start | bytes 233480 | tf_op jit(solution)/shard_map/ppermute | solution.py:35
  15.8 13.1 %collective-permute-start.7 = (bf16[1,216,384]{2,1,0:T(8,128)(2,1)S(1)}, bf16[1,216,384]{2,1,0:T(8,128)(2,1)S(1)}, u32[]{:S(2)}, u32[]{:S(2)}) collective-permute-start(bf16[1,216,384]{2,1,0:T(8,128)(2,1)S(1)} %maximum_bitcast_fusion), channel_id=1, source_target_pairs={{0,24},{4,28},{8,16},{12,20},{16,8},{20,12},{24,0},{28,4},{1,25},{... | collective-permute-start | bytes 497672 | tf_op jit(solution)/shard_map/ppermute | solution.py:35
  19.1 13.2 %collective-permute-start.6 = (bf16[1,216,384]{2,1,0:T(8,128)(2,1)S(1)}, bf16[1,216,384]{2,1,0:T(8,128)(2,1)S(1)}, u32[]{:S(2)}, u32[]{:S(2)}) collective-permute-start(bf16[1,216,384]{2,1,0:T(8,128)(2,1)S(1)} %maximum_bitcast_fusion), channel_id=1, source_target_pairs={{0,16},{4,20},{8,24},{12,28},{16,0},{20,4},{24,8},{28,12},{1,17},{... | collective-permute-start | bytes 497672 | tf_op jit(solution)/shard_map/ppermute | solution.py:35
  19.1 13.2 %collective-permute-start.5 = (bf16[1,216,384]{2,1,0:T(8,128)(2,1)S(1)}, bf16[1,216,384]{2,1,0:T(8,128)(2,1)S(1)}, u32[]{:S(2)}, u32[]{:S(2)}) collective-permute-start(bf16[1,216,384]{2,1,0:T(8,128)(2,1)S(1)} %maximum_bitcast_fusion), channel_id=1, source_target_pairs={{0,8},{4,12},{8,0},{12,4},{16,24},{20,28},{24,16},{28,20},{1,9},{5... | collective-permute-start | bytes 497672 | tf_op jit(solution)/shard_map/ppermute | solution.py:35
  36.1 12.6 %collective-permute-start.17 = (bf16[4,144,384]{2,1,0:T(8,128)(2,1)S(1)}, bf16[4,144,384]{2,1,0:T(8,128)(2,1)S(1)}, u32[]{:S(2)}, u32[]{:S(2)}) collective-permute-start(bf16[4,144,384]{2,1,0:T(8,128)(2,1)S(1)} %constant_dynamic-update-slice_fusion.20), channel_id=1, source_target_pairs={{0,4},{4,0},{8,12},{12,8},{16,20},{20,16},{24,28},{28,24},{1,5},{5... | collective-permute-start | bytes 1327112 | tf_op jit(solution)/shard_map/ppermute | solution.py:35
  41.0 9.4 %collective-permute-start.14 = (bf16[1,128,384]{2,1,0:T(8,128)(2,1)S(1)}, bf16[1,128,384]{2,1,0:T(8,128)(2,1)S(1)}, u32[]{:S(2)}, u32[]{:S(2)}) collective-permute-start(bf16[1,128,384]{2,1,0:T(8,128)(2,1)S(1)} %bitcast.40), channel_id=1, source_target_pairs={{0,24},{4,28},{8,16},{12,20},{16,8},{20,12},{24,0},{28,4},{1,25},{... | collective-permute-start | bytes 294920 | tf_op jit(solution)/shard_map/ppermute | solution.py:35
  43.5 9.8 %collective-permute-start.13 = (bf16[1,128,384]{2,1,0:T(8,128)(2,1)S(1)}, bf16[1,128,384]{2,1,0:T(8,128)(2,1)S(1)}, u32[]{:S(2)}, u32[]{:S(2)}) collective-permute-start(bf16[1,128,384]{2,1,0:T(8,128)(2,1)S(1)} %bitcast.41), channel_id=1, source_target_pairs={{0,16},{4,20},{8,24},{12,28},{16,0},{20,4},{24,8},{28,12},{1,17},{... | collective-permute-start | bytes 294920 | tf_op jit(solution)/shard_map/ppermute | solution.py:35
  48.8 21.3 %collective-permute-start.18 = (bf16[8,144,384]{2,1,0:T(8,128)(2,1)S(1)}, bf16[8,144,384]{2,1,0:T(8,128)(2,1)S(1)}, u32[]{:S(2)}, u32[]{:S(2)}) collective-permute-start(bf16[8,144,384]{2,1,0:T(8,128)(2,1)S(1)} %constant_dynamic-update-slice_fusion.24.refs_0_), channel_id=1, source_target_pairs={{0,2},{1,3},{2,0},{3,1},{4,6},{5,7},{6,4},{7,5},{8,10},{9,11},{10,... | collective-permute-start | bytes 2654216 | tf_op jit(solution)/shard_map/ppermute | solution.py:35
  49.0 18.2 %collective-permute-start.22 = (bf16[8,72,384]{2,1,0:T(8,128)(2,1)S(1)}, bf16[8,72,384]{2,1,0:T(8,128)(2,1)S(1)}, u32[]{:S(2)}, u32[]{:S(2)}) collective-permute-start(bf16[8,72,384]{2,1,0:T(8,128)(2,1)S(1)} %constant_dynamic-update-slice_fusion.30), channel_id=1, source_target_pairs={{0,4},{4,0},{8,12},{12,8},{16,20},{20,16},{24,28},{28,24},{1,5},{5... | collective-permute-start | bytes 1327112 | tf_op jit(solution)/shard_map/ppermute | solution.py:35
  53.3 13.8 %collective-permute-start.15 = (bf16[3,128,384]{2,1,0:T(8,128)(2,1)S(1)}, bf16[3,128,384]{2,1,0:T(8,128)(2,1)S(1)}, u32[]{:S(2)}, u32[]{:S(2)}) collective-permute-start(bf16[3,128,384]{2,1,0:T(8,128)(2,1)S(1)} %pad_maximum_fusion), channel_id=1, source_target_pairs={{0,4},{4,0},{8,12},{12,8},{16,20},{20,16},{24,28},{28,24},{1,5},{5... | collective-permute-start | bytes 884744 | tf_op jit(solution)/shard_map/ppermute | solution.py:35
  67.3 11.0 %collective-permute-start.23 = (bf16[16,72,384]{2,1,0:T(8,128)(2,1)S(1)}, bf16[16,72,384]{2,1,0:T(8,128)(2,1)S(1)}, u32[]{:S(2)}, u32[]{:S(2)}) collective-permute-start(bf16[16,72,384]{2,1,0:T(8,128)(2,1)S(1)} %constant_dynamic-update-slice_fusion.32.refs_4_), channel_id=1, source_target_pairs={{0,1},{1,0},{2,3},{3,2},{4,5},{5,4},{6,7},{7,6},{8,9},{9,8},{10,11... | collective-permute-start | bytes 2654216 | tf_op jit(solution)/shard_map/ppermute | solution.py:35
  70.1 8.2 %collective-permute-start.20 = (bf16[8,144,384]{2,1,0:T(8,128)(2,1)S(1)}, bf16[8,144,384]{2,1,0:T(8,128)(2,1)S(1)}, u32[]{:S(2)}, u32[]{:S(2)}) collective-permute-start(bf16[8,144,384]{2,1,0:T(8,128)(2,1)S(1)} %collective-permute-done.18.refs_1_), channel_id=1, source_target_pairs={{0,1},{1,0},{2,3},{3,2},{4,5},{5,4},{6,7},{7,6},{8,9},{9,8},{10,11... | collective-permute-start | bytes 2654216 | tf_op jit(solution)/shard_map/ppermute | solution.py:35
  91.9 21.6 %collective-permute-start.30 = (bf16[8,144,384]{2,1,0:T(8,128)(2,1)S(1)}, bf16[8,144,384]{2,1,0:T(8,128)(2,1)S(1)}, u32[]{:S(2)}, u32[]{:S(2)}) collective-permute-start(bf16[8,144,384]{2,1,0:T(8,128)(2,1)S(1)} %get-tuple-element.230), channel_id=1, source_target_pairs={{0,2},{1,3},{2,0},{3,1},{4,6},{5,7},{6,4},{7,5},{8,10},{9,11},{10,... | collective-permute-start | bytes 2654216 | tf_op jit(solution)/shard_map/ppermute | solution.py:35
  93.0 12.1 %collective-permute-start.26 = (bf16[4,128,384]{2,1,0:T(8,128)(2,1)S(1)}, bf16[4,128,384]{2,1,0:T(8,128)(2,1)S(1)}, u32[]{:S(2)}, u32[]{:S(2)}) collective-permute-start(bf16[4,128,384]{2,1,0:T(8,128)(2,1)S(1)} %get-tuple-element.165), channel_id=1, source_target_pairs={{0,4},{4,0},{8,12},{12,8},{16,20},{20,16},{24,28},{28,24},{1,5},{5... | collective-permute-start | bytes 1179656 | tf_op jit(solution)/shard_map/ppermute | solution.py:35
  94.3 18.9 %collective-permute-start.31 = (bf16[8,72,384]{2,1,0:T(8,128)(2,1)S(1)}, bf16[8,72,384]{2,1,0:T(8,128)(2,1)S(1)}, u32[]{:S(2)}, u32[]{:S(2)}) collective-permute-start(bf16[8,72,384]{2,1,0:T(8,128)(2,1)S(1)} %get-tuple-element.234), channel_id=1, source_target_pairs={{0,4},{4,0},{8,12},{12,8},{16,20},{20,16},{24,28},{28,24},{1,5},{5... | collective-permute-start | bytes 1327112 | tf_op jit(solution)/shard_map/ppermute | solution.py:35
  105.2 11.1 %collective-permute-start.29 = (bf16[1,128,384]{2,1,0:T(8,128)(2,1)S(1)}, bf16[1,128,384]{2,1,0:T(8,128)(2,1)S(1)}, u32[]{:S(2)}, u32[]{:S(2)}) collective-permute-start(bf16[1,128,384]{2,1,0:T(8,128)(2,1)S(1)} %get-tuple-element.249), channel_id=1, source_target_pairs={{0,24},{4,28},{8,16},{12,20},{16,8},{20,12},{24,0},{28,4},{1,25},{... | collective-permute-start | bytes 294920 | tf_op jit(solution)/shard_map/ppermute | solution.py:35
  113.7 11.3 %collective-permute-start.32 = (bf16[4,144,384]{2,1,0:T(8,128)(2,1)S(1)}, bf16[4,144,384]{2,1,0:T(8,128)(2,1)S(1)}, u32[]{:S(2)}, u32[]{:S(2)}) collective-permute-start(bf16[4,144,384]{2,1,0:T(8,128)(2,1)S(1)} %get-tuple-element.232), channel_id=1, source_target_pairs={{0,4},{4,0},{8,12},{12,8},{16,20},{20,16},{24,28},{28,24},{1,5},{5... | collective-permute-start | bytes 1327112 | tf_op jit(solution)/shard_map/ppermute | solution.py:35
  128.1 9.9 %collective-permute-start.36 = (bf16[8,80,256]{2,1,0:T(8,128)(2,1)S(1)}, bf16[8,80,256]{2,1,0:T(8,128)(2,1)S(1)}, u32[]{:S(2)}, u32[]{:S(2)}) collective-permute-start(bf16[8,80,256]{2,1,0:T(8,128)(2,1)S(1)} %get-tuple-element.235), channel_id=1, source_target_pairs={{0,2},{1,3},{2,0},{3,1},{4,6},{5,7},{6,4},{7,5},{8,10},{9,11},{10,... | collective-permute-start | bytes 983048 | tf_op jit(solution)/shard_map/ppermute | solution.py:35
  129.1 8.8 %collective-permute-start.37 = (bf16[8,72,256]{2,1,0:T(8,128)(2,1)S(1)}, bf16[8,72,256]{2,1,0:T(8,128)(2,1)S(1)}, u32[]{:S(2)}, u32[]{:S(2)}) collective-permute-start(bf16[8,72,256]{2,1,0:T(8,128)(2,1)S(1)} %get-tuple-element.237), channel_id=1, source_target_pairs={{0,4},{4,0},{8,12},{12,8},{16,20},{20,16},{24,28},{28,24},{1,5},{5... | collective-permute-start | bytes 884744 | tf_op jit(solution)/shard_map/ppermute | solution.py:35
  130.6 10.1 %collective-permute-start.45 = (bf16[1,216,384]{2,1,0:T(8,128)(2,1)S(1)}, bf16[1,216,384]{2,1,0:T(8,128)(2,1)S(1)}, u32[]{:S(2)}, u32[]{:S(2)}) collective-permute-start(bf16[1,216,384]{2,1,0:T(8,128)(2,1)S(1)} %get-tuple-element.241), channel_id=1, source_target_pairs={{0,24},{4,28},{8,16},{12,20},{16,8},{20,12},{24,0},{28,4},{1,25},{... | collective-permute-start | bytes 497672 | tf_op jit(solution)/shard_map/ppermute | solution.py:35
  134.5 9.2 %collective-permute-start.43 = (bf16[1,216,384]{2,1,0:T(8,128)(2,1)S(1)}, bf16[1,216,384]{2,1,0:T(8,128)(2,1)S(1)}, u32[]{:S(2)}, u32[]{:S(2)}) collective-permute-start(bf16[1,216,384]{2,1,0:T(8,128)(2,1)S(1)} %get-tuple-element.243), channel_id=1, source_target_pairs={{0,8},{4,12},{8,0},{12,4},{16,24},{20,28},{24,16},{28,20},{1,9},{5... | collective-permute-start | bytes 497672 | tf_op jit(solution)/shard_map/ppermute | solution.py:35
  134.5 13.2 %collective-permute-start.44 = (bf16[1,216,384]{2,1,0:T(8,128)(2,1)S(1)}, bf16[1,216,384]{2,1,0:T(8,128)(2,1)S(1)}, u32[]{:S(2)}, u32[]{:S(2)}) collective-permute-start(bf16[1,216,384]{2,1,0:T(8,128)(2,1)S(1)} %get-tuple-element.244), channel_id=1, source_target_pairs={{0,16},{4,20},{8,24},{12,28},{16,0},{20,4},{24,8},{28,12},{1,17},{... | collective-permute-start | bytes 497672 | tf_op jit(solution)/shard_map/ppermute | solution.py:35
  138.1 10.5 %collective-permute-start.38 = (bf16[4,80,256]{2,1,0:T(8,128)(2,1)S(1)}, bf16[4,80,256]{2,1,0:T(8,128)(2,1)S(1)}, u32[]{:S(2)}, u32[]{:S(2)}) collective-permute-start(bf16[4,80,256]{2,1,0:T(8,128)(2,1)S(1)} %get-tuple-element.245), channel_id=1, source_target_pairs={{0,4},{4,0},{8,12},{12,8},{16,20},{20,16},{24,28},{28,24},{1,5},{5... | collective-permute-start | bytes 491528 | tf_op jit(solution)/shard_map/ppermute | solution.py:35
  139.5 9.1 %collective-permute-start.39 = (bf16[4,72,256]{2,1,0:T(8,128)(2,1)S(1)}, bf16[4,72,256]{2,1,0:T(8,128)(2,1)S(1)}, u32[]{:S(2)}, u32[]{:S(2)}) collective-permute-start(bf16[4,72,256]{2,1,0:T(8,128)(2,1)S(1)} %get-tuple-element.247), channel_id=1, source_target_pairs={{0,2},{1,3},{2,0},{3,1},{4,6},{5,7},{6,4},{7,5},{8,10},{9,11},{10,... | collective-permute-start | bytes 442376 | tf_op jit(solution)/shard_map/ppermute | solution.py:35
  (24 other events, 143.7 us)

commit v4 on v3

--- a/solution.py
+++ b/solution.py
@@ -123,9 +123,10 @@
         self.out = add_low(a[size:], got_a[size:]), add_low(b[size:], got_b[size:])
         return self.out
 
-    def second(self, *before):
+    def second(self, *before, late=None):
         a, b = self.fold(self.shards, *before)
-        self.got_a, self.got_b = swap(a, "fsdp", 2), swap(b, "ctx", 1)
+        wait = () if late is None else late(a, b)
+        self.got_a, self.got_b = swap(a, "fsdp", 2), swap(after(b, *wait), "ctx", 1)
 
     def third(self, *before):
         a, b = self.fold(self.shards // 2, *before)
@@ -135,9 +136,8 @@
         a, b, got_a, got_b = lax.optimization_barrier(
             (self.a, self.b, self.got_a, self.got_b, *before)
         )[:4]
-        self.terms = scatter_outer(
-            jnp.concatenate([add_low(a, got_a), add_low(b, got_b)], 1), self.shards
-        )
+        self.last = jnp.concatenate([add_low(a, got_a), add_low(b, got_b)], 1)
+        self.terms = scatter_outer(self.last, self.shards)
 
     def total(self, *before):
         return add_terms(self.terms, *before)[0]
@@ -563,18 +563,45 @@
             (bk_ref, bs_ref)[m & 1][place_b(c ^ mc, m >> 1, shards), feat - split :] = gains
 
 
-def call(kernel, outs, scratch, flops, moved, *args, on_chip=False, leave=()):
+def pack_kernel(wq_ref, wkt_ref, wvt_ref, wo_ref, ga_ref, gf_ref, own_ref, t_s):
+    feat, cq = wq_ref.shape
+    ck = wkt_ref.shape[0]
+    t_s[...] = jnp.zeros_like(t_s)
+    t_s[:feat, :cq] = wq_ref[...].astype(F32)
+    t_s[:feat, cq : cq + ck] = jnp.transpose(wkt_ref[...].astype(F32))
+    t_s[:feat, cq + ck : cq + 2 * ck] = jnp.transpose(wvt_ref[...].astype(F32))
+    t_s[:feat, 128 : 128 + cq] = wo_ref[...].astype(F32)
+    t_s[feat : feat + 1, :cq] = ga_ref[...].astype(F32)
+    t_s[feat : feat + 1, 128 : 128 + cq] = gf_ref[...].astype(F32)
+    own_ref[...] = t_s[...].astype(BF16)
+
+
+def finish_kernel(ck, *refs):
+    *terms, gq_ref, gkt_ref, gvt_ref, go_ref, ga_ref, gf_ref = refs
+    feat, cq = gq_ref.shape
+    total = functools.reduce(lambda a, b: a + b, [t[...].astype(F32) for t in terms])
+    gq_ref[...] = total[:feat, :cq]
+    turned_round = jnp.transpose(total[:feat, :128])
+    gkt_ref[...] = turned_round[cq : cq + ck]
+    gvt_ref[...] = turned_round[cq + ck : cq + 2 * ck]
+    go_ref[...] = total[:feat, 128 : 128 + cq]
+    ga_ref[...] = total[feat : feat + 1, :cq]
+    gf_ref[...] = total[feat : feat + 1, 128 : 128 + cq]
+
+
+def call(kernel, outs, scratch, flops, moved, *args, on_chip=False, leave=(), scalars=1):
     smem = pl.BlockSpec(memory_space=pltpu.SMEM)
     vmem = pl.BlockSpec(memory_space=pltpu.VMEM)
     if on_chip:
-        args = args[:1] + tuple(pltpu.with_memory_space_constraint(a, pltpu.VMEM) for a in args[1:])
+        held = [pltpu.with_memory_space_constraint(a, pltpu.VMEM) for a in args[scalars:]]
+        args = (*args[:scalars], *held)
         outs = [
             o if n in leave else pltpu.VMEM(o.shape, o.dtype) for n, o in enumerate(outs)
         ]
     return pl.pallas_call(
         kernel,
         out_shape=outs,
-        in_specs=[smem] + [vmem] * (len(args) - 1),
+        in_specs=[smem] * scalars + [vmem] * (len(args) - scalars),
         out_specs=[vmem] * len(outs),
         scratch_shapes=scratch,
         cost_estimate=pl.CostEstimate(flops=flops, bytes_accessed=moved, transcendentals=0),
@@ -606,11 +633,19 @@
         return parts + [jnp.zeros((parts[0].shape[0], total - used), BF16)]
 
     lanes = 256
-    body = jnp.concatenate(
-        fill([w_query, key_weight, value_weight], 128) + fill([w_out], 128), 1
-    )
-    gains_row = jnp.concatenate(fill([gain_attn[None]], 128) + fill([gain_ffn[None]], 128), 1)
-    own = jnp.concatenate([body, jnp.broadcast_to(gains_row, (8, lanes))], 0)
+    if cq % 8 == 0 and ck % 8 == 0:
+        (own,) = call(
+            pack_kernel, [pltpu.VMEM((feat + 8, lanes), BF16)], [pltpu.VMEM((feat + 8, lanes), F32)],
+            0, 200_000,
+            w_query, key_weight.T, value_weight.T, w_out, gain_attn[None], gain_ffn[None],
+            scalars=0,
+        )
+    else:
+        body = jnp.concatenate(
+            fill([w_query, key_weight, value_weight], 128) + fill([w_out], 128), 1
+        )
+        gains_row = jnp.concatenate(fill([gain_attn[None]], 128) + fill([gain_ffn[None]], 128), 1)
+        own = jnp.concatenate([body, jnp.broadcast_to(gains_row, (8, lanes))], 0)
     split = 80
 
     cgl = round_up(2 * cg, 128)
@@ -701,8 +736,6 @@
         on_chip=packed, leave=(0,),
     )
     ffn_sum = Scatter(*g_ffn, shards)
-    ffn_sum.second()
-
     dq, dkv_near, dkv_far = call(
         functools.partial(attend_back_kernel, (shards, chunks, blk)),
         [arr((rows, width), BF16)] + [arr((shards // 2, rows, kvl), BF16)] * 2,
@@ -710,8 +743,14 @@
         10 * hrows * shards * rows * 128, 5_000_000,
         meta, qp, gp, ot, lse, cos_t, sin_t, kv_near, *kv_far, on_chip=packed,
     )
-    dkv_far = after(dkv_far, *ffn_sum.out)
-    dkv_terms = scatter_outer(add_low(dkv_near, swap(dkv_far, "ctx", 1)), shards)
+    dkv_got = []
+
+    def send_far(*sent):
+        dkv_got.append(swap(after(dkv_far, *sent), "ctx", 1))
+        return dkv_got
+
+    ffn_sum.second(late=send_far)
+    dkv_terms = scatter_outer(add_low(dkv_near, dkv_got[0]), shards)
     ffn_sum.third()
     dkv = add_terms(dkv_terms, *ffn_sum.out)[0]
 
@@ -729,25 +768,34 @@
         meta, x, dq, dkv, att, dmid, gains, ggain, cos_t, sin_t, *attn_in,
         on_chip=packed, leave=(0,),
     )
-    attn_sum = Scatter(*g_attn, shards, ffn_sum.got_a, ffn_sum.got_b)
+    attn_sum = Scatter(*g_attn, shards)
+    attn_sum.second(ffn_sum.got_a, ffn_sum.got_b)
     ffn_sum.outer()
-    attn_sum.second()
     attn_sum.third()
-    ffn_own = ffn_sum.total(*attn_sum.out)
     attn_sum.outer()
-    attn_own = attn_sum.total()
+    ffn_own = ffn_sum.total(attn_sum.last)
+    if packed:
+        gq, gkt, gvt, go, gain_a, gain_f = call(
+            functools.partial(finish_kernel, ck),
+            [arr((feat, cq), F32)] + [arr((ck, feat), F32)] * 2
+            + [arr((feat, cq), F32)] + [arr((1, cq), F32)] * 2,
+            [], 0, 400_000, *[t[0] for t in attn_sum.terms],
+            on_chip=True, leave=range(6), scalars=0,
+        )
+        attn_grads = gq, gkt.T, gvt.T, go
+        gain_grads = gain_a[0], gain_f[0]
+    else:
+        attn_own = attn_sum.total()
+        attn_grads = (
+            attn_own[:feat, :cq], attn_own[:feat, cq : cq + ck],
+            attn_own[:feat, cq + ck : cq + 2 * ck], attn_own[:feat, 128 : 128 + cq],
+        )
+        gain_grads = attn_own[feat, :cq], attn_own[feat, 128 : 128 + cq]
+    down_rows = ffn_own[feat:]
+    grad_down = jnp.concatenate([down_rows[t * cq : (t + 1) * cq] for t in range(tiles)], 1).T
     return (
-        out.T[None],
-        grad_input.T[None],
-        attn_own[feat, :cq],
-        attn_own[:feat, :cq],
-        attn_own[:feat, cq : cq + ck],
-        attn_own[:feat, cq + ck : cq + 2 * ck],
-        attn_own[:feat, 128 : 128 + cq],
-        attn_own[feat, 128 : 128 + cq],
-        ffn_own[:feat, :cg],
-        ffn_own[:feat, cg : 2 * cg],
-        jnp.concatenate([ffn_own[feat + t * cq : feat + (t + 1) * cq] for t in range(tiles)], 1).T,
+        out.T[None], grad_input.T[None], gain_grads[0], *attn_grads, gain_grads[1],
+        ffn_own[:feat, :cg], ffn_own[:feat, cg : 2 * cg], grad_down,
     )
 
 

time: 160 us -> 154 us (0.963)
  local copies, waits for them, and re-layouts: 8.53 us -> 3.31 us
  waiting for transfers between devices: 71.6 us -> 68.5 us
  Pallas kernels: 20.6 us -> 22.3 us
    ppermute x46, waiting for transfers between devices: 71.6 us -> 68.5 us  [swap(): return lax.ppermute(x, axis, [(i, i ^ mask) for i in range(size)])]
    unnamed x31 -> x27, local copies, waits for them, and re-layouts: 4.43 us -> 1.41 us
    pallas_call x5 -> x7, Pallas kernels: 20.6 us -> 22.3 us  [call(): pl.pallas_call(kernel, out_shape=outs, in_specs=[smem] * scalars + [vmem]...]
  transfers between devices with their start and end apart: 46 -> 46, of which waited for: 25 -> 24; matrix products, arithmetic and copies ran while one was open for 5% -> 5% of each run, Pallas kernels for 8% -> 8%
where the time goes in v4:
time: 154 us
  waiting for transfers between devices  68.5 us (44%)
  starting transfers between devices  51.7 us (34%)
  Pallas kernels  22.3 us (14%)
  other arithmetic  5.15 us (3%)
  local copies, waits for them, and re-layouts  3.31 us (2%)
  between operations  2.6 us (2%)
    ppermute x46, waiting for transfers between devices, swap(): return lax.ppermute(x, axis, [(i, i ^ mask) for i in range(size)])  68.5 us
    ppermute x46, starting transfers between devices, swap(): return lax.ppermute(x, axis, [(i, i ^ mask) for i in range(size)])  51.7 us
    pallas_call x7, Pallas kernels, call(): pl.pallas_call(kernel, out_shape=outs, in_specs=[smem] * scalars + [vmem]...  22.3 us
  transfers between devices with their start and end apart: 46, of which 24 were waited for; matrix products, arithmetic and copies ran while one was open for 5% of the time, Pallas kernels for 8%

profile of v4, /device:TPU:0, one launch (start us, length us, event | category | flops | bytes accessed | tf_op | source)
XLA Modules:
  0.0 153.6 jit_solution(8851808105985224643)
XLA Ops:
  1.6 5.1 %collective-permute-start.2 = (bf16[1,152,256]{2,1,0:T(8,128)(2,1)S(1)}, bf16[1,152,256]{2,1,0:T(8,128)(2,1)S(1)}, u32[]{:S(2)}, u32[]{:S(2)}) collective-permute-start(bf16[1,152,256]{2,1,0:T(8,128)(2,1)S(1)} %bitcast.48), channel_id=1, source_target_pairs={{0,24},{4,28},{8,16},{12,20},{16,8},{20,12},{24,0},{28,4},{1,25},{... | collective-permute-start | bytes 233480 | tf_op jit(solution)/shard_map/ppermute | solution.py:35
  13.4 3.3 %collective-permute-start.7 = (bf16[1,216,384]{2,1,0:T(8,128)(2,1)S(1)}, bf16[1,216,384]{2,1,0:T(8,128)(2,1)S(1)}, u32[]{:S(2)}, u32[]{:S(2)}) collective-permute-start(bf16[1,216,384]{2,1,0:T(8,128)(2,1)S(1)} %maximum_bitcast_fusion), channel_id=1, source_target_pairs={{0,24},{4,28},{8,16},{12,20},{16,8},{20,12},{24,0},{28,4},{1,25},{... | collective-permute-start | bytes 497672 | tf_op jit(solution)/shard_map/ppermute | solution.py:35
  21.0 2.0 %collective-permute-done.9 = bf16[4,72,256]{2,1,0:T(8,128)(2,1)S(1)} collective-permute-done((bf16[4,72,256]{2,1,0:T(8,128)(2,1)S(1)}, bf16[4,72,256]{2,1,0:T(8,128)(2,1)S(1)}, u32[]{:S(2)}, u32[]{:S(2)}) %collective-permute-start.9) | collective-permute-done | bytes 147488 | tf_op jit(solution)/shard_map/ppermute | solution.py:35
  26.5 3.4 %collective-permute-done.6 = bf16[1,216,384]{2,1,0:T(8,128)(2,1)S(1)} collective-permute-done((bf16[1,216,384]{2,1,0:T(8,128)(2,1)S(1)}, bf16[1,216,384]{2,1,0:T(8,128)(2,1)S(1)}, u32[]{:S(2)}, u32[]{:S(2)}) %collective-permute-start.6) | collective-permute-done | bytes 165920 | tf_op jit(solution)/shard_map/ppermute | solution.py:35
  31.3 2.2 %collective-permute-done.4 = bf16[8,80,256]{2,1,0:T(8,128)(2,1)S(1)} collective-permute-done((bf16[8,80,256]{2,1,0:T(8,128)(2,1)S(1)}, bf16[8,80,256]{2,1,0:T(8,128)(2,1)S(1)}, u32[]{:S(2)}, u32[]{:S(2)}) %collective-permute-start.4) | collective-permute-done | bytes 327712 | tf_op jit(solution)/shard_map/ppermute | solution.py:35
  38.6 2.5 %collective-permute-start.14 = (bf16[1,128,384]{2,1,0:T(8,128)(2,1)S(1)}, bf16[1,128,384]{2,1,0:T(8,128)(2,1)S(1)}, u32[]{:S(2)}, u32[]{:S(2)}) collective-permute-start(bf16[1,128,384]{2,1,0:T(8,128)(2,1)S(1)} %bitcast.44), channel_id=1, source_target_pairs={{0,24},{4,28},{8,16},{12,20},{16,8},{20,12},{24,0},{28,4},{1,25},{... | collective-permute-start | bytes 294920 | tf_op jit(solution)/shard_map/ppermute | solution.py:35
  42.7 3.6 %collective-permute-done.17 = bf16[4,144,384]{2,1,0:T(8,128)(2,1)S(1)} collective-permute-done((bf16[4,144,384]{2,1,0:T(8,128)(2,1)S(1)}, bf16[4,144,384]{2,1,0:T(8,128)(2,1)S(1)}, u32[]{:S(2)}, u32[]{:S(2)}) %collective-permute-start.17) | collective-permute-done | bytes 442400 | tf_op jit(solution)/shard_map/ppermute | solution.py:35
  48.0 2.9 %collective-permute-done.13 = bf16[1,128,384]{2,1,0:T(8,128)(2,1)S(1)} collective-permute-done((bf16[1,128,384]{2,1,0:T(8,128)(2,1)S(1)}, bf16[1,128,384]{2,1,0:T(8,128)(2,1)S(1)}, u32[]{:S(2)}, u32[]{:S(2)}) %collective-permute-start.13) | collective-permute-done | bytes 98336 | tf_op jit(solution)/shard_map/ppermute | solution.py:35
  52.5 12.3 %collective-permute-done.15.refs_1_ = bf16[3,128,384]{2,1,0:T(8,128)(2,1)S(1)} collective-permute-done((bf16[3,128,384]{2,1,0:T(8,128)(2,1)S(1)}, bf16[3,128,384]{2,1,0:T(8,128)(2,1)S(1)}, u32[]{:S(2)}, u32[]{:S(2)}) %collective-permute-start.15) | collective-permute-done | bytes 294944 | tf_op jit(solution)/shard_map/ppermute | solution.py:35
  65.0 2.8 %collective-permute-done.18.refs_1_ = bf16[8,144,384]{2,1,0:T(8,128)(2,1)S(1)} collective-permute-done((bf16[8,144,384]{2,1,0:T(8,128)(2,1)S(1)}, bf16[8,144,384]{2,1,0:T(8,128)(2,1)S(1)}, u32[]{:S(2)}, u32[]{:S(2)}) %collective-permute-start.18) | collective-permute-done | bytes 884768 | tf_op jit(solution)/shard_map/ppermute | solution.py:35
  69.7 3.3 %collective-permute-done.16.refs_2_ = bf16[1,128,384]{2,1,0:T(8,128)(2,1)S(1)} collective-permute-done((bf16[1,128,384]{2,1,0:T(8,128)(2,1)S(1)}, bf16[1,128,384]{2,1,0:T(8,128)(2,1)S(1)}, u32[]{:S(2)}, u32[]{:S(2)}) %collective-permute-start.16) | collective-permute-done | bytes 98336 | tf_op jit(solution)/shard_map/ppermute | solution.py:35
  73.0 2.9 %shard_map.205 = (bf16[128,576]{1,0:T(8,128)(2,1)S(1)}, f32[3,128,384]{2,1,0:T(8,128)S(1)}, f32[8,384]{1,0:T(8,128)S(1)}) custom-call(s32[10]{0:T(128)S(1)} %pad_add_fusion.meta, bf16[1152,128]{1,0:T(8,128)(2,1)S(1)} %get-tuple-element.127.qp_ref, bf16[4,128,384]{2,1,0:T(8,128)(2,1)S(1)} %constant_dynamic-update-slice_fusion.16.refs_0_, ...), custom_call_target="tpu_custom_call" | custom-call | flops 603979776 | bytes 3000000 | tf_op jit(solution)/shard_map/pallas_call | solution.py:601
  75.9 7.9 %shard_map.206 = (bf16[576,128]{1,0:T(8,128)(2,1)}, bf16[16,144,384]{2,1,0:T(8,128)(2,1)S(1)}, bf16[16,144,384]{2,1,0:T(8,128)(2,1)S(1)}, bf16[16,72,384]{2,1,0:...) custom-call(s32[10]{0:T(128)S(1)} %pad_add_fusion.meta, ...), custom_call_target="tpu_custom_call" | custom-call | flops 2038431744 | bytes 14000000 | tf_op jit(solution)/shard_map/pallas_call | solution.py:601
  84.4 4.6 %shard_map.207 = (bf16[128,576]{1,0:T(8,128)(2,1)S(1)}, bf16[4,128,384]{2,1,0:T(8,128)(2,1)S(1)}, bf16[4,128,384]{2,1,0:T(8,128)(2,1)S(1)}) custom-call(s32[10]{0:T(128)S(1)} %pad_add_fusion.meta, bf16[1152,128]{1,0:T(8,128)(2,1)S(1)} %get-tuple-element.127.qp_ref, bf16[1152,128]{1,0:T(8,128)(2,1)S(1)} %get-tuple-element.152.gp_ref, ...), custom_call_target="tpu_custom_call" | custom-call | flops 1509949440 | bytes 5000000 | tf_op jit(solution)/shard_map/pallas_call | solution.py:601
  91.9 9.4 %collective-permute-done.26 = bf16[4,128,384]{2,1,0:T(8,128)(2,1)S(1)} collective-permute-done((bf16[4,128,384]{2,1,0:T(8,128)(2,1)S(1)}, bf16[4,128,384]{2,1,0:T(8,128)(2,1)S(1)}, u32[]{:S(2)}, u32[]{:S(2)}) %collective-permute-start.26) | collective-permute-done | bytes 393248 | tf_op jit(solution)/shard_map/ppermute | solution.py:35
  102.8 3.9 %collective-permute-start.29 = (bf16[1,128,384]{2,1,0:T(8,128)(2,1)S(1)}, bf16[1,128,384]{2,1,0:T(8,128)(2,1)S(1)}, u32[]{:S(2)}, u32[]{:S(2)}) collective-permute-start(bf16[1,128,384]{2,1,0:T(8,128)(2,1)S(1)} %get-tuple-element.229), channel_id=1, source_target_pairs={{0,24},{4,28},{8,16},{12,20},{16,8},{20,12},{24,0},{28,4},{1,25},{... | collective-permute-start | bytes 294920 | tf_op jit(solution)/shard_map/ppermute | solution.py:35
  107.3 5.0 %collective-permute-done.31 = bf16[8,72,384]{2,1,0:T(8,128)(2,1)S(1)} collective-permute-done((bf16[8,72,384]{2,1,0:T(8,128)(2,1)S(1)}, bf16[8,72,384]{2,1,0:T(8,128)(2,1)S(1)}, u32[]{:S(2)}, u32[]{:S(2)}) %collective-permute-start.31) | collective-permute-done | bytes 442400 | tf_op jit(solution)/shard_map/ppermute | solution.py:35
  115.4 3.5 %shard_map.208 = (f32[576,128]{1,0:T(8,128)}, bf16[16,80,256]{2,1,0:T(8,128)(2,1)S(1)}, bf16[16,80,256]{2,1,0:T(8,128)(2,1)S(1)}, bf16[16,72,256]{2,1,0:T(8,128)(2,1)S(1)}, bf16[16,72,256]{2,1,0:T(8,128)(2,1)S(1)}) custom-call(s32[10]{0:T(128)S(1)} %pad_add_fusion.meta, bf16[128,576]{1,0:T(8,128)(2,1)S(1)} %bitcast.42, ...), custom_call_target="tpu_custom_call" | custom-call | flops 905969664 | bytes 6000000 | tf_op jit(solution)/shard_map/pallas_call | solution.py:601
  120.0 2.6 %collective-permute-done.34 = bf16[4,144,384]{2,1,0:T(8,128)(2,1)S(1)} collective-permute-done((bf16[4,144,384]{2,1,0:T(8,128)(2,1)S(1)}, bf16[4,144,384]{2,1,0:T(8,128)(2,1)S(1)}, u32[]{:S(2)}, u32[]{:S(2)}) %collective-permute-start.34) | collective-permute-done | bytes 442400 | tf_op jit(solution)/shard_map/ppermute | solution.py:35
  122.9 3.6 %collective-permute-start.45 = (bf16[1,216,384]{2,1,0:T(8,128)(2,1)S(1)}, bf16[1,216,384]{2,1,0:T(8,128)(2,1)S(1)}, u32[]{:S(2)}, u32[]{:S(2)}) collective-permute-start(bf16[1,216,384]{2,1,0:T(8,128)(2,1)S(1)} %get-tuple-element.221), channel_id=1, source_target_pairs={{0,24},{4,28},{8,16},{12,20},{16,8},{20,12},{24,0},{28,4},{1,25},{... | collective-permute-start | bytes 497672 | tf_op jit(solution)/shard_map/ppermute | solution.py:35
  131.7 2.0 %collective-permute-done.43 = bf16[1,216,384]{2,1,0:T(8,128)(2,1)S(1)} collective-permute-done((bf16[1,216,384]{2,1,0:T(8,128)(2,1)S(1)}, bf16[1,216,384]{2,1,0:T(8,128)(2,1)S(1)}, u32[]{:S(2)}, u32[]{:S(2)}) %collective-permute-start.43) | collective-permute-done | bytes 165920 | tf_op jit(solution)/shard_map/ppermute | solution.py:35
  133.7 3.7 %collective-permute-done.44 = bf16[1,216,384]{2,1,0:T(8,128)(2,1)S(1)} collective-permute-done((bf16[1,216,384]{2,1,0:T(8,128)(2,1)S(1)}, bf16[1,216,384]{2,1,0:T(8,128)(2,1)S(1)}, u32[]{:S(2)}, u32[]{:S(2)}) %collective-permute-start.44) | collective-permute-done | bytes 165920 | tf_op jit(solution)/shard_map/ppermute | solution.py:35
  141.2 3.2 %collective-permute-done.39 = bf16[4,72,256]{2,1,0:T(8,128)(2,1)S(1)} collective-permute-done((bf16[4,72,256]{2,1,0:T(8,128)(2,1)S(1)}, bf16[4,72,256]{2,1,0:T(8,128)(2,1)S(1)}, u32[]{:S(2)}, u32[]{:S(2)}) %collective-permute-start.39) | collective-permute-done | bytes 147488 | tf_op jit(solution)/shard_map/ppermute | solution.py:35
  144.6 3.0 %collective-permute-start.42 = (bf16[1,152,256]{2,1,0:T(8,128)(2,1)S(1)}, bf16[1,152,256]{2,1,0:T(8,128)(2,1)S(1)}, u32[]{:S(2)}, u32[]{:S(2)}) collective-permute-start(bf16[1,152,256]{2,1,0:T(8,128)(2,1)S(1)} %get-tuple-element.235), channel_id=1, source_target_pairs={{0,24},{4,28},{8,16},{12,20},{16,8},{20,12},{24,0},{28,4},{1,25},{... | collective-permute-start | bytes 233480 | tf_op jit(solution)/shard_map/ppermute | solution.py:35
  (160 shorter events, 52.2 us)
Async XLA Ops:
  1.6 11.1 %collective-permute-start.2 = (bf16[1,152,256]{2,1,0:T(8,128)(2,1)S(1)}, bf16[1,152,256]{2,1,0:T(8,128)(2,1)S(1)}, u32[]{:S(2)}, u32[]{:S(2)}) collective-permute-start(bf16[1,152,256]{2,1,0:T(8,128)(2,1)S(1)} %bitcast.48), channel_id=1, source_target_pairs={{0,24},{4,28},{8,16},{12,20},{16,8},{20,12},{24,0},{28,4},{1,25},{... | collective-permute-start | bytes 233480 | tf_op jit(solution)/shard_map/ppermute | solution.py:35
  13.4 13.1 %collective-permute-start.7 = (bf16[1,216,384]{2,1,0:T(8,128)(2,1)S(1)}, bf16[1,216,384]{2,1,0:T(8,128)(2,1)S(1)}, u32[]{:S(2)}, u32[]{:S(2)}) collective-permute-start(bf16[1,216,384]{2,1,0:T(8,128)(2,1)S(1)} %maximum_bitcast_fusion), channel_id=1, source_target_pairs={{0,24},{4,28},{8,16},{12,20},{16,8},{20,12},{24,0},{28,4},{1,25},{... | collective-permute-start | bytes 497672 | tf_op jit(solution)/shard_map/ppermute | solution.py:35
  16.7 13.2 %collective-permute-start.6 = (bf16[1,216,384]{2,1,0:T(8,128)(2,1)S(1)}, bf16[1,216,384]{2,1,0:T(8,128)(2,1)S(1)}, u32[]{:S(2)}, u32[]{:S(2)}) collective-permute-start(bf16[1,216,384]{2,1,0:T(8,128)(2,1)S(1)} %maximum_bitcast_fusion), channel_id=1, source_target_pairs={{0,16},{4,20},{8,24},{12,28},{16,0},{20,4},{24,8},{28,12},{1,17},{... | collective-permute-start | bytes 497672 | tf_op jit(solution)/shard_map/ppermute | solution.py:35
  16.7 13.2 %collective-permute-start.5 = (bf16[1,216,384]{2,1,0:T(8,128)(2,1)S(1)}, bf16[1,216,384]{2,1,0:T(8,128)(2,1)S(1)}, u32[]{:S(2)}, u32[]{:S(2)}) collective-permute-start(bf16[1,216,384]{2,1,0:T(8,128)(2,1)S(1)} %maximum_bitcast_fusion), channel_id=1, source_target_pairs={{0,8},{4,12},{8,0},{12,4},{16,24},{20,28},{24,16},{28,20},{1,9},{5... | collective-permute-start | bytes 497672 | tf_op jit(solution)/shard_map/ppermute | solution.py:35
  33.7 12.6 %collective-permute-start.17 = (bf16[4,144,384]{2,1,0:T(8,128)(2,1)S(1)}, bf16[4,144,384]{2,1,0:T(8,128)(2,1)S(1)}, u32[]{:S(2)}, u32[]{:S(2)}) collective-permute-start(bf16[4,144,384]{2,1,0:T(8,128)(2,1)S(1)} %constant_dynamic-update-slice_fusion.20), channel_id=1, source_target_pairs={{0,4},{4,0},{8,12},{12,8},{16,20},{20,16},{24,28},{28,24},{1,5},{5... | collective-permute-start | bytes 1327112 | tf_op jit(solution)/shard_map/ppermute | solution.py:35
  38.6 9.4 %collective-permute-start.14 = (bf16[1,128,384]{2,1,0:T(8,128)(2,1)S(1)}, bf16[1,128,384]{2,1,0:T(8,128)(2,1)S(1)}, u32[]{:S(2)}, u32[]{:S(2)}) collective-permute-start(bf16[1,128,384]{2,1,0:T(8,128)(2,1)S(1)} %bitcast.44), channel_id=1, source_target_pairs={{0,24},{4,28},{8,16},{12,20},{16,8},{20,12},{24,0},{28,4},{1,25},{... | collective-permute-start | bytes 294920 | tf_op jit(solution)/shard_map/ppermute | solution.py:35
  41.1 9.8 %collective-permute-start.13 = (bf16[1,128,384]{2,1,0:T(8,128)(2,1)S(1)}, bf16[1,128,384]{2,1,0:T(8,128)(2,1)S(1)}, u32[]{:S(2)}, u32[]{:S(2)}) collective-permute-start(bf16[1,128,384]{2,1,0:T(8,128)(2,1)S(1)} %bitcast.45), channel_id=1, source_target_pairs={{0,16},{4,20},{8,24},{12,28},{16,0},{20,4},{24,8},{28,12},{1,17},{... | collective-permute-start | bytes 294920 | tf_op jit(solution)/shard_map/ppermute | solution.py:35
  46.4 21.3 %collective-permute-start.18 = (bf16[8,144,384]{2,1,0:T(8,128)(2,1)S(1)}, bf16[8,144,384]{2,1,0:T(8,128)(2,1)S(1)}, u32[]{:S(2)}, u32[]{:S(2)}) collective-permute-start(bf16[8,144,384]{2,1,0:T(8,128)(2,1)S(1)} %constant_dynamic-update-slice_fusion.24.refs_0_), channel_id=1, source_target_pairs={{0,2},{1,3},{2,0},{3,1},{4,6},{5,7},{6,4},{7,5},{8,10},{9,11},{10,... | collective-permute-start | bytes 2654216 | tf_op jit(solution)/shard_map/ppermute | solution.py:35
  46.6 18.2 %collective-permute-start.22 = (bf16[8,72,384]{2,1,0:T(8,128)(2,1)S(1)}, bf16[8,72,384]{2,1,0:T(8,128)(2,1)S(1)}, u32[]{:S(2)}, u32[]{:S(2)}) collective-permute-start(bf16[8,72,384]{2,1,0:T(8,128)(2,1)S(1)} %constant_dynamic-update-slice_fusion.30), channel_id=1, source_target_pairs={{0,4},{4,0},{8,12},{12,8},{16,20},{20,16},{24,28},{28,24},{1,5},{5... | collective-permute-start | bytes 1327112 | tf_op jit(solution)/shard_map/ppermute | solution.py:35
  50.9 13.8 %collective-permute-start.15 = (bf16[3,128,384]{2,1,0:T(8,128)(2,1)S(1)}, bf16[3,128,384]{2,1,0:T(8,128)(2,1)S(1)}, u32[]{:S(2)}, u32[]{:S(2)}) collective-permute-start(bf16[3,128,384]{2,1,0:T(8,128)(2,1)S(1)} %pad_maximum_fusion.1), channel_id=1, source_target_pairs={{0,4},{4,0},{8,12},{12,8},{16,20},{20,16},{24,28},{28,24},{1,5},{5... | collective-permute-start | bytes 884744 | tf_op jit(solution)/shard_map/ppermute | solution.py:35
  64.9 11.0 %collective-permute-start.23 = (bf16[16,72,384]{2,1,0:T(8,128)(2,1)S(1)}, bf16[16,72,384]{2,1,0:T(8,128)(2,1)S(1)}, u32[]{:S(2)}, u32[]{:S(2)}) collective-permute-start(bf16[16,72,384]{2,1,0:T(8,128)(2,1)S(1)} %constant_dynamic-update-slice_fusion.32.refs_4_), channel_id=1, source_target_pairs={{0,1},{1,0},{2,3},{3,2},{4,5},{5,4},{6,7},{7,6},{8,9},{9,8},{10,11... | collective-permute-start | bytes 2654216 | tf_op jit(solution)/shard_map/ppermute | solution.py:35
  89.5 22.8 %collective-permute-start.30 = (bf16[8,144,384]{2,1,0:T(8,128)(2,1)S(1)}, bf16[8,144,384]{2,1,0:T(8,128)(2,1)S(1)}, u32[]{:S(2)}, u32[]{:S(2)}) collective-permute-start(bf16[8,144,384]{2,1,0:T(8,128)(2,1)S(1)} %get-tuple-element.210), channel_id=1, source_target_pairs={{0,2},{1,3},{2,0},{3,1},{4,6},{5,7},{6,4},{7,5},{8,10},{9,11},{10,... | collective-permute-start | bytes 2654216 | tf_op jit(solution)/shard_map/ppermute | solution.py:35
  90.6 10.8 %collective-permute-start.26 = (bf16[4,128,384]{2,1,0:T(8,128)(2,1)S(1)}, bf16[4,128,384]{2,1,0:T(8,128)(2,1)S(1)}, u32[]{:S(2)}, u32[]{:S(2)}) collective-permute-start(bf16[4,128,384]{2,1,0:T(8,128)(2,1)S(1)} %get-tuple-element.166), channel_id=1, source_target_pairs={{0,4},{4,0},{8,12},{12,8},{16,20},{20,16},{24,28},{28,24},{1,5},{5... | collective-permute-start | bytes 1179656 | tf_op jit(solution)/shard_map/ppermute | solution.py:35
  101.4 10.9 %collective-permute-start.31 = (bf16[8,72,384]{2,1,0:T(8,128)(2,1)S(1)}, bf16[8,72,384]{2,1,0:T(8,128)(2,1)S(1)}, u32[]{:S(2)}, u32[]{:S(2)}) collective-permute-start(bf16[8,72,384]{2,1,0:T(8,128)(2,1)S(1)} %get-tuple-element.167), channel_id=1, source_target_pairs={{0,4},{4,0},{8,12},{12,8},{16,20},{20,16},{24,28},{28,24},{1,5},{5... | collective-permute-start | bytes 1327112 | tf_op jit(solution)/shard_map/ppermute | solution.py:35
  102.8 12.5 %collective-permute-start.29 = (bf16[1,128,384]{2,1,0:T(8,128)(2,1)S(1)}, bf16[1,128,384]{2,1,0:T(8,128)(2,1)S(1)}, u32[]{:S(2)}, u32[]{:S(2)}) collective-permute-start(bf16[1,128,384]{2,1,0:T(8,128)(2,1)S(1)} %get-tuple-element.229), channel_id=1, source_target_pairs={{0,24},{4,28},{8,16},{12,20},{16,8},{20,12},{24,0},{28,4},{1,25},{... | collective-permute-start | bytes 294920 | tf_op jit(solution)/shard_map/ppermute | solution.py:35
  106.7 8.6 %collective-permute-start.28 = (bf16[1,128,384]{2,1,0:T(8,128)(2,1)S(1)}, bf16[1,128,384]{2,1,0:T(8,128)(2,1)S(1)}, u32[]{:S(2)}, u32[]{:S(2)}) collective-permute-start(bf16[1,128,384]{2,1,0:T(8,128)(2,1)S(1)} %get-tuple-element.230), channel_id=1, source_target_pairs={{0,16},{4,20},{8,24},{12,28},{16,0},{20,4},{24,8},{28,12},{1,17},{... | collective-permute-start | bytes 294920 | tf_op jit(solution)/shard_map/ppermute | solution.py:35
  106.7 8.6 %collective-permute-start.27 = (bf16[1,128,384]{2,1,0:T(8,128)(2,1)S(1)}, bf16[1,128,384]{2,1,0:T(8,128)(2,1)S(1)}, u32[]{:S(2)}, u32[]{:S(2)}) collective-permute-start(bf16[1,128,384]{2,1,0:T(8,128)(2,1)S(1)} %get-tuple-element.231), channel_id=1, source_target_pairs={{0,8},{4,12},{8,0},{12,4},{16,24},{20,28},{24,16},{28,20},{1,9},{5... | collective-permute-start | bytes 294920 | tf_op jit(solution)/shard_map/ppermute | solution.py:35
  112.5 10.1 %collective-permute-start.34 = (bf16[4,144,384]{2,1,0:T(8,128)(2,1)S(1)}, bf16[4,144,384]{2,1,0:T(8,128)(2,1)S(1)}, u32[]{:S(2)}, u32[]{:S(2)}) collective-permute-start(bf16[4,144,384]{2,1,0:T(8,128)(2,1)S(1)} %get-tuple-element.212), channel_id=1, source_target_pairs={{0,4},{4,0},{8,12},{12,8},{16,20},{20,16},{24,28},{28,24},{1,5},{5... | collective-permute-start | bytes 1327112 | tf_op jit(solution)/shard_map/ppermute | solution.py:35
  118.9 8.4 %collective-permute-start.32 = (bf16[16,80,256]{2,1,0:T(8,128)(2,1)S(1)}, bf16[16,80,256]{2,1,0:T(8,128)(2,1)S(1)}, u32[]{:S(2)}, u32[]{:S(2)}) collective-permute-start(bf16[16,80,256]{2,1,0:T(8,128)(2,1)S(1)} %get-tuple-element.181), channel_id=1, source_target_pairs={{0,1},{1,0},{2,3},{3,2},{4,5},{5,4},{6,7},{7,6},{8,9},{9,8},{10,11... | collective-permute-start | bytes 1966088 | tf_op jit(solution)/shard_map/ppermute | solution.py:35
  118.9 8.4 %collective-permute-start.33 = (bf16[16,72,256]{2,1,0:T(8,128)(2,1)S(1)}, bf16[16,72,256]{2,1,0:T(8,128)(2,1)S(1)}, u32[]{:S(2)}, u32[]{:S(2)}) collective-permute-start(bf16[16,72,256]{2,1,0:T(8,128)(2,1)S(1)} %get-tuple-element.182), channel_id=1, source_target_pairs={{0,1},{1,0},{2,3},{3,2},{4,5},{5,4},{6,7},{7,6},{8,9},{9,8},{10,11... | collective-permute-start | bytes 1769480 | tf_op jit(solution)/shard_map/ppermute | solution.py:35
  122.9 8.8 %collective-permute-start.45 = (bf16[1,216,384]{2,1,0:T(8,128)(2,1)S(1)}, bf16[1,216,384]{2,1,0:T(8,128)(2,1)S(1)}, u32[]{:S(2)}, u32[]{:S(2)}) collective-permute-start(bf16[1,216,384]{2,1,0:T(8,128)(2,1)S(1)} %get-tuple-element.221), channel_id=1, source_target_pairs={{0,24},{4,28},{8,16},{12,20},{16,8},{20,12},{24,0},{28,4},{1,25},{... | collective-permute-start | bytes 497672 | tf_op jit(solution)/shard_map/ppermute | solution.py:35
  126.5 10.9 %collective-permute-start.44 = (bf16[1,216,384]{2,1,0:T(8,128)(2,1)S(1)}, bf16[1,216,384]{2,1,0:T(8,128)(2,1)S(1)}, u32[]{:S(2)}, u32[]{:S(2)}) collective-permute-start(bf16[1,216,384]{2,1,0:T(8,128)(2,1)S(1)} %get-tuple-element.224), channel_id=1, source_target_pairs={{0,16},{4,20},{8,24},{12,28},{16,0},{20,4},{24,8},{28,12},{1,17},{... | collective-permute-start | bytes 497672 | tf_op jit(solution)/shard_map/ppermute | solution.py:35
  127.5 10.0 %collective-permute-start.36 = (bf16[8,80,256]{2,1,0:T(8,128)(2,1)S(1)}, bf16[8,80,256]{2,1,0:T(8,128)(2,1)S(1)}, u32[]{:S(2)}, u32[]{:S(2)}) collective-permute-start(bf16[8,80,256]{2,1,0:T(8,128)(2,1)S(1)} %get-tuple-element.215), channel_id=1, source_target_pairs={{0,2},{1,3},{2,0},{3,1},{4,6},{5,7},{6,4},{7,5},{8,10},{9,11},{10,... | collective-permute-start | bytes 983048 | tf_op jit(solution)/shard_map/ppermute | solution.py:35
  128.9 8.6 %collective-permute-start.37 = (bf16[8,72,256]{2,1,0:T(8,128)(2,1)S(1)}, bf16[8,72,256]{2,1,0:T(8,128)(2,1)S(1)}, u32[]{:S(2)}, u32[]{:S(2)}) collective-permute-start(bf16[8,72,256]{2,1,0:T(8,128)(2,1)S(1)} %get-tuple-element.217), channel_id=1, source_target_pairs={{0,4},{4,0},{8,12},{12,8},{16,20},{20,16},{24,28},{28,24},{1,5},{5... | collective-permute-start | bytes 884744 | tf_op jit(solution)/shard_map/ppermute | solution.py:35
  (24 other events, 148.2 us)

commit v5 on v4

--- a/solution.py
+++ b/solution.py
@@ -662,12 +662,12 @@
 
     attn = Gather(own, split, shards)
     attn.outer()
+    attn.second()
     if packed:
-        ffn.outer(*attn.a, *attn.b)
-    attn.second()
+        ffn.outer(*attn.now)
     attn.third()
     if packed:
-        attn_in = attn.cores(*ffn.a, *ffn.b)
+        attn_in = attn.cores(ffn.a[3], ffn.b[3])
         ffn.second()
     else:
         attn_in = attn.cores()

time: 154 us -> 151 us (0.981)
  starting transfers between devices: 51.7 us -> 49 us
    ppermute x46, starting transfers between devices: 51.7 us -> 49 us  [swap(): return lax.ppermute(x, axis, [(i, i ^ mask) for i in range(size)])]
  transfers between devices with their start and end apart: 46 -> 46, of which waited for: 24 -> 22; matrix products, arithmetic and copies ran while one was open for 5% -> 5% of each run, Pallas kernels for 8% -> 8%
where the time goes in v5:
time: 151 us; the launch traced here: 150 us
  waiting for transfers between devices  68.1 us (45%)
  starting transfers between devices  49 us (32%)
  Pallas kernels  22.3 us (15%)
  other arithmetic  5.14 us (3%)
  local copies, waits for them, and re-layouts  3.31 us (2%)
  between operations  2.57 us (2%)
    ppermute x46, waiting for transfers between devices, swap(): return lax.ppermute(x, axis, [(i, i ^ mask) for i in range(size)])  68.1 us
    ppermute x46, starting transfers between devices, swap(): return lax.ppermute(x, axis, [(i, i ^ mask) for i in range(size)])  49 us
    pallas_call x7, Pallas kernels, call(): pl.pallas_call(kernel, out_shape=outs, in_specs=[smem] * scalars + [vmem]...  22.3 us
  transfers between devices with their start and end apart: 46, of which 22 were waited for; matrix products, arithmetic and copies ran while one was open for 5% of the time, Pallas kernels for 8%

profile of v5, /device:TPU:0, one launch (start us, length us, event | category | flops | bytes accessed | tf_op | source)
XLA Modules:
  0.0 150.4 jit_solution(9340908794013219506)
XLA Ops:
  1.6 5.1 %collective-permute-start.2 = (bf16[1,152,256]{2,1,0:T(8,128)(2,1)S(1)}, bf16[1,152,256]{2,1,0:T(8,128)(2,1)S(1)}, u32[]{:S(2)}, u32[]{:S(2)}) collective-permute-start(bf16[1,152,256]{2,1,0:T(8,128)(2,1)S(1)} %bitcast.48), channel_id=1, source_target_pairs={{0,24},{4,28},{8,16},{12,20},{16,8},{20,12},{24,0},{28,4},{1,25},{... | collective-permute-start | bytes 233480 | tf_op jit(solution)/shard_map/ppermute | solution.py:35
  18.4 2.0 %collective-permute-start.15 = (bf16[1,216,384]{2,1,0:T(8,128)(2,1)S(1)}, bf16[1,216,384]{2,1,0:T(8,128)(2,1)S(1)}, u32[]{:S(2)}, u32[]{:S(2)}) collective-permute-start(bf16[1,216,384]{2,1,0:T(8,128)(2,1)S(1)} %maximum_bitcast_fusion), channel_id=1, source_target_pairs={{0,8},{4,12},{8,0},{12,4},{16,24},{20,28},{24,16},{28,20},{1,9},{5... | collective-permute-start | bytes 497672 | tf_op jit(solution)/shard_map/ppermute | solution.py:35
  22.2 5.9 %collective-permute-done.16 = bf16[1,216,384]{2,1,0:T(8,128)(2,1)S(1)} collective-permute-done((bf16[1,216,384]{2,1,0:T(8,128)(2,1)S(1)}, bf16[1,216,384]{2,1,0:T(8,128)(2,1)S(1)}, u32[]{:S(2)}, u32[]{:S(2)}) %collective-permute-start.16) | collective-permute-done | bytes 165920 | tf_op jit(solution)/shard_map/ppermute | solution.py:35
  34.9 4.0 %collective-permute-start.10 = (bf16[1,128,384]{2,1,0:T(8,128)(2,1)S(1)}, bf16[1,128,384]{2,1,0:T(8,128)(2,1)S(1)}, u32[]{:S(2)}, u32[]{:S(2)}) collective-permute-start(bf16[1,128,384]{2,1,0:T(8,128)(2,1)S(1)} %bitcast.43), channel_id=1, source_target_pairs={{0,8},{4,12},{8,0},{12,4},{16,24},{20,28},{24,16},{28,20},{1,9},{5... | collective-permute-start | bytes 294920 | tf_op jit(solution)/shard_map/ppermute | solution.py:35
  38.8 2.4 %collective-permute-start.12 = (bf16[1,128,384]{2,1,0:T(8,128)(2,1)S(1)}, bf16[1,128,384]{2,1,0:T(8,128)(2,1)S(1)}, u32[]{:S(2)}, u32[]{:S(2)}) collective-permute-start(bf16[1,128,384]{2,1,0:T(8,128)(2,1)S(1)} %bitcast.44), channel_id=1, source_target_pairs={{0,24},{4,28},{8,16},{12,20},{16,8},{20,12},{24,0},{28,4},{1,25},{... | collective-permute-start | bytes 294920 | tf_op jit(solution)/shard_map/ppermute | solution.py:35
  44.5 2.5 %collective-permute-done.12 = bf16[1,128,384]{2,1,0:T(8,128)(2,1)S(1)} collective-permute-done((bf16[1,128,384]{2,1,0:T(8,128)(2,1)S(1)}, bf16[1,128,384]{2,1,0:T(8,128)(2,1)S(1)}, u32[]{:S(2)}, u32[]{:S(2)}) %collective-permute-start.12) | collective-permute-done | bytes 98336 | tf_op jit(solution)/shard_map/ppermute | solution.py:35
  47.0 3.3 %collective-permute-done.11 = bf16[1,128,384]{2,1,0:T(8,128)(2,1)S(1)} collective-permute-done((bf16[1,128,384]{2,1,0:T(8,128)(2,1)S(1)}, bf16[1,128,384]{2,1,0:T(8,128)(2,1)S(1)}, u32[]{:S(2)}, u32[]{:S(2)}) %collective-permute-start.11) | collective-permute-done | bytes 98336 | tf_op jit(solution)/shard_map/ppermute | solution.py:35
  50.9 10.4 %collective-permute-done.13.refs_1_ = bf16[3,128,384]{2,1,0:T(8,128)(2,1)S(1)} collective-permute-done((bf16[3,128,384]{2,1,0:T(8,128)(2,1)S(1)}, bf16[3,128,384]{2,1,0:T(8,128)(2,1)S(1)}, u32[]{:S(2)}, u32[]{:S(2)}) %collective-permute-start.13) | collective-permute-done | bytes 294944 | tf_op jit(solution)/shard_map/ppermute | solution.py:35
  61.5 2.5 %collective-permute-done.18.refs_1_ = bf16[8,144,384]{2,1,0:T(8,128)(2,1)S(1)} collective-permute-done((bf16[8,144,384]{2,1,0:T(8,128)(2,1)S(1)}, bf16[8,144,384]{2,1,0:T(8,128)(2,1)S(1)}, u32[]{:S(2)}, u32[]{:S(2)}) %collective-permute-start.18) | collective-permute-done | bytes 884768 | tf_op jit(solution)/shard_map/ppermute | solution.py:35
  65.2 4.1 %collective-permute-done.14.refs_2_ = bf16[1,128,384]{2,1,0:T(8,128)(2,1)S(1)} collective-permute-done((bf16[1,128,384]{2,1,0:T(8,128)(2,1)S(1)}, bf16[1,128,384]{2,1,0:T(8,128)(2,1)S(1)}, u32[]{:S(2)}, u32[]{:S(2)}) %collective-permute-start.14) | collective-permute-done | bytes 98336 | tf_op jit(solution)/shard_map/ppermute | solution.py:35
  69.3 2.9 %shard_map.205 = (bf16[128,576]{1,0:T(8,128)(2,1)S(1)}, f32[3,128,384]{2,1,0:T(8,128)S(1)}, f32[8,384]{1,0:T(8,128)S(1)}) custom-call(s32[10]{0:T(128)S(1)} %pad_add_fusion.meta, bf16[1152,128]{1,0:T(8,128)(2,1)S(1)} %get-tuple-element.127.qp_ref, bf16[4,128,384]{2,1,0:T(8,128)(2,1)S(1)} %constant_dynamic-update-slice_fusion.16.refs_0_, ...), custom_call_target="tpu_custom_call" | custom-call | flops 603979776 | bytes 3000000 | tf_op jit(solution)/shard_map/pallas_call | solution.py:601
  72.2 7.9 %shard_map.206 = (bf16[576,128]{1,0:T(8,128)(2,1)}, bf16[16,144,384]{2,1,0:T(8,128)(2,1)S(1)}, bf16[16,144,384]{2,1,0:T(8,128)(2,1)S(1)}, bf16[16,72,384]{2,1,0:...) custom-call(s32[10]{0:T(128)S(1)} %pad_add_fusion.meta, ...), custom_call_target="tpu_custom_call" | custom-call | flops 2038431744 | bytes 14000000 | tf_op jit(solution)/shard_map/pallas_call | solution.py:601
  80.7 4.6 %shard_map.207 = (bf16[128,576]{1,0:T(8,128)(2,1)S(1)}, bf16[4,128,384]{2,1,0:T(8,128)(2,1)S(1)}, bf16[4,128,384]{2,1,0:T(8,128)(2,1)S(1)}) custom-call(s32[10]{0:T(128)S(1)} %pad_add_fusion.meta, bf16[1152,128]{1,0:T(8,128)(2,1)S(1)} %get-tuple-element.127.qp_ref, bf16[1152,128]{1,0:T(8,128)(2,1)S(1)} %get-tuple-element.152.gp_ref, ...), custom_call_target="tpu_custom_call" | custom-call | flops 1509949440 | bytes 5000000 | tf_op jit(solution)/shard_map/pallas_call | solution.py:601
  87.7 10.2 %collective-permute-done.26 = bf16[4,128,384]{2,1,0:T(8,128)(2,1)S(1)} collective-permute-done((bf16[4,128,384]{2,1,0:T(8,128)(2,1)S(1)}, bf16[4,128,384]{2,1,0:T(8,128)(2,1)S(1)}, u32[]{:S(2)}, u32[]{:S(2)}) %collective-permute-start.26) | collective-permute-done | bytes 393248 | tf_op jit(solution)/shard_map/ppermute | solution.py:35
  98.6 3.2 %collective-permute-start.29 = (bf16[1,128,384]{2,1,0:T(8,128)(2,1)S(1)}, bf16[1,128,384]{2,1,0:T(8,128)(2,1)S(1)}, u32[]{:S(2)}, u32[]{:S(2)}) collective-permute-start(bf16[1,128,384]{2,1,0:T(8,128)(2,1)S(1)} %get-tuple-element.229), channel_id=1, source_target_pairs={{0,24},{4,28},{8,16},{12,20},{16,8},{20,12},{24,0},{28,4},{1,25},{... | collective-permute-start | bytes 294920 | tf_op jit(solution)/shard_map/ppermute | solution.py:35
  101.8 2.1 %collective-permute-start.28 = (bf16[1,128,384]{2,1,0:T(8,128)(2,1)S(1)}, bf16[1,128,384]{2,1,0:T(8,128)(2,1)S(1)}, u32[]{:S(2)}, u32[]{:S(2)}) collective-permute-start(bf16[1,128,384]{2,1,0:T(8,128)(2,1)S(1)} %get-tuple-element.230), channel_id=1, source_target_pairs={{0,16},{4,20},{8,24},{12,28},{16,0},{20,4},{24,8},{28,12},{1,17},{... | collective-permute-start | bytes 294920 | tf_op jit(solution)/shard_map/ppermute | solution.py:35
  104.1 4.8 %collective-permute-done.31 = bf16[8,72,384]{2,1,0:T(8,128)(2,1)S(1)} collective-permute-done((bf16[8,72,384]{2,1,0:T(8,128)(2,1)S(1)}, bf16[8,72,384]{2,1,0:T(8,128)(2,1)S(1)}, u32[]{:S(2)}, u32[]{:S(2)}) %collective-permute-start.31) | collective-permute-done | bytes 442400 | tf_op jit(solution)/shard_map/ppermute | solution.py:35
  110.8 3.5 %shard_map.208 = (f32[576,128]{1,0:T(8,128)}, bf16[16,80,256]{2,1,0:T(8,128)(2,1)S(1)}, bf16[16,80,256]{2,1,0:T(8,128)(2,1)S(1)}, bf16[16,72,256]{2,1,0:T(8,128)(2,1)S(1)}, bf16[16,72,256]{2,1,0:T(8,128)(2,1)S(1)}) custom-call(s32[10]{0:T(128)S(1)} %pad_add_fusion.meta, bf16[128,576]{1,0:T(8,128)(2,1)S(1)} %bitcast.42, ...), custom_call_target="tpu_custom_call" | custom-call | flops 905969664 | bytes 6000000 | tf_op jit(solution)/shard_map/pallas_call | solution.py:601
  115.7 3.4 %collective-permute-done.34 = bf16[4,144,384]{2,1,0:T(8,128)(2,1)S(1)} collective-permute-done((bf16[4,144,384]{2,1,0:T(8,128)(2,1)S(1)}, bf16[4,144,384]{2,1,0:T(8,128)(2,1)S(1)}, u32[]{:S(2)}, u32[]{:S(2)}) %collective-permute-start.34) | collective-permute-done | bytes 442400 | tf_op jit(solution)/shard_map/ppermute | solution.py:35
  119.4 3.2 %collective-permute-start.45 = (bf16[1,216,384]{2,1,0:T(8,128)(2,1)S(1)}, bf16[1,216,384]{2,1,0:T(8,128)(2,1)S(1)}, u32[]{:S(2)}, u32[]{:S(2)}) collective-permute-start(bf16[1,216,384]{2,1,0:T(8,128)(2,1)S(1)} %get-tuple-element.221), channel_id=1, source_target_pairs={{0,24},{4,28},{8,16},{12,20},{16,8},{20,12},{24,0},{28,4},{1,25},{... | collective-permute-start | bytes 497672 | tf_op jit(solution)/shard_map/ppermute | solution.py:35
  122.6 2.3 %collective-permute-start.43 = (bf16[1,216,384]{2,1,0:T(8,128)(2,1)S(1)}, bf16[1,216,384]{2,1,0:T(8,128)(2,1)S(1)}, u32[]{:S(2)}, u32[]{:S(2)}) collective-permute-start(bf16[1,216,384]{2,1,0:T(8,128)(2,1)S(1)} %get-tuple-element.223), channel_id=1, source_target_pairs={{0,8},{4,12},{8,0},{12,4},{16,24},{20,28},{24,16},{28,20},{1,9},{5... | collective-permute-start | bytes 497672 | tf_op jit(solution)/shard_map/ppermute | solution.py:35
  129.5 5.9 %collective-permute-done.44 = bf16[1,216,384]{2,1,0:T(8,128)(2,1)S(1)} collective-permute-done((bf16[1,216,384]{2,1,0:T(8,128)(2,1)S(1)}, bf16[1,216,384]{2,1,0:T(8,128)(2,1)S(1)}, u32[]{:S(2)}, u32[]{:S(2)}) %collective-permute-start.44) | collective-permute-done | bytes 165920 | tf_op jit(solution)/shard_map/ppermute | solution.py:35
  138.2 3.3 %collective-permute-done.39 = bf16[4,72,256]{2,1,0:T(8,128)(2,1)S(1)} collective-permute-done((bf16[4,72,256]{2,1,0:T(8,128)(2,1)S(1)}, bf16[4,72,256]{2,1,0:T(8,128)(2,1)S(1)}, u32[]{:S(2)}, u32[]{:S(2)}) %collective-permute-start.39) | collective-permute-done | bytes 147488 | tf_op jit(solution)/shard_map/ppermute | solution.py:35
  141.6 2.8 %collective-permute-start.42 = (bf16[1,152,256]{2,1,0:T(8,128)(2,1)S(1)}, bf16[1,152,256]{2,1,0:T(8,128)(2,1)S(1)}, u32[]{:S(2)}, u32[]{:S(2)}) collective-permute-start(bf16[1,152,256]{2,1,0:T(8,128)(2,1)S(1)} %get-tuple-element.235), channel_id=1, source_target_pairs={{0,24},{4,28},{8,16},{12,20},{16,8},{20,12},{24,0},{28,4},{1,25},{... | collective-permute-start | bytes 233480 | tf_op jit(solution)/shard_map/ppermute | solution.py:35
  (160 shorter events, 45.5 us)
Async XLA Ops:
  1.6 11.1 %collective-permute-start.2 = (bf16[1,152,256]{2,1,0:T(8,128)(2,1)S(1)}, bf16[1,152,256]{2,1,0:T(8,128)(2,1)S(1)}, u32[]{:S(2)}, u32[]{:S(2)}) collective-permute-start(bf16[1,152,256]{2,1,0:T(8,128)(2,1)S(1)} %bitcast.48), channel_id=1, source_target_pairs={{0,24},{4,28},{8,16},{12,20},{16,8},{20,12},{24,0},{28,4},{1,25},{... | collective-permute-start | bytes 233480 | tf_op jit(solution)/shard_map/ppermute | solution.py:35
  16.6 11.6 %collective-permute-start.16 = (bf16[1,216,384]{2,1,0:T(8,128)(2,1)S(1)}, bf16[1,216,384]{2,1,0:T(8,128)(2,1)S(1)}, u32[]{:S(2)}, u32[]{:S(2)}) collective-permute-start(bf16[1,216,384]{2,1,0:T(8,128)(2,1)S(1)} %maximum_bitcast_fusion), channel_id=1, source_target_pairs={{0,16},{4,20},{8,24},{12,28},{16,0},{20,4},{24,8},{28,12},{1,17},{... | collective-permute-start | bytes 497672 | tf_op jit(solution)/shard_map/ppermute | solution.py:35
  18.4 9.8 %collective-permute-start.15 = (bf16[1,216,384]{2,1,0:T(8,128)(2,1)S(1)}, bf16[1,216,384]{2,1,0:T(8,128)(2,1)S(1)}, u32[]{:S(2)}, u32[]{:S(2)}) collective-permute-start(bf16[1,216,384]{2,1,0:T(8,128)(2,1)S(1)} %maximum_bitcast_fusion), channel_id=1, source_target_pairs={{0,8},{4,12},{8,0},{12,4},{16,24},{20,28},{24,16},{28,20},{1,9},{5... | collective-permute-start | bytes 497672 | tf_op jit(solution)/shard_map/ppermute | solution.py:35
  20.4 9.6 %collective-permute-start.5 = (bf16[1,216,384]{2,1,0:T(8,128)(2,1)S(1)}, bf16[1,216,384]{2,1,0:T(8,128)(2,1)S(1)}, u32[]{:S(2)}, u32[]{:S(2)}) collective-permute-start(bf16[1,216,384]{2,1,0:T(8,128)(2,1)S(1)} %maximum_bitcast_fusion), channel_id=1, source_target_pairs={{0,24},{4,28},{8,16},{12,20},{16,8},{20,12},{24,0},{28,4},{1,25},{... | collective-permute-start | bytes 497672 | tf_op jit(solution)/shard_map/ppermute | solution.py:35
  21.0 9.1 %collective-permute-start.8 = (bf16[8,72,256]{2,1,0:T(8,128)(2,1)S(1)}, bf16[8,72,256]{2,1,0:T(8,128)(2,1)S(1)}, u32[]{:S(2)}, u32[]{:S(2)}) collective-permute-start(bf16[8,72,256]{2,1,0:T(8,128)(2,1)S(1)} %constant_dynamic-update-slice_fusion.12), channel_id=1, source_target_pairs={{0,4},{4,0},{8,12},{12,8},{16,20},{20,16},{24,28},{28,24},{1,5},{5... | collective-permute-start | bytes 884744 | tf_op jit(solution)/shard_map/ppermute | solution.py:35
  31.0 12.2 %collective-permute-start.17 = (bf16[4,144,384]{2,1,0:T(8,128)(2,1)S(1)}, bf16[4,144,384]{2,1,0:T(8,128)(2,1)S(1)}, u32[]{:S(2)}, u32[]{:S(2)}) collective-permute-start(bf16[4,144,384]{2,1,0:T(8,128)(2,1)S(1)} %constant_dynamic-update-slice_fusion.20), channel_id=1, source_target_pairs={{0,4},{4,0},{8,12},{12,8},{16,20},{20,16},{24,28},{28,24},{1,5},{5... | collective-permute-start | bytes 1327112 | tf_op jit(solution)/shard_map/ppermute | solution.py:35
  31.6 9.7 %collective-permute-start.21 = (bf16[4,72,384]{2,1,0:T(8,128)(2,1)S(1)}, bf16[4,72,384]{2,1,0:T(8,128)(2,1)S(1)}, u32[]{:S(2)}, u32[]{:S(2)}) collective-permute-start(bf16[4,72,384]{2,1,0:T(8,128)(2,1)S(1)} %constant_dynamic-update-slice_fusion.26), channel_id=1, source_target_pairs={{0,2},{1,3},{2,0},{3,1},{4,6},{5,7},{6,4},{7,5},{8,10},{9,11},{10,... | collective-permute-start | bytes 663560 | tf_op jit(solution)/shard_map/ppermute | solution.py:35
  41.2 9.1 %collective-permute-start.11 = (bf16[1,128,384]{2,1,0:T(8,128)(2,1)S(1)}, bf16[1,128,384]{2,1,0:T(8,128)(2,1)S(1)}, u32[]{:S(2)}, u32[]{:S(2)}) collective-permute-start(bf16[1,128,384]{2,1,0:T(8,128)(2,1)S(1)} %bitcast.45), channel_id=1, source_target_pairs={{0,16},{4,20},{8,24},{12,28},{16,0},{20,4},{24,8},{28,12},{1,17},{... | collective-permute-start | bytes 294920 | tf_op jit(solution)/shard_map/ppermute | solution.py:35
  43.3 20.8 %collective-permute-start.18 = (bf16[8,144,384]{2,1,0:T(8,128)(2,1)S(1)}, bf16[8,144,384]{2,1,0:T(8,128)(2,1)S(1)}, u32[]{:S(2)}, u32[]{:S(2)}) collective-permute-start(bf16[8,144,384]{2,1,0:T(8,128)(2,1)S(1)} %constant_dynamic-update-slice_fusion.24.refs_0_), channel_id=1, source_target_pairs={{0,2},{1,3},{2,0},{3,1},{4,6},{5,7},{6,4},{7,5},{8,10},{9,11},{10,... | collective-permute-start | bytes 2654216 | tf_op jit(solution)/shard_map/ppermute | solution.py:35
  43.9 17.4 %collective-permute-start.22 = (bf16[8,72,384]{2,1,0:T(8,128)(2,1)S(1)}, bf16[8,72,384]{2,1,0:T(8,128)(2,1)S(1)}, u32[]{:S(2)}, u32[]{:S(2)}) collective-permute-start(bf16[8,72,384]{2,1,0:T(8,128)(2,1)S(1)} %constant_dynamic-update-slice_fusion.30), channel_id=1, source_target_pairs={{0,4},{4,0},{8,12},{12,8},{16,20},{20,16},{24,28},{28,24},{1,5},{5... | collective-permute-start | bytes 1327112 | tf_op jit(solution)/shard_map/ppermute | solution.py:35
  50.4 10.9 %collective-permute-start.13 = (bf16[3,128,384]{2,1,0:T(8,128)(2,1)S(1)}, bf16[3,128,384]{2,1,0:T(8,128)(2,1)S(1)}, u32[]{:S(2)}, u32[]{:S(2)}) collective-permute-start(bf16[3,128,384]{2,1,0:T(8,128)(2,1)S(1)} %pad_maximum_fusion.1), channel_id=1, source_target_pairs={{0,4},{4,0},{8,12},{12,8},{16,20},{20,16},{24,28},{28,24},{1,5},{5... | collective-permute-start | bytes 884744 | tf_op jit(solution)/shard_map/ppermute | solution.py:35
  61.4 10.8 %collective-permute-start.23 = (bf16[16,72,384]{2,1,0:T(8,128)(2,1)S(1)}, bf16[16,72,384]{2,1,0:T(8,128)(2,1)S(1)}, u32[]{:S(2)}, u32[]{:S(2)}) collective-permute-start(bf16[16,72,384]{2,1,0:T(8,128)(2,1)S(1)} %constant_dynamic-update-slice_fusion.32.refs_4_), channel_id=1, source_target_pairs={{0,1},{1,0},{2,3},{3,2},{4,5},{5,4},{6,7},{7,6},{8,9},{9,8},{10,11... | collective-permute-start | bytes 2654216 | tf_op jit(solution)/shard_map/ppermute | solution.py:35
  85.8 23.1 %collective-permute-start.30 = (bf16[8,144,384]{2,1,0:T(8,128)(2,1)S(1)}, bf16[8,144,384]{2,1,0:T(8,128)(2,1)S(1)}, u32[]{:S(2)}, u32[]{:S(2)}) collective-permute-start(bf16[8,144,384]{2,1,0:T(8,128)(2,1)S(1)} %get-tuple-element.210), channel_id=1, source_target_pairs={{0,2},{1,3},{2,0},{3,1},{4,6},{5,7},{6,4},{7,5},{8,10},{9,11},{10,... | collective-permute-start | bytes 2654216 | tf_op jit(solution)/shard_map/ppermute | solution.py:35
  87.1 10.8 %collective-permute-start.26 = (bf16[4,128,384]{2,1,0:T(8,128)(2,1)S(1)}, bf16[4,128,384]{2,1,0:T(8,128)(2,1)S(1)}, u32[]{:S(2)}, u32[]{:S(2)}) collective-permute-start(bf16[4,128,384]{2,1,0:T(8,128)(2,1)S(1)} %get-tuple-element.166), channel_id=1, source_target_pairs={{0,4},{4,0},{8,12},{12,8},{16,20},{20,16},{24,28},{28,24},{1,5},{5... | collective-permute-start | bytes 1179656 | tf_op jit(solution)/shard_map/ppermute | solution.py:35
  97.9 10.9 %collective-permute-start.31 = (bf16[8,72,384]{2,1,0:T(8,128)(2,1)S(1)}, bf16[8,72,384]{2,1,0:T(8,128)(2,1)S(1)}, u32[]{:S(2)}, u32[]{:S(2)}) collective-permute-start(bf16[8,72,384]{2,1,0:T(8,128)(2,1)S(1)} %get-tuple-element.167), channel_id=1, source_target_pairs={{0,4},{4,0},{8,12},{12,8},{16,20},{20,16},{24,28},{28,24},{1,5},{5... | collective-permute-start | bytes 1327112 | tf_op jit(solution)/shard_map/ppermute | solution.py:35
  98.6 12.2 %collective-permute-start.29 = (bf16[1,128,384]{2,1,0:T(8,128)(2,1)S(1)}, bf16[1,128,384]{2,1,0:T(8,128)(2,1)S(1)}, u32[]{:S(2)}, u32[]{:S(2)}) collective-permute-start(bf16[1,128,384]{2,1,0:T(8,128)(2,1)S(1)} %get-tuple-element.229), channel_id=1, source_target_pairs={{0,24},{4,28},{8,16},{12,20},{16,8},{20,12},{24,0},{28,4},{1,25},{... | collective-permute-start | bytes 294920 | tf_op jit(solution)/shard_map/ppermute | solution.py:35
  101.8 9.0 %collective-permute-start.28 = (bf16[1,128,384]{2,1,0:T(8,128)(2,1)S(1)}, bf16[1,128,384]{2,1,0:T(8,128)(2,1)S(1)}, u32[]{:S(2)}, u32[]{:S(2)}) collective-permute-start(bf16[1,128,384]{2,1,0:T(8,128)(2,1)S(1)} %get-tuple-element.230), channel_id=1, source_target_pairs={{0,16},{4,20},{8,24},{12,28},{16,0},{20,4},{24,8},{28,12},{1,17},{... | collective-permute-start | bytes 294920 | tf_op jit(solution)/shard_map/ppermute | solution.py:35
  109.1 10.0 %collective-permute-start.34 = (bf16[4,144,384]{2,1,0:T(8,128)(2,1)S(1)}, bf16[4,144,384]{2,1,0:T(8,128)(2,1)S(1)}, u32[]{:S(2)}, u32[]{:S(2)}) collective-permute-start(bf16[4,144,384]{2,1,0:T(8,128)(2,1)S(1)} %get-tuple-element.212), channel_id=1, source_target_pairs={{0,4},{4,0},{8,12},{12,8},{16,20},{20,16},{24,28},{28,24},{1,5},{5... | collective-permute-start | bytes 1327112 | tf_op jit(solution)/shard_map/ppermute | solution.py:35
  114.4 10.5 %collective-permute-start.32 = (bf16[16,80,256]{2,1,0:T(8,128)(2,1)S(1)}, bf16[16,80,256]{2,1,0:T(8,128)(2,1)S(1)}, u32[]{:S(2)}, u32[]{:S(2)}) collective-permute-start(bf16[16,80,256]{2,1,0:T(8,128)(2,1)S(1)} %get-tuple-element.181), channel_id=1, source_target_pairs={{0,1},{1,0},{2,3},{3,2},{4,5},{5,4},{6,7},{7,6},{8,9},{9,8},{10,11... | collective-permute-start | bytes 1966088 | tf_op jit(solution)/shard_map/ppermute | solution.py:35
  114.4 10.5 %collective-permute-start.33 = (bf16[16,72,256]{2,1,0:T(8,128)(2,1)S(1)}, bf16[16,72,256]{2,1,0:T(8,128)(2,1)S(1)}, u32[]{:S(2)}, u32[]{:S(2)}) collective-permute-start(bf16[16,72,256]{2,1,0:T(8,128)(2,1)S(1)} %get-tuple-element.182), channel_id=1, source_target_pairs={{0,1},{1,0},{2,3},{3,2},{4,5},{5,4},{6,7},{7,6},{8,9},{9,8},{10,11... | collective-permute-start | bytes 1769480 | tf_op jit(solution)/shard_map/ppermute | solution.py:35
  119.4 9.1 %collective-permute-start.45 = (bf16[1,216,384]{2,1,0:T(8,128)(2,1)S(1)}, bf16[1,216,384]{2,1,0:T(8,128)(2,1)S(1)}, u32[]{:S(2)}, u32[]{:S(2)}) collective-permute-start(bf16[1,216,384]{2,1,0:T(8,128)(2,1)S(1)} %get-tuple-element.221), channel_id=1, source_target_pairs={{0,24},{4,28},{8,16},{12,20},{16,8},{20,12},{24,0},{28,4},{1,25},{... | collective-permute-start | bytes 497672 | tf_op jit(solution)/shard_map/ppermute | solution.py:35
  124.8 10.6 %collective-permute-start.44 = (bf16[1,216,384]{2,1,0:T(8,128)(2,1)S(1)}, bf16[1,216,384]{2,1,0:T(8,128)(2,1)S(1)}, u32[]{:S(2)}, u32[]{:S(2)}) collective-permute-start(bf16[1,216,384]{2,1,0:T(8,128)(2,1)S(1)} %get-tuple-element.224), channel_id=1, source_target_pairs={{0,16},{4,20},{8,24},{12,28},{16,0},{20,4},{24,8},{28,12},{1,17},{... | collective-permute-start | bytes 497672 | tf_op jit(solution)/shard_map/ppermute | solution.py:35
  125.0 10.5 %collective-permute-start.36 = (bf16[8,80,256]{2,1,0:T(8,128)(2,1)S(1)}, bf16[8,80,256]{2,1,0:T(8,128)(2,1)S(1)}, u32[]{:S(2)}, u32[]{:S(2)}) collective-permute-start(bf16[8,80,256]{2,1,0:T(8,128)(2,1)S(1)} %get-tuple-element.215), channel_id=1, source_target_pairs={{0,2},{1,3},{2,0},{3,1},{4,6},{5,7},{6,4},{7,5},{8,10},{9,11},{10,... | collective-permute-start | bytes 983048 | tf_op jit(solution)/shard_map/ppermute | solution.py:35
  126.2 9.3 %collective-permute-start.37 = (bf16[8,72,256]{2,1,0:T(8,128)(2,1)S(1)}, bf16[8,72,256]{2,1,0:T(8,128)(2,1)S(1)}, u32[]{:S(2)}, u32[]{:S(2)}) collective-permute-start(bf16[8,72,256]{2,1,0:T(8,128)(2,1)S(1)} %get-tuple-element.217), channel_id=1, source_target_pairs={{0,4},{4,0},{8,12},{12,8},{16,20},{20,16},{24,28},{28,24},{1,5},{5... | collective-permute-start | bytes 884744 | tf_op jit(solution)/shard_map/ppermute | solution.py:35
  (24 other events, 147.3 us)

commit v6 on v5

--- a/solution.py
+++ b/solution.py
@@ -239,7 +239,7 @@
         for h in (2 * t, 2 * t + 1):
             if h < QUERY_HEADS:
                 half = K_HALF[h // GROUP]
-                qp_ref[head_rows(h), :] = only_half(to_half(u, h % 2, half), half).astype(BF16)
+                qp_ref[head_rows(h), :] = (only_half(to_half(u, h % 2, half), half) * SCALE).astype(BF16)
     for t in range(3):
         u = kv_s[:, t * 128 : (t + 1) * 128]
         if t < 2:
@@ -289,7 +289,7 @@
         for g in range(KEY_VALUE_HEADS):
             keys = kv[:, K_TILE[g] * 128 : (K_TILE[g] + 1) * 128]
             vals = kv[:, V_TILE[g] * 128 : (V_TILE[g] + 1) * 128]
-            s = masked(dot_nt(keys, qp_ref[g * span : (g + 1) * span, :]) * SCALE, mask, blk)
+            s = masked(dot_nt(keys, qp_ref[g * span : (g + 1) * span, :]), mask, blk)
             top = jnp.max(s, axis=0, keepdims=True)
             if not first:
                 top = jnp.maximum(top, m_s[g : g + 1, :])
@@ -473,9 +473,9 @@
             vals = kv[:, V_TILE[g] * 128 : (V_TILE[g] + 1) * 128]
             qg = qp_ref[g * span : (g + 1) * span, :]
             gg = gp_ref[g * span : (g + 1) * span, :]
-            s = masked(dot_nt(keys, qg) * SCALE, mask, blk)
+            s = masked(dot_nt(keys, qg), mask, blk)
             p = jnp.exp(s - lse_ref[g : g + 1, :])
-            ds = (p * (dot_nt(vals, gg) - deltas[g]) * SCALE).astype(BF16)
+            ds = (p * (dot_nt(vals, gg) - deltas[g])).astype(BF16)
             put(V_TILE[g], dot(p.astype(BF16), gg))
             put(K_TILE[g], dot(ds, qg))
             dq = dot_tn(ds, keys)
@@ -498,7 +498,7 @@
     cos, sin = cos_ref[...], sin_ref[...]
     tiles = {}
     for h in range(QUERY_HEADS):
-        u = dq_s[head_rows(h), :]
+        u = dq_s[head_rows(h), :] * SCALE
         tiles[h] = to_half(u * cos - turned(u) * sin, K_HALF[h // GROUP], h % 2)
     for t in range(5):
         if 2 * t + 1 < QUERY_HEADS:

time: 151 us -> 151 us (level)
  no operation moved by 1% of the time
where the time goes in v6:
time: 151 us; the launch traced here: 150 us
  waiting for transfers between devices  68.1 us (45%)
  starting transfers between devices  48.9 us (32%)
  Pallas kernels  22.3 us (15%)
  other arithmetic  5.14 us (3%)
  local copies, waits for them, and re-layouts  3.31 us (2%)
  between operations  2.57 us (2%)
    ppermute x46, waiting for transfers between devices, swap(): return lax.ppermute(x, axis, [(i, i ^ mask) for i in range(size)])  68.1 us
    ppermute x46, starting transfers between devices, swap(): return lax.ppermute(x, axis, [(i, i ^ mask) for i in range(size)])  48.9 us
    pallas_call x7, Pallas kernels, call(): pl.pallas_call(kernel, out_shape=outs, in_specs=[smem] * scalars + [vmem]...  22.3 us
  transfers between devices with their start and end apart: 46, of which 22 were waited for; matrix products, arithmetic and copies ran while one was open for 5% of the time, Pallas kernels for 8%

profile of v6, /device:TPU:0, one launch (start us, length us, event | category | flops | bytes accessed | tf_op | source)
XLA Modules:
  0.0 150.4 jit_solution(14990020445742875029)
XLA Ops:
  1.6 5.1 %collective-permute-start.2 = (bf16[1,152,256]{2,1,0:T(8,128)(2,1)S(1)}, bf16[1,152,256]{2,1,0:T(8,128)(2,1)S(1)}, u32[]{:S(2)}, u32[]{:S(2)}) collective-permute-start(bf16[1,152,256]{2,1,0:T(8,128)(2,1)S(1)} %bitcast.48), channel_id=1, source_target_pairs={{0,24},{4,28},{8,16},{12,20},{16,8},{20,12},{24,0},{28,4},{1,25},{... | collective-permute-start | bytes 233480 | tf_op jit(solution)/shard_map/ppermute | solution.py:35
  18.4 2.0 %collective-permute-start.15 = (bf16[1,216,384]{2,1,0:T(8,128)(2,1)S(1)}, bf16[1,216,384]{2,1,0:T(8,128)(2,1)S(1)}, u32[]{:S(2)}, u32[]{:S(2)}) collective-permute-start(bf16[1,216,384]{2,1,0:T(8,128)(2,1)S(1)} %maximum_bitcast_fusion), channel_id=1, source_target_pairs={{0,8},{4,12},{8,0},{12,4},{16,24},{20,28},{24,16},{28,20},{1,9},{5... | collective-permute-start | bytes 497672 | tf_op jit(solution)/shard_map/ppermute | solution.py:35
  22.2 5.9 %collective-permute-done.16 = bf16[1,216,384]{2,1,0:T(8,128)(2,1)S(1)} collective-permute-done((bf16[1,216,384]{2,1,0:T(8,128)(2,1)S(1)}, bf16[1,216,384]{2,1,0:T(8,128)(2,1)S(1)}, u32[]{:S(2)}, u32[]{:S(2)}) %collective-permute-start.16) | collective-permute-done | bytes 165920 | tf_op jit(solution)/shard_map/ppermute | solution.py:35
  34.9 4.0 %collective-permute-start.10 = (bf16[1,128,384]{2,1,0:T(8,128)(2,1)S(1)}, bf16[1,128,384]{2,1,0:T(8,128)(2,1)S(1)}, u32[]{:S(2)}, u32[]{:S(2)}) collective-permute-start(bf16[1,128,384]{2,1,0:T(8,128)(2,1)S(1)} %bitcast.43), channel_id=1, source_target_pairs={{0,8},{4,12},{8,0},{12,4},{16,24},{20,28},{24,16},{28,20},{1,9},{5... | collective-permute-start | bytes 294920 | tf_op jit(solution)/shard_map/ppermute | solution.py:35
  38.9 2.4 %collective-permute-start.12 = (bf16[1,128,384]{2,1,0:T(8,128)(2,1)S(1)}, bf16[1,128,384]{2,1,0:T(8,128)(2,1)S(1)}, u32[]{:S(2)}, u32[]{:S(2)}) collective-permute-start(bf16[1,128,384]{2,1,0:T(8,128)(2,1)S(1)} %bitcast.44), channel_id=1, source_target_pairs={{0,24},{4,28},{8,16},{12,20},{16,8},{20,12},{24,0},{28,4},{1,25},{... | collective-permute-start | bytes 294920 | tf_op jit(solution)/shard_map/ppermute | solution.py:35
  44.5 2.6 %collective-permute-done.12 = bf16[1,128,384]{2,1,0:T(8,128)(2,1)S(1)} collective-permute-done((bf16[1,128,384]{2,1,0:T(8,128)(2,1)S(1)}, bf16[1,128,384]{2,1,0:T(8,128)(2,1)S(1)}, u32[]{:S(2)}, u32[]{:S(2)}) %collective-permute-start.12) | collective-permute-done | bytes 98336 | tf_op jit(solution)/shard_map/ppermute | solution.py:35
  47.1 3.3 %collective-permute-done.11 = bf16[1,128,384]{2,1,0:T(8,128)(2,1)S(1)} collective-permute-done((bf16[1,128,384]{2,1,0:T(8,128)(2,1)S(1)}, bf16[1,128,384]{2,1,0:T(8,128)(2,1)S(1)}, u32[]{:S(2)}, u32[]{:S(2)}) %collective-permute-start.11) | collective-permute-done | bytes 98336 | tf_op jit(solution)/shard_map/ppermute | solution.py:35
  51.0 10.3 %collective-permute-done.13.refs_1_ = bf16[3,128,384]{2,1,0:T(8,128)(2,1)S(1)} collective-permute-done((bf16[3,128,384]{2,1,0:T(8,128)(2,1)S(1)}, bf16[3,128,384]{2,1,0:T(8,128)(2,1)S(1)}, u32[]{:S(2)}, u32[]{:S(2)}) %collective-permute-start.13) | collective-permute-done | bytes 294944 | tf_op jit(solution)/shard_map/ppermute | solution.py:35
  61.5 2.5 %collective-permute-done.18.refs_1_ = bf16[8,144,384]{2,1,0:T(8,128)(2,1)S(1)} collective-permute-done((bf16[8,144,384]{2,1,0:T(8,128)(2,1)S(1)}, bf16[8,144,384]{2,1,0:T(8,128)(2,1)S(1)}, u32[]{:S(2)}, u32[]{:S(2)}) %collective-permute-start.18) | collective-permute-done | bytes 884768 | tf_op jit(solution)/shard_map/ppermute | solution.py:35
  65.2 4.1 %collective-permute-done.14.refs_2_ = bf16[1,128,384]{2,1,0:T(8,128)(2,1)S(1)} collective-permute-done((bf16[1,128,384]{2,1,0:T(8,128)(2,1)S(1)}, bf16[1,128,384]{2,1,0:T(8,128)(2,1)S(1)}, u32[]{:S(2)}, u32[]{:S(2)}) %collective-permute-start.14) | collective-permute-done | bytes 98336 | tf_op jit(solution)/shard_map/ppermute | solution.py:35
  69.3 2.9 %shard_map.205 = (bf16[128,576]{1,0:T(8,128)(2,1)S(1)}, f32[3,128,384]{2,1,0:T(8,128)S(1)}, f32[8,384]{1,0:T(8,128)S(1)}) custom-call(s32[10]{0:T(128)S(1)} %pad_add_fusion.meta, bf16[1152,128]{1,0:T(8,128)(2,1)S(1)} %get-tuple-element.127.qp_ref, bf16[4,128,384]{2,1,0:T(8,128)(2,1)S(1)} %constant_dynamic-update-slice_fusion.16.refs_0_, ...), custom_call_target="tpu_custom_call" | custom-call | flops 603979776 | bytes 3000000 | tf_op jit(solution)/shard_map/pallas_call | solution.py:601
  72.2 7.9 %shard_map.206 = (bf16[576,128]{1,0:T(8,128)(2,1)}, bf16[16,144,384]{2,1,0:T(8,128)(2,1)S(1)}, bf16[16,144,384]{2,1,0:T(8,128)(2,1)S(1)}, bf16[16,72,384]{2,1,0:...) custom-call(s32[10]{0:T(128)S(1)} %pad_add_fusion.meta, ...), custom_call_target="tpu_custom_call" | custom-call | flops 2038431744 | bytes 14000000 | tf_op jit(solution)/shard_map/pallas_call | solution.py:601
  80.6 4.6 %shard_map.207 = (bf16[128,576]{1,0:T(8,128)(2,1)S(1)}, bf16[4,128,384]{2,1,0:T(8,128)(2,1)S(1)}, bf16[4,128,384]{2,1,0:T(8,128)(2,1)S(1)}) custom-call(s32[10]{0:T(128)S(1)} %pad_add_fusion.meta, bf16[1152,128]{1,0:T(8,128)(2,1)S(1)} %get-tuple-element.127.qp_ref, bf16[1152,128]{1,0:T(8,128)(2,1)S(1)} %get-tuple-element.152.gp_ref, ...), custom_call_target="tpu_custom_call" | custom-call | flops 1509949440 | bytes 5000000 | tf_op jit(solution)/shard_map/pallas_call | solution.py:601
  87.6 10.2 %collective-permute-done.26 = bf16[4,128,384]{2,1,0:T(8,128)(2,1)S(1)} collective-permute-done((bf16[4,128,384]{2,1,0:T(8,128)(2,1)S(1)}, bf16[4,128,384]{2,1,0:T(8,128)(2,1)S(1)}, u32[]{:S(2)}, u32[]{:S(2)}) %collective-permute-start.26) | collective-permute-done | bytes 393248 | tf_op jit(solution)/shard_map/ppermute | solution.py:35
  98.5 3.2 %collective-permute-start.29 = (bf16[1,128,384]{2,1,0:T(8,128)(2,1)S(1)}, bf16[1,128,384]{2,1,0:T(8,128)(2,1)S(1)}, u32[]{:S(2)}, u32[]{:S(2)}) collective-permute-start(bf16[1,128,384]{2,1,0:T(8,128)(2,1)S(1)} %get-tuple-element.229), channel_id=1, source_target_pairs={{0,24},{4,28},{8,16},{12,20},{16,8},{20,12},{24,0},{28,4},{1,25},{... | collective-permute-start | bytes 294920 | tf_op jit(solution)/shard_map/ppermute | solution.py:35
  101.7 2.1 %collective-permute-start.28 = (bf16[1,128,384]{2,1,0:T(8,128)(2,1)S(1)}, bf16[1,128,384]{2,1,0:T(8,128)(2,1)S(1)}, u32[]{:S(2)}, u32[]{:S(2)}) collective-permute-start(bf16[1,128,384]{2,1,0:T(8,128)(2,1)S(1)} %get-tuple-element.230), channel_id=1, source_target_pairs={{0,16},{4,20},{8,24},{12,28},{16,0},{20,4},{24,8},{28,12},{1,17},{... | collective-permute-start | bytes 294920 | tf_op jit(solution)/shard_map/ppermute | solution.py:35
  104.0 4.8 %collective-permute-done.31 = bf16[8,72,384]{2,1,0:T(8,128)(2,1)S(1)} collective-permute-done((bf16[8,72,384]{2,1,0:T(8,128)(2,1)S(1)}, bf16[8,72,384]{2,1,0:T(8,128)(2,1)S(1)}, u32[]{:S(2)}, u32[]{:S(2)}) %collective-permute-start.31) | collective-permute-done | bytes 442400 | tf_op jit(solution)/shard_map/ppermute | solution.py:35
  110.8 3.5 %shard_map.208 = (f32[576,128]{1,0:T(8,128)}, bf16[16,80,256]{2,1,0:T(8,128)(2,1)S(1)}, bf16[16,80,256]{2,1,0:T(8,128)(2,1)S(1)}, bf16[16,72,256]{2,1,0:T(8,128)(2,1)S(1)}, bf16[16,72,256]{2,1,0:T(8,128)(2,1)S(1)}) custom-call(s32[10]{0:T(128)S(1)} %pad_add_fusion.meta, bf16[128,576]{1,0:T(8,128)(2,1)S(1)} %bitcast.42, ...), custom_call_target="tpu_custom_call" | custom-call | flops 905969664 | bytes 6000000 | tf_op jit(solution)/shard_map/pallas_call | solution.py:601
  115.7 3.4 %collective-permute-done.34 = bf16[4,144,384]{2,1,0:T(8,128)(2,1)S(1)} collective-permute-done((bf16[4,144,384]{2,1,0:T(8,128)(2,1)S(1)}, bf16[4,144,384]{2,1,0:T(8,128)(2,1)S(1)}, u32[]{:S(2)}, u32[]{:S(2)}) %collective-permute-start.34) | collective-permute-done | bytes 442400 | tf_op jit(solution)/shard_map/ppermute | solution.py:35
  119.3 3.2 %collective-permute-start.45 = (bf16[1,216,384]{2,1,0:T(8,128)(2,1)S(1)}, bf16[1,216,384]{2,1,0:T(8,128)(2,1)S(1)}, u32[]{:S(2)}, u32[]{:S(2)}) collective-permute-start(bf16[1,216,384]{2,1,0:T(8,128)(2,1)S(1)} %get-tuple-element.221), channel_id=1, source_target_pairs={{0,24},{4,28},{8,16},{12,20},{16,8},{20,12},{24,0},{28,4},{1,25},{... | collective-permute-start | bytes 497672 | tf_op jit(solution)/shard_map/ppermute | solution.py:35
  122.5 2.3 %collective-permute-start.43 = (bf16[1,216,384]{2,1,0:T(8,128)(2,1)S(1)}, bf16[1,216,384]{2,1,0:T(8,128)(2,1)S(1)}, u32[]{:S(2)}, u32[]{:S(2)}) collective-permute-start(bf16[1,216,384]{2,1,0:T(8,128)(2,1)S(1)} %get-tuple-element.223), channel_id=1, source_target_pairs={{0,8},{4,12},{8,0},{12,4},{16,24},{20,28},{24,16},{28,20},{1,9},{5... | collective-permute-start | bytes 497672 | tf_op jit(solution)/shard_map/ppermute | solution.py:35
  129.5 6.0 %collective-permute-done.44 = bf16[1,216,384]{2,1,0:T(8,128)(2,1)S(1)} collective-permute-done((bf16[1,216,384]{2,1,0:T(8,128)(2,1)S(1)}, bf16[1,216,384]{2,1,0:T(8,128)(2,1)S(1)}, u32[]{:S(2)}, u32[]{:S(2)}) %collective-permute-start.44) | collective-permute-done | bytes 165920 | tf_op jit(solution)/shard_map/ppermute | solution.py:35
  138.2 3.3 %collective-permute-done.39 = bf16[4,72,256]{2,1,0:T(8,128)(2,1)S(1)} collective-permute-done((bf16[4,72,256]{2,1,0:T(8,128)(2,1)S(1)}, bf16[4,72,256]{2,1,0:T(8,128)(2,1)S(1)}, u32[]{:S(2)}, u32[]{:S(2)}) %collective-permute-start.39) | collective-permute-done | bytes 147488 | tf_op jit(solution)/shard_map/ppermute | solution.py:35
  141.6 2.8 %collective-permute-start.42 = (bf16[1,152,256]{2,1,0:T(8,128)(2,1)S(1)}, bf16[1,152,256]{2,1,0:T(8,128)(2,1)S(1)}, u32[]{:S(2)}, u32[]{:S(2)}) collective-permute-start(bf16[1,152,256]{2,1,0:T(8,128)(2,1)S(1)} %get-tuple-element.235), channel_id=1, source_target_pairs={{0,24},{4,28},{8,16},{12,20},{16,8},{20,12},{24,0},{28,4},{1,25},{... | collective-permute-start | bytes 233480 | tf_op jit(solution)/shard_map/ppermute | solution.py:35
  (160 shorter events, 45.5 us)
Async XLA Ops:
  1.6 11.1 %collective-permute-start.2 = (bf16[1,152,256]{2,1,0:T(8,128)(2,1)S(1)}, bf16[1,152,256]{2,1,0:T(8,128)(2,1)S(1)}, u32[]{:S(2)}, u32[]{:S(2)}) collective-permute-start(bf16[1,152,256]{2,1,0:T(8,128)(2,1)S(1)} %bitcast.48), channel_id=1, source_target_pairs={{0,24},{4,28},{8,16},{12,20},{16,8},{20,12},{24,0},{28,4},{1,25},{... | collective-permute-start | bytes 233480 | tf_op jit(solution)/shard_map/ppermute | solution.py:35
  16.6 11.6 %collective-permute-start.16 = (bf16[1,216,384]{2,1,0:T(8,128)(2,1)S(1)}, bf16[1,216,384]{2,1,0:T(8,128)(2,1)S(1)}, u32[]{:S(2)}, u32[]{:S(2)}) collective-permute-start(bf16[1,216,384]{2,1,0:T(8,128)(2,1)S(1)} %maximum_bitcast_fusion), channel_id=1, source_target_pairs={{0,16},{4,20},{8,24},{12,28},{16,0},{20,4},{24,8},{28,12},{1,17},{... | collective-permute-start | bytes 497672 | tf_op jit(solution)/shard_map/ppermute | solution.py:35
  18.4 9.8 %collective-permute-start.15 = (bf16[1,216,384]{2,1,0:T(8,128)(2,1)S(1)}, bf16[1,216,384]{2,1,0:T(8,128)(2,1)S(1)}, u32[]{:S(2)}, u32[]{:S(2)}) collective-permute-start(bf16[1,216,384]{2,1,0:T(8,128)(2,1)S(1)} %maximum_bitcast_fusion), channel_id=1, source_target_pairs={{0,8},{4,12},{8,0},{12,4},{16,24},{20,28},{24,16},{28,20},{1,9},{5... | collective-permute-start | bytes 497672 | tf_op jit(solution)/shard_map/ppermute | solution.py:35
  20.4 9.6 %collective-permute-start.5 = (bf16[1,216,384]{2,1,0:T(8,128)(2,1)S(1)}, bf16[1,216,384]{2,1,0:T(8,128)(2,1)S(1)}, u32[]{:S(2)}, u32[]{:S(2)}) collective-permute-start(bf16[1,216,384]{2,1,0:T(8,128)(2,1)S(1)} %maximum_bitcast_fusion), channel_id=1, source_target_pairs={{0,24},{4,28},{8,16},{12,20},{16,8},{20,12},{24,0},{28,4},{1,25},{... | collective-permute-start | bytes 497672 | tf_op jit(solution)/shard_map/ppermute | solution.py:35
  21.0 9.1 %collective-permute-start.8 = (bf16[8,72,256]{2,1,0:T(8,128)(2,1)S(1)}, bf16[8,72,256]{2,1,0:T(8,128)(2,1)S(1)}, u32[]{:S(2)}, u32[]{:S(2)}) collective-permute-start(bf16[8,72,256]{2,1,0:T(8,128)(2,1)S(1)} %constant_dynamic-update-slice_fusion.12), channel_id=1, source_target_pairs={{0,4},{4,0},{8,12},{12,8},{16,20},{20,16},{24,28},{28,24},{1,5},{5... | collective-permute-start | bytes 884744 | tf_op jit(solution)/shard_map/ppermute | solution.py:35
  31.0 12.2 %collective-permute-start.17 = (bf16[4,144,384]{2,1,0:T(8,128)(2,1)S(1)}, bf16[4,144,384]{2,1,0:T(8,128)(2,1)S(1)}, u32[]{:S(2)}, u32[]{:S(2)}) collective-permute-start(bf16[4,144,384]{2,1,0:T(8,128)(2,1)S(1)} %constant_dynamic-update-slice_fusion.20), channel_id=1, source_target_pairs={{0,4},{4,0},{8,12},{12,8},{16,20},{20,16},{24,28},{28,24},{1,5},{5... | collective-permute-start | bytes 1327112 | tf_op jit(solution)/shard_map/ppermute | solution.py:35
  31.6 9.7 %collective-permute-start.21 = (bf16[4,72,384]{2,1,0:T(8,128)(2,1)S(1)}, bf16[4,72,384]{2,1,0:T(8,128)(2,1)S(1)}, u32[]{:S(2)}, u32[]{:S(2)}) collective-permute-start(bf16[4,72,384]{2,1,0:T(8,128)(2,1)S(1)} %constant_dynamic-update-slice_fusion.26), channel_id=1, source_target_pairs={{0,2},{1,3},{2,0},{3,1},{4,6},{5,7},{6,4},{7,5},{8,10},{9,11},{10,... | collective-permute-start | bytes 663560 | tf_op jit(solution)/shard_map/ppermute | solution.py:35
  41.3 9.1 %collective-permute-start.11 = (bf16[1,128,384]{2,1,0:T(8,128)(2,1)S(1)}, bf16[1,128,384]{2,1,0:T(8,128)(2,1)S(1)}, u32[]{:S(2)}, u32[]{:S(2)}) collective-permute-start(bf16[1,128,384]{2,1,0:T(8,128)(2,1)S(1)} %bitcast.45), channel_id=1, source_target_pairs={{0,16},{4,20},{8,24},{12,28},{16,0},{20,4},{24,8},{28,12},{1,17},{... | collective-permute-start | bytes 294920 | tf_op jit(solution)/shard_map/ppermute | solution.py:35
  43.3 20.8 %collective-permute-start.18 = (bf16[8,144,384]{2,1,0:T(8,128)(2,1)S(1)}, bf16[8,144,384]{2,1,0:T(8,128)(2,1)S(1)}, u32[]{:S(2)}, u32[]{:S(2)}) collective-permute-start(bf16[8,144,384]{2,1,0:T(8,128)(2,1)S(1)} %constant_dynamic-update-slice_fusion.24.refs_0_), channel_id=1, source_target_pairs={{0,2},{1,3},{2,0},{3,1},{4,6},{5,7},{6,4},{7,5},{8,10},{9,11},{10,... | collective-permute-start | bytes 2654216 | tf_op jit(solution)/shard_map/ppermute | solution.py:35
  43.9 17.4 %collective-permute-start.22 = (bf16[8,72,384]{2,1,0:T(8,128)(2,1)S(1)}, bf16[8,72,384]{2,1,0:T(8,128)(2,1)S(1)}, u32[]{:S(2)}, u32[]{:S(2)}) collective-permute-start(bf16[8,72,384]{2,1,0:T(8,128)(2,1)S(1)} %constant_dynamic-update-slice_fusion.30), channel_id=1, source_target_pairs={{0,4},{4,0},{8,12},{12,8},{16,20},{20,16},{24,28},{28,24},{1,5},{5... | collective-permute-start | bytes 1327112 | tf_op jit(solution)/shard_map/ppermute | solution.py:35
  50.4 10.8 %collective-permute-start.13 = (bf16[3,128,384]{2,1,0:T(8,128)(2,1)S(1)}, bf16[3,128,384]{2,1,0:T(8,128)(2,1)S(1)}, u32[]{:S(2)}, u32[]{:S(2)}) collective-permute-start(bf16[3,128,384]{2,1,0:T(8,128)(2,1)S(1)} %pad_maximum_fusion.1), channel_id=1, source_target_pairs={{0,4},{4,0},{8,12},{12,8},{16,20},{20,16},{24,28},{28,24},{1,5},{5... | collective-permute-start | bytes 884744 | tf_op jit(solution)/shard_map/ppermute | solution.py:35
  61.4 10.7 %collective-permute-start.23 = (bf16[16,72,384]{2,1,0:T(8,128)(2,1)S(1)}, bf16[16,72,384]{2,1,0:T(8,128)(2,1)S(1)}, u32[]{:S(2)}, u32[]{:S(2)}) collective-permute-start(bf16[16,72,384]{2,1,0:T(8,128)(2,1)S(1)} %constant_dynamic-update-slice_fusion.32.refs_4_), channel_id=1, source_target_pairs={{0,1},{1,0},{2,3},{3,2},{4,5},{5,4},{6,7},{7,6},{8,9},{9,8},{10,11... | collective-permute-start | bytes 2654216 | tf_op jit(solution)/shard_map/ppermute | solution.py:35
  85.7 23.1 %collective-permute-start.30 = (bf16[8,144,384]{2,1,0:T(8,128)(2,1)S(1)}, bf16[8,144,384]{2,1,0:T(8,128)(2,1)S(1)}, u32[]{:S(2)}, u32[]{:S(2)}) collective-permute-start(bf16[8,144,384]{2,1,0:T(8,128)(2,1)S(1)} %get-tuple-element.210), channel_id=1, source_target_pairs={{0,2},{1,3},{2,0},{3,1},{4,6},{5,7},{6,4},{7,5},{8,10},{9,11},{10,... | collective-permute-start | bytes 2654216 | tf_op jit(solution)/shard_map/ppermute | solution.py:35
  87.0 10.8 %collective-permute-start.26 = (bf16[4,128,384]{2,1,0:T(8,128)(2,1)S(1)}, bf16[4,128,384]{2,1,0:T(8,128)(2,1)S(1)}, u32[]{:S(2)}, u32[]{:S(2)}) collective-permute-start(bf16[4,128,384]{2,1,0:T(8,128)(2,1)S(1)} %get-tuple-element.166), channel_id=1, source_target_pairs={{0,4},{4,0},{8,12},{12,8},{16,20},{20,16},{24,28},{28,24},{1,5},{5... | collective-permute-start | bytes 1179656 | tf_op jit(solution)/shard_map/ppermute | solution.py:35
  97.9 10.9 %collective-permute-start.31 = (bf16[8,72,384]{2,1,0:T(8,128)(2,1)S(1)}, bf16[8,72,384]{2,1,0:T(8,128)(2,1)S(1)}, u32[]{:S(2)}, u32[]{:S(2)}) collective-permute-start(bf16[8,72,384]{2,1,0:T(8,128)(2,1)S(1)} %get-tuple-element.167), channel_id=1, source_target_pairs={{0,4},{4,0},{8,12},{12,8},{16,20},{20,16},{24,28},{28,24},{1,5},{5... | collective-permute-start | bytes 1327112 | tf_op jit(solution)/shard_map/ppermute | solution.py:35
  98.5 12.2 %collective-permute-start.29 = (bf16[1,128,384]{2,1,0:T(8,128)(2,1)S(1)}, bf16[1,128,384]{2,1,0:T(8,128)(2,1)S(1)}, u32[]{:S(2)}, u32[]{:S(2)}) collective-permute-start(bf16[1,128,384]{2,1,0:T(8,128)(2,1)S(1)} %get-tuple-element.229), channel_id=1, source_target_pairs={{0,24},{4,28},{8,16},{12,20},{16,8},{20,12},{24,0},{28,4},{1,25},{... | collective-permute-start | bytes 294920 | tf_op jit(solution)/shard_map/ppermute | solution.py:35
  101.7 9.0 %collective-permute-start.28 = (bf16[1,128,384]{2,1,0:T(8,128)(2,1)S(1)}, bf16[1,128,384]{2,1,0:T(8,128)(2,1)S(1)}, u32[]{:S(2)}, u32[]{:S(2)}) collective-permute-start(bf16[1,128,384]{2,1,0:T(8,128)(2,1)S(1)} %get-tuple-element.230), channel_id=1, source_target_pairs={{0,16},{4,20},{8,24},{12,28},{16,0},{20,4},{24,8},{28,12},{1,17},{... | collective-permute-start | bytes 294920 | tf_op jit(solution)/shard_map/ppermute | solution.py:35
  109.0 10.0 %collective-permute-start.34 = (bf16[4,144,384]{2,1,0:T(8,128)(2,1)S(1)}, bf16[4,144,384]{2,1,0:T(8,128)(2,1)S(1)}, u32[]{:S(2)}, u32[]{:S(2)}) collective-permute-start(bf16[4,144,384]{2,1,0:T(8,128)(2,1)S(1)} %get-tuple-element.212), channel_id=1, source_target_pairs={{0,4},{4,0},{8,12},{12,8},{16,20},{20,16},{24,28},{28,24},{1,5},{5... | collective-permute-start | bytes 1327112 | tf_op jit(solution)/shard_map/ppermute | solution.py:35
  114.3 10.5 %collective-permute-start.32 = (bf16[16,80,256]{2,1,0:T(8,128)(2,1)S(1)}, bf16[16,80,256]{2,1,0:T(8,128)(2,1)S(1)}, u32[]{:S(2)}, u32[]{:S(2)}) collective-permute-start(bf16[16,80,256]{2,1,0:T(8,128)(2,1)S(1)} %get-tuple-element.181), channel_id=1, source_target_pairs={{0,1},{1,0},{2,3},{3,2},{4,5},{5,4},{6,7},{7,6},{8,9},{9,8},{10,11... | collective-permute-start | bytes 1966088 | tf_op jit(solution)/shard_map/ppermute | solution.py:35
  114.3 10.5 %collective-permute-start.33 = (bf16[16,72,256]{2,1,0:T(8,128)(2,1)S(1)}, bf16[16,72,256]{2,1,0:T(8,128)(2,1)S(1)}, u32[]{:S(2)}, u32[]{:S(2)}) collective-permute-start(bf16[16,72,256]{2,1,0:T(8,128)(2,1)S(1)} %get-tuple-element.182), channel_id=1, source_target_pairs={{0,1},{1,0},{2,3},{3,2},{4,5},{5,4},{6,7},{7,6},{8,9},{9,8},{10,11... | collective-permute-start | bytes 1769480 | tf_op jit(solution)/shard_map/ppermute | solution.py:35
  119.3 9.1 %collective-permute-start.45 = (bf16[1,216,384]{2,1,0:T(8,128)(2,1)S(1)}, bf16[1,216,384]{2,1,0:T(8,128)(2,1)S(1)}, u32[]{:S(2)}, u32[]{:S(2)}) collective-permute-start(bf16[1,216,384]{2,1,0:T(8,128)(2,1)S(1)} %get-tuple-element.221), channel_id=1, source_target_pairs={{0,24},{4,28},{8,16},{12,20},{16,8},{20,12},{24,0},{28,4},{1,25},{... | collective-permute-start | bytes 497672 | tf_op jit(solution)/shard_map/ppermute | solution.py:35
  124.8 10.6 %collective-permute-start.44 = (bf16[1,216,384]{2,1,0:T(8,128)(2,1)S(1)}, bf16[1,216,384]{2,1,0:T(8,128)(2,1)S(1)}, u32[]{:S(2)}, u32[]{:S(2)}) collective-permute-start(bf16[1,216,384]{2,1,0:T(8,128)(2,1)S(1)} %get-tuple-element.224), channel_id=1, source_target_pairs={{0,16},{4,20},{8,24},{12,28},{16,0},{20,4},{24,8},{28,12},{1,17},{... | collective-permute-start | bytes 497672 | tf_op jit(solution)/shard_map/ppermute | solution.py:35
  125.0 10.5 %collective-permute-start.36 = (bf16[8,80,256]{2,1,0:T(8,128)(2,1)S(1)}, bf16[8,80,256]{2,1,0:T(8,128)(2,1)S(1)}, u32[]{:S(2)}, u32[]{:S(2)}) collective-permute-start(bf16[8,80,256]{2,1,0:T(8,128)(2,1)S(1)} %get-tuple-element.215), channel_id=1, source_target_pairs={{0,2},{1,3},{2,0},{3,1},{4,6},{5,7},{6,4},{7,5},{8,10},{9,11},{10,... | collective-permute-start | bytes 983048 | tf_op jit(solution)/shard_map/ppermute | solution.py:35
  126.1 9.4 %collective-permute-start.37 = (bf16[8,72,256]{2,1,0:T(8,128)(2,1)S(1)}, bf16[8,72,256]{2,1,0:T(8,128)(2,1)S(1)}, u32[]{:S(2)}, u32[]{:S(2)}) collective-permute-start(bf16[8,72,256]{2,1,0:T(8,128)(2,1)S(1)} %get-tuple-element.217), channel_id=1, source_target_pairs={{0,4},{4,0},{8,12},{12,8},{16,20},{20,16},{24,28},{28,24},{1,5},{5... | collective-permute-start | bytes 884744 | tf_op jit(solution)/shard_map/ppermute | solution.py:35
  (24 other events, 147.1 us)
